TPU v7x, 512 devices: a whole 4x4x16 slice. The times are simulated.
512 devices in a mesh: dp: 2 (over y_lo), tensor: 4 (over x), context: 64 (over z, y_hi, core).
Axes of the slice: x: 4, y: 4 (y_hi: 2, y_lo: 2; y = y_hi * 2 + y_lo), z: 16, core: 2. Of those that a mesh axis runs over, the one named last changes fastest.
Arguments:
- q_in: bfloat16 [2, 8192, 4096], P('dp', 'context', 'tensor'), may hold values from -44 to 44
- k_in: bfloat16 [2, 8192, 4096], P('dp', 'context', 'tensor'), may hold values from -6 to 6
- v_in: bfloat16 [2, 8192, 4096], P('dp', 'context', 'tensor'), may hold values from -6 to 6
- short_filt: float32 [3, 7, 4096], P(None, None, 'tensor'), may hold values from -2 to 2
- long_filt: float32 [8192, 4096], P('context', 'tensor'), may hold values from -1.1 to 1.1
- norm_gain: float32 [4096], P('tensor'), may hold values from 0.1 to 1.9
- grad_out: bfloat16 [2, 8192, 4096], P('dp', 'context', 'tensor'), may hold values from -6 to 6
Outputs:
- mixed: bfloat16 [2, 8192, 4096], P('dp', 'context', 'tensor')
- grad_inputs: bfloat16 [3, 2, 8192, 4096], P(None, 'dp', 'context', 'tensor')
- grad_long: float32 [8192, 4096], P('context', 'tensor')
- grad_short: float32 [3, 7, 4096], P(None, None, 'tensor')
All inputs are finite; a program needn't handle non-finite values.
Results may differ from a plain program's by a relative error of at most 0.00225.
Values may be sent and summed in bfloat16 or wider, within the bound.
No kernel may reach another device: no remote copies, remote signals or barrier semaphores. Data moves between devices by JAX's collectives and lax.ppermute only.
A program may use at most 128 MiB of HBM per device.

v0:
```python
import math

import jax
import jax.numpy as jnp
from jax import lax
from jax.sharding import PartitionSpec as P

D = 4096
FILT = 7


EPS = 1e-06
HIGH = lax.Precision.HIGHEST


def passed_along(shard, axis, by):
    peers = lax.axis_size(axis)
    pairs = [(i, i + by) for i in range(peers) if 0 <= i + by < peers]
    return lax.ppermute(shard, axis, pairs)


def phases(first, second, modulus):
    product = first[:, None] * second[None, :] % modulus
    return product.astype(jnp.float32) * (2.0 * math.pi / modulus)


def block_table(block_len, sign):
    index = jnp.arange(block_len, dtype=jnp.int32)
    angle = phases(index, index, block_len)
    cosine = jnp.cos(angle)
    sine = jnp.sin(angle) * sign
    return jnp.stack([jnp.stack([cosine, sine]), jnp.stack([-sine, cosine])])


def forward_rows(values, modulus):
    count, block_len, width = values.shape
    ctx_size = lax.axis_size("context")
    sub_len = block_len // ctx_size
    spread = lax.all_to_all(
        values.reshape(count, 1, block_len, width),
        "context",
        split_axis=2,
        concat_axis=1,
        tiled=True,
    )
    freq = jnp.arange(2 * ctx_size, dtype=jnp.int32)
    place = (
        jnp.arange(ctx_size, dtype=jnp.int32)[:, None] * block_len
        + lax.axis_index("context") * sub_len
        + jnp.arange(sub_len, dtype=jnp.int32)[None, :]
    )
    angle = (freq[:, None, None] * place[None] % modulus).astype(jnp.float32) * (
        2.0 * math.pi / modulus
    )
    table = jnp.stack([jnp.cos(angle), -jnp.sin(angle)])
    turned = jnp.einsum("pkcs,ncsx->npksx", table, spread, precision=HIGH)
    moved = lax.all_to_all(turned, "context", split_axis=2, concat_axis=3, tiled=True)
    return jnp.einsum("pqmb,nqjbx->npjmx", block_table(block_len, 1.0), moved, precision=HIGH)


def inverse_rows(spec, modulus):
    rows = spec.shape[2]
    block_len = spec.shape[3]
    ctx_size = lax.axis_size("context")
    index = jnp.arange(block_len, dtype=jnp.int32)
    freq = 2 * lax.axis_index("context") + jnp.arange(rows, dtype=jnp.int32)
    total = freq[:, None, None] + 2 * ctx_size * index[None, :, None]
    angle = (total * index[None, None, :] % modulus).astype(jnp.float32) * (2.0 * math.pi / modulus)
    cosine = jnp.cos(angle)
    sine = jnp.sin(angle)
    table = jnp.stack([jnp.stack([cosine, -sine]), jnp.stack([sine, cosine])])
    turned = jnp.einsum("pqjmb,nqjmx->npjbx", table, spec, precision=HIGH)
    moved = lax.all_to_all(turned, "context", split_axis=3, concat_axis=2, tiled=True)
    outer = phases(
        jnp.arange(ctx_size, dtype=jnp.int32),
        jnp.arange(2 * ctx_size, dtype=jnp.int32),
        2 * ctx_size,
    )
    real_table = jnp.stack([jnp.cos(outer), -jnp.sin(outer)])
    values = jnp.einsum("qck,nqksx->ncsx", real_table, moved, precision=HIGH) / modulus
    back = lax.all_to_all(values, "context", split_axis=1, concat_axis=2, tiled=True)
    return back.reshape(back.shape[0], back.shape[2], back.shape[3])


def shards(q_in, k_in, v_in, short_filt, long_filt, norm_gain, grad_out):
    block_len = q_in.shape[1]
    channels = q_in.shape[2]
    edge_rows = FILT - 1
    modulus = 2 * lax.axis_size("context") * block_len
    branches = jnp.stack([q_in[0], k_in[0], v_in[0]])
    before = passed_along(branches[:, block_len - edge_rows :], "context", 1)
    inputs = jnp.concatenate([before, branches], 1).astype(jnp.float32)
    shorts = jnp.zeros((3, block_len, channels), jnp.float32)
    for lag in range(FILT):
        shorts = (
            shorts
            + short_filt[:, lag][:, None, :]
            * inputs[:, edge_rows - lag : edge_rows - lag + block_len]
        )
    q_short = shorts[0]
    k_short = shorts[1]
    v_short = shorts[2]
    kv_prod = k_short * v_short
    spectra = forward_rows(jnp.stack([kv_prod, long_filt]), modulus)
    kv_real, kv_imag = (spectra[0, 0], spectra[0, 1])
    filt_real, filt_imag = (spectra[1, 0], spectra[1, 1])
    conv_spec = jnp.stack(
        [kv_real * filt_real - kv_imag * filt_imag, kv_real * filt_imag + kv_imag * filt_real]
    )[None]
    conv = inverse_rows(conv_spec, modulus)[0]
    y_out = q_short * conv
    squares = lax.psum(jnp.sum(y_out * y_out, axis=-1), "tensor")
    rms = jnp.sqrt(squares / D + EPS)[:, None]
    mixed = (y_out / rms * norm_gain).astype(jnp.bfloat16)[None]
    grad_z = grad_out[0].astype(jnp.float32) * norm_gain
    prods = lax.psum(jnp.sum(grad_z * y_out, axis=-1), "tensor")[:, None]
    grad_y = grad_z / rms - y_out * prods / (D * rms**3)
    dconv = grad_y * q_short
    grad_q = grad_y * conv
    grad_spec = forward_rows(dconv[None], modulus)[0]
    grad_real = grad_spec[0]
    grad_imag = grad_spec[1]
    dkv_spec = jnp.stack(
        [
            filt_real * grad_real + filt_imag * grad_imag,
            filt_real * grad_imag - filt_imag * grad_real,
        ]
    )
    dfilt_spec = jnp.stack(
        [kv_real * grad_real + kv_imag * grad_imag, kv_real * grad_imag - kv_imag * grad_real]
    )
    results = inverse_rows(jnp.stack([dkv_spec, dfilt_spec]), modulus)
    dkv = results[0]
    dfilt_local = results[1]
    grads = jnp.stack([grad_q, dkv * v_short, dkv * k_short])
    after = passed_along(grads[:, :edge_rows].astype(jnp.bfloat16), "context", -1).astype(
        jnp.float32
    )
    extended = jnp.concatenate([grads, after], 1)
    grad_inputs = jnp.zeros((3, block_len, channels), jnp.float32)
    for lag in range(FILT):
        grad_inputs = (
            grad_inputs + short_filt[:, lag][:, None, :] * extended[:, lag : lag + block_len]
        )
    short_local = jnp.stack(
        [
            jnp.sum(grads * inputs[:, edge_rows - lag : edge_rows - lag + block_len], axis=1)
            for lag in range(FILT)
        ],
        1,
    )
    scale = 1.0 / math.sqrt(lax.axis_size("dp") * block_len * lax.axis_size("context"))
    grad_long = lax.psum(dfilt_local, "dp") * scale
    grad_short = lax.psum(short_local, ("dp", "context")) * scale
    return (mixed, grad_inputs.astype(jnp.bfloat16)[:, None], grad_long, grad_short)


def solution(mesh):
    in_specs = (
        P("dp", "context", "tensor"),
        P("dp", "context", "tensor"),
        P("dp", "context", "tensor"),
        P(None, None, "tensor"),
        P("context", "tensor"),
        P("tensor"),
        P("dp", "context", "tensor"),
    )
    out_specs = (
        P("dp", "context", "tensor"),
        P(None, "dp", "context", "tensor"),
        P("context", "tensor"),
        P(None, None, "tensor"),
    )
    return jax.shard_map(shards, mesh=mesh, in_specs=in_specs, out_specs=out_specs, check_vma=False)
```

profile of v0, /device:TPU:1, one launch (start us, length us, event | category | flops | bytes accessed | tf_op | source)
XLA Modules:
  0.0 1352.6 jit_solution(16455876887592393104)
XLA Ops:
  11.4 6.2 collective-permute-start
  22.3 3.9 multiply_add_fusion
  31.3 17.8 %all-to-all-start = ((f32[2,1,128,1024]{3,0,1,2:T(2,128)}), f32[2,1,128,1024]{3,0,1,2:T(2,128)S(1)}, u32[]{:S(2)}, u32[]{:S(2)}) async-start(f32[2,1,128,1024]{3,0,1,2:T(2,128)} %maximum_bitcast_fusion.4), calls=%async_computation | async-start | bytes 2097152 | tf_op jit(solution)/shard_map/all_to_all | solution.py:39
  49.5 53.7 %all-to-all-done = f32[2,1,128,1024]{3,0,1,2:T(2,128)S(1)} async-done(((f32[2,1,128,1024]{3,0,1,2:T(2,128)}), f32[2,1,128,1024]{3,0,1,2:T(2,128)S(1)}, u32[]{:S(2)}, u32[]{:S(2)}) %all-to-all-start) | async-done | bytes 1048608 | tf_op jit(solution)/shard_map/all_to_all | solution.py:39
  103.1 5.2 convolution_bitcast_fusion
  108.3 7.3 copy.68
  115.6 7.8 all-to-all-start.1
  124.8 184.3 %all-to-all-done.1 = f32[2,2,128,2,1024]{4,1,0,3,2:T(2,128)} async-done(((f32[2,2,128,2,1024]{4,1,0,3,2:T(2,128)}), f32[2,2,128,2,1024]{4,1,0,3,2:T(2,128)}, u32[]{:S(2)}, u32[]{:S(2)}) %all-to-all-start.1) | async-done | bytes 4194336 | tf_op jit(solution)/shard_map/all_to_all | solution.py:57
  309.1 5.4 copy.70
  314.5 8.1 fusion.4
  324.6 3.3 fusion.21
  328.0 4.2 copy.79
  332.2 10.6 all-to-all-start.2
  343.0 98.5 %all-to-all-done.2 = f32[1,2,2,128,1024]{4,1,2,0,3:T(2,128)} async-done(((f32[1,2,2,128,1024]{4,1,2,0,3:T(2,128)}), f32[1,2,2,128,1024]{4,1,2,0,3:T(2,128)}, u32[]{:S(2)}, u32[]{:S(2)}) %all-to-all-start.2) | async-done | bytes 2097184 | tf_op jit(solution)/shard_map/all_to_all | solution.py:73
  441.4 2.7 copy.80
  444.1 2.2 copy.81
  446.3 3.7 reshape.785
  450.0 3.1 fusion.30
  454.3 7.7 all-to-all-start.3
  463.2 32.8 %all-to-all-done.3 = f32[1,64,2,1024]{3,2,0,1:T(2,128)S(1)} async-done(((f32[1,64,2,1024]{3,2,0,1:T(2,128)}), f32[1,64,2,1024]{3,2,0,1:T(2,128)S(1)}, u32[]{:S(2)}, u32[]{:S(2)}) %all-to-all-start.3) | async-done | bytes 524320 | tf_op jit(solution)/shard_map/all_to_all | solution.py:81
  497.2 2.2 fusion.44
  499.4 9.3 all-reduce
  511.5 3.0 fusion.48
  514.5 40.9 %all_to_all.105 = f32[1,1,128,1024]{3,0,1,2:T(1,128)} all-to-all(f32[1,1,128,1024]{3,0,1,2:T(1,128)S(1)} %fusion.48), channel_id=1, replica_groups=mesh['dp'=2,'tensor'=4,'context'=64] {'context'}, dimensions={2} | all-to-all | bytes 1048576 | tf_op jit(solution)/shard_map/all_to_all | solution.py:39
  555.4 3.1 reduce
  560.6 4.3 convolution_bitcast_fusion.1
  564.9 4.2 copy.86
  569.1 103.5 %all_to_all.106 = f32[1,2,128,2,1024]{4,1,3,0,2:T(2,128)S(1)} all-to-all(f32[1,2,128,2,1024]{4,1,3,0,2:T(2,128)} %copy.86), channel_id=1, replica_groups=mesh['dp'=2,'tensor'=4,'context'=64] {'context'}, dimensions={2} | all-to-all | bytes 4194304 | tf_op jit(solution)/shard_map/all_to_all | solution.py:57
  673.7 2.5 copy.88
  676.2 4.1 copy.89
  680.3 3.6 fusion.24
  684.8 5.0 fusion.7
  689.7 7.3 copy.95
  697.1 196.5 %all_to_all.107 = f32[2,2,2,128,1024]{4,1,0,2,3:T(2,128)S(1)} all-to-all(f32[2,2,2,128,1024]{4,1,0,2,3:T(2,128)} %copy.95), channel_id=1, replica_groups=mesh['dp'=2,'tensor'=4,'context'=64] {'context'}, dimensions={3} | all-to-all | bytes 8388608 | tf_op jit(solution)/shard_map/all_to_all | solution.py:73
  893.6 5.3 copy.97
  898.8 6.0 all_to_all.95
  904.9 4.6 fusion.28
  911.2 8.2 all-to-all-start.7
  921.1 52.3 %all-to-all-done.7 = f32[2,64,2,1024]{3,2,0,1:T(2,128)} async-done(((f32[2,64,2,1024]{3,2,0,1:T(2,128)}), f32[2,64,2,1024]{3,2,0,1:T(2,128)}, u32[]{:S(2)}, u32[]{:S(2)}) %all-to-all-start.7) | async-done | bytes 1048608 | tf_op jit(solution)/shard_map/all_to_all | solution.py:81
  977.1 7.5 fusion.41
  984.6 4.3 multiply_reduce_fusion
  990.1 2.5 pad_maximum_fusion.1
  992.6 4.4 collective-permute-start.1
  999.2 2.3 collective-permute-done.1
  1001.5 2.5 pad_maximum_fusion
  1004.1 3.8 fusion.40
  1009.0 289.3 %all-reduce.6.cloned.1.call-done = f32[3,7,1024]{2,0,1:T(4,128)} async-done(((f32[3,7,1024]{2,0,1:T(4,128)}), f32[3,7,1024]{2,0,1:T(4,128)}) %all-reduce.6.cloned.1.call-update) | async-done | bytes 86032 | tf_op jit(solution)/shard_map/psum | solution.py:154
  1299.9 43.4 %all-reduce.4.cloned.1.call-done = f32[128,1024]{1,0:T(8,128)} async-done(((f32[128,1024]{1,0:T(8,128)}), f32[128,1024]{1,0:T(8,128)}) %all-reduce.4.cloned.1.call-update) | async-done | bytes 524304 | tf_op jit(solution)/shard_map/psum | solution.py:153
  (127 shorter events, 42.8 us)
Async XLA Ops:
  7.2 10.5 copy-start.28
  7.2 10.7 copy-start.12
  11.4 8.9 collective-permute-start
  17.7 4.5 copy-start.16
  17.8 4.4 copy-start.18
  17.8 4.4 copy-start.20
  17.8 4.4 copy-start.22
  17.8 4.4 copy-start.24
  17.9 4.4 copy-start.26
  26.2 1.4 copy-start.2
  31.3 71.9 %all-to-all-start = ((f32[2,1,128,1024]{3,0,1,2:T(2,128)}), f32[2,1,128,1024]{3,0,1,2:T(2,128)S(1)}, u32[]{:S(2)}, u32[]{:S(2)}) async-start(f32[2,1,128,1024]{3,0,1,2:T(2,128)} %maximum_bitcast_fusion.4), calls=%async_computation | async-start | bytes 2097152 | tf_op jit(solution)/shard_map/all_to_all | solution.py:39
  49.4 58.9 %copy-start.10 = (f32[1,128,64,2]{1,2,0,3:T(8,128)}, f32[1,128,64,2]{1,2,0,3:T(8,128)S(1)}, u32[]{:S(2)}) copy-start(f32[1,128,64,2]{1,2,0,3:T(8,128)S(1)} %get-tuple-element.55) | copy-start | bytes 196612
  49.5 58.9 %copy-start.11 = (f32[1,128,64,2]{1,2,0,3:T(8,128)}, f32[1,128,64,2]{1,2,0,3:T(8,128)S(1)}, u32[]{:S(2)}) copy-start(f32[1,128,64,2]{1,2,0,3:T(8,128)S(1)} %get-tuple-element.56) | copy-start | bytes 196612
  115.6 193.4 %all-to-all-start.1 = ((f32[2,2,128,2,1024]{4,1,0,3,2:T(2,128)}), f32[2,2,128,2,1024]{4,1,0,3,2:T(2,128)}, u32[]{:S(2)}, u32[]{:S(2)}) async-start(f32[2,2,128,2,1024]{4,1,0,3,2:T(2,128)} %copy.68), calls=%async_computation.1 | async-start | bytes 8388608 | tf_op jit(solution)/shard_map/all_to_all | solution.py:57
  124.0 190.5 %copy-start.8 = (f32[1,2,128,128]{3,2,1,0:T(8,128)}, f32[1,2,128,128]{3,2,1,0:T(8,128)S(1)}, u32[]{:S(2)}) copy-start(f32[1,2,128,128]{3,2,1,0:T(8,128)S(1)} %get-tuple-element.50) | copy-start | bytes 393220
  124.0 190.5 %copy-start.9 = (f32[1,2,128,128]{3,2,1,0:T(8,128)}, f32[1,2,128,128]{3,2,1,0:T(8,128)S(1)}, u32[]{:S(2)}) copy-start(f32[1,2,128,128]{3,2,1,0:T(8,128)S(1)} %get-tuple-element.51) | copy-start | bytes 393220
  322.7 2.0 copy-start
  332.2 109.2 %all-to-all-start.2 = ((f32[1,2,2,128,1024]{4,1,2,0,3:T(2,128)}), f32[1,2,2,128,1024]{4,1,2,0,3:T(2,128)}, u32[]{:S(2)}, u32[]{:S(2)}) async-start(f32[1,2,2,128,1024]{4,1,2,0,3:T(2,128)} %copy.79), calls=%async_computation.2 | async-start | bytes 4194304 | tf_op jit(solution)/shard_map/all_to_all | solution.py:73
  342.9 107.1 %copy-start.13 = (f32[1,64,128]{2,1,0:T(8,128)}, f32[1,64,128]{2,1,0:T(8,128)S(1)}, u32[]{:S(2)}) copy-start(f32[1,64,128]{2,1,0:T(8,128)S(1)} %get-tuple-element.68) | copy-start | bytes 98308
  450.0 12.0 copy-start.5
  454.3 41.7 %all-to-all-start.3 = ((f32[1,64,2,1024]{3,2,0,1:T(2,128)}), f32[1,64,2,1024]{3,2,0,1:T(2,128)S(1)}, u32[]{:S(2)}, u32[]{:S(2)}) async-start(f32[1,64,2,1024]{3,2,0,1:T(2,128)} %copy.82), calls=%async_computation.3 | async-start | bytes 1048576 | tf_op jit(solution)/shard_map/all_to_all | solution.py:81
  680.3 3.6 copy-start.1
  898.8 6.0 copy-start.14
  911.2 62.2 %all-to-all-start.7 = ((f32[2,64,2,1024]{3,2,0,1:T(2,128)}), f32[2,64,2,1024]{3,2,0,1:T(2,128)}, u32[]{:S(2)}, u32[]{:S(2)}) async-start(f32[2,64,2,1024]{3,2,0,1:T(2,128)} %copy.98), calls=%async_computation.7 | async-start | bytes 2097152 | tf_op jit(solution)/shard_map/all_to_all | solution.py:81
  919.5 57.7 %copy-start.29 = (f32[1024]{0:T(1024)S(1)}, f32[1024]{0:T(1024)}, u32[]{:S(2)}) copy-start(f32[1024]{0:T(1024)} %param.12) | copy-start | bytes 12292
  919.5 57.6 %copy-start.30 = (f32[128]{0:T(128)S(1)}, f32[128]{0:T(128)}, u32[]{:S(2)}) copy-start(f32[128]{0:T(128)} %get-tuple-element.22) | copy-start | bytes 1540
  919.5 57.6 %copy-start.31 = (f32[128]{0:T(128)S(1)}, f32[128]{0:T(128)}, u32[]{:S(2)}) copy-start(f32[128]{0:T(128)} %get-tuple-element.57) | copy-start | bytes 1540
  919.5 57.6 %copy-start.32 = (f32[128]{0:T(128)S(1)}, f32[128]{0:T(128)}, u32[]{:S(2)}) copy-start(f32[128]{0:T(128)} %get-tuple-element.58) | copy-start | bytes 1540
  919.5 378.8 %all-reduce.6.cloned.1.call-start = ((), (), s32[]{:S(2)}) async-start(), calls=%async_computation.9 | async-start | bytes 229376 | tf_op jit(solution)/shard_map/psum | solution.py:154
  984.6 4.3 copy-start.3
  989.0 8.1 copy-start.7
  989.0 9.3 copy-start.6
  989.1 0.6 copy-start.15
  989.8 353.6 %all-reduce.4.cloned.1.call-start = ((), (), s32[]{:S(2)}) async-start(), calls=%async_computation.8 | async-start | bytes 1048576 | tf_op jit(solution)/shard_map/psum | solution.py:153
  992.6 8.8 collective-permute-start.1
  999.1 4.9 copy-start.4
  999.1 4.9 copy-start.17
  999.1 4.9 copy-start.19
  999.1 4.9 copy-start.21
  999.1 4.9 copy-start.23
  999.1 4.9 copy-start.25
  999.2 4.9 copy-start.27
Sparse Core Ops, SparseCore 0:
  989.9 308.3 all-reduce.5
  1301.2 42.1 all-reduce.3
where the time goes:
time: 1360 us; the launch traced here: 1350 us
  waiting for transfers between devices  759 us (56%)
  blocking collectives  350 us (26%)
  local copies, waits for them, and re-layouts  81.6 us (6%)
  starting transfers between devices  63.1 us (5%)
  other arithmetic  46.6 us (3%)
  matrix products  37.2 us (3%)
  between operations  15.3 us (1%)
    psum x1, waiting for transfers between devices, shards(): grad_short = lax.psum(short_local, ('dp', 'context')) * scale  289 us
    all_to_all x1, blocking collectives, inverse_rows(): lax.all_to_all(turned, 'context', split_axis=3, concat_axis=2, tiled=True)  196 us
    all_to_all x1, waiting for transfers between devices, forward_rows(): lax.all_to_all(turned, 'context', split_axis=2, concat_axis=3, tiled=True)  184 us
    all_to_all x1, blocking collectives, forward_rows(): lax.all_to_all(turned, 'context', split_axis=2, concat_axis=3, tiled=True)  103 us
    all_to_all x1, waiting for transfers between devices, inverse_rows(): lax.all_to_all(turned, 'context', split_axis=3, concat_axis=2, tiled=True)  98.5 us
    all_to_all x2, waiting for transfers between devices, inverse_rows(): lax.all_to_all(values, 'context', split_axis=1, concat_axis=2, tiled=True)  85 us
    all_to_all x1, waiting for transfers between devices, forward_rows(): lax.all_to_all(values.reshape(count, 1, block_len, width), 'context', spl...  53.7 us
    psum x1, waiting for transfers between devices, shards(): grad_long = lax.psum(dfilt_local, 'dp') * scale  43.4 us
  transfers between devices with their start and end apart: 9, of which 9 were waited for; matrix products, arithmetic and copies ran while one was open for 1% of the time, Pallas kernels for 0%

commit v1 on v0

v1 whole, which is shorter than its diff:
```python
import functools
import math

import jax
import jax.numpy as jnp
import numpy as np
from jax import lax
from jax.experimental import pallas as pl
from jax.experimental.pallas import tpu as pltpu
from jax.sharding import PartitionSpec as P

D = 4096
FILT = 7
EPS = 1e-06
LANES = 128
F32 = jnp.float32
BF16 = jnp.bfloat16
VMEM = pl.BlockSpec(memory_space=pltpu.VMEM)
SMEM = pl.BlockSpec(memory_space=pltpu.SMEM)
PARAMS = pltpu.CompilerParams(vmem_limit_bytes=56 * 2**20)


def halves(table):
    high = table.astype(jnp.bfloat16)
    low = (table - high.astype(np.float64)).astype(jnp.bfloat16)
    return high, low


@functools.cache
def tables(rows):
    size = rows * LANES
    row = np.arange(rows)
    lane = np.arange(LANES)
    angle = 2 * np.pi * np.outer(row + 0.25, row) / rows
    high, low = halves(np.concatenate([np.cos(angle), -np.sin(angle)], 0))
    first = np.concatenate([high, high, low], 1)
    high, low = halves(np.concatenate([np.cos(angle).T, -np.sin(angle).T], 1) / size)
    last = np.concatenate([high, high, low], 1)
    turn = 2 * np.pi * np.outer(row + 0.25, lane) / size
    twiddle = np.stack([np.cos(turn), -np.sin(turn)]).astype(np.float32)
    grid = 2 * np.pi * (np.outer(lane, lane) % LANES) / LANES
    cosine, sine = np.cos(grid), -np.sin(grid)
    high, low = halves(np.block([[cosine, sine], [-sine, cosine]]))
    inner = np.concatenate([high, high, low], 0)
    high, low = halves(np.block([[cosine, -sine], [sine, cosine]]))
    outer = np.concatenate([high, high, low], 0)
    return first, last, twiddle, inner, outer


def split(values):
    high = values.astype(BF16)
    return high, (values - high.astype(F32)).astype(BF16)


def dot(left, right):
    return jnp.dot(left, right, preferred_element_type=F32)


def forward(blocks, first_ref, twiddle_ref, inner_ref):
    rows = blocks[0].shape[0]
    real, imag = twiddle_ref[0], twiddle_ref[1]
    parts = []
    for pair in range(0, len(blocks), 2):
        high, low = split(jnp.concatenate(blocks[pair : pair + 2], 1))
        mixed = dot(first_ref[...], jnp.concatenate([high, low, high], 0))
        for side in range(2):
            lanes = slice(side * LANES, (side + 1) * LANES)
            re, im = mixed[:rows, lanes], mixed[rows:, lanes]
            parts.append(jnp.concatenate([re * real - im * imag, re * imag + im * real], 1))
    high, low = split(jnp.concatenate(parts, 0))
    return dot(jnp.concatenate([high, low, high], 1), inner_ref[...])


def inverse(spectra, rows, last_ref, twiddle_ref, outer_ref):
    real, imag = twiddle_ref[0], twiddle_ref[1]
    high, low = split(spectra)
    turned = dot(jnp.concatenate([high, low, high], 1), outer_ref[...])
    count = spectra.shape[0] // rows
    blocks = []
    for pair in range(0, count, 2):
        sides = []
        for block in (pair, pair + 1):
            re = turned[block * rows : (block + 1) * rows, :LANES]
            im = turned[block * rows : (block + 1) * rows, LANES:]
            sides.append(jnp.concatenate([re * real + im * imag, im * real - re * imag], 0))
        high, low = split(jnp.concatenate(sides, 1))
        out = dot(last_ref[...], jnp.concatenate([high, low, high], 0))
        blocks += [out[:, :LANES], out[:, LANES:]]
    return blocks


def times(left, right, conjugate):
    re_l, im_l = left[:, :LANES], left[:, LANES:]
    re_r, im_r = right[:, :LANES], right[:, LANES:]
    if conjugate:
        return jnp.concatenate([re_l * re_r + im_l * im_r, re_l * im_r - im_l * re_r], 1)
    return jnp.concatenate([re_l * re_r - im_l * im_r, re_l * im_r + im_l * re_r], 1)


def lagged(block):
    row = lax.broadcasted_iota(jnp.int32, block.shape, 0)
    lane = lax.broadcasted_iota(jnp.int32, block.shape, 1)
    above = jnp.where(row == 0, 0.0, pltpu.roll(block, 1, 0))
    return [block] + [
        pltpu.roll(jnp.where(lane >= LANES - lag, above, block), lag, 1) for lag in range(1, FILT)
    ]


def led(block):
    rows = block.shape[0]
    row = lax.broadcasted_iota(jnp.int32, block.shape, 0)
    lane = lax.broadcasted_iota(jnp.int32, block.shape, 1)
    below = jnp.where(row == rows - 1, 0.0, pltpu.roll(block, rows - 1, 0))
    return [block] + [
        pltpu.roll(jnp.where(lane < lag, below, block), LANES - lag, 1) for lag in range(1, FILT)
    ]


def filtered(shifted, taps_ref, branch, channel):
    total = shifted[0] * taps_ref[branch * FILT, channel]
    for lag in range(1, FILT):
        total = total + shifted[lag] * taps_ref[branch * FILT + lag, channel]
    return total


def strided(ref, channel, count):
    return ref[pl.ds(channel, ref.shape[0] // count, stride=count), :]


def widen(source_ref, start, count, target_ref):
    rows = source_ref.shape[0]
    target_ref[...] = source_ref[:, start : start + count, :].astype(F32).reshape(rows * count, LANES)


def turn_kernel(count, width, *refs):
    for index, ref in enumerate(refs[:count]):
        out_ref = refs[count]
        for start in range(0, ref.shape[1], LANES):
            block = ref[:, start : start + LANES].astype(F32).T.astype(out_ref.dtype)
            out_ref[start // width : (start + LANES) // width, index * width : (index + 1) * width, :] = (
                block.reshape(LANES // width, width, LANES)
            )


def turn(arrays, width):
    channels = arrays[0].shape[1]
    shape = (channels // width, len(arrays) * width, LANES)
    return pl.pallas_call(
        functools.partial(turn_kernel, len(arrays), width),
        out_shape=jax.ShapeDtypeStruct(shape, arrays[0].dtype),
        in_specs=[VMEM] * len(arrays),
        out_specs=VMEM,
        compiler_params=PARAMS,
    )(*arrays)


def unturn_kernel(count, width, scale, in_ref, *out_refs):
    for index in range(count):
        out_ref = out_refs[index]
        for start in range(0, out_ref.shape[1], LANES):
            block = in_ref[start // width : (start + LANES) // width, index * width : (index + 1) * width, :]
            block = block.astype(F32).reshape(LANES, LANES).T
            if scale is not None:
                block = block * scale
            out_ref[:, start : start + LANES] = block.astype(out_ref.dtype)


def unturn(payload, count, scale=None):
    groups, rows, _ = payload.shape
    width = rows // count
    return pl.pallas_call(
        functools.partial(unturn_kernel, count, width, scale),
        out_shape=[jax.ShapeDtypeStruct((LANES, groups * width), payload.dtype)] * count,
        in_specs=[VMEM],
        out_specs=[VMEM] * count,
        compiler_params=PARAMS,
    )(payload)


STEP = 4


def conv_kernel(width, pair_ref, filt_ref, taps_ref, first_ref, last_ref, twiddle_ref, inner_ref, outer_ref,
                conv_ref, spec_kv_ref, spec_filt_ref, k_ref, v_ref):
    rows = pair_ref.shape[0]
    widen(pair_ref, 0, width, k_ref)
    widen(pair_ref, width, width, v_ref)
    for start in range(0, width, STEP):
        products = []
        filters = []
        for channel in range(start, start + STEP):
            k_short = filtered(lagged(strided(k_ref, channel, width)), taps_ref, 1, channel)
            v_short = filtered(lagged(strided(v_ref, channel, width)), taps_ref, 2, channel)
            products.append(k_short * v_short)
            filters.append(strided(filt_ref, channel, width))
        spec_kv = forward(products, first_ref, twiddle_ref, inner_ref)
        spec_filt = forward(filters, first_ref, twiddle_ref, inner_ref)
        part = slice(start * rows, (start + STEP) * rows)
        spec_kv_ref[part, :] = spec_kv
        spec_filt_ref[part, :] = spec_filt
        convs = inverse(times(spec_kv, spec_filt, False), rows, last_ref, twiddle_ref, outer_ref)
        for index, block in enumerate(convs):
            conv_ref[start + index] = block


def stats_kernel(width, pair_ref, conv_ref, taps_ref, gain_ref, q_short_ref, stats_ref, q_ref, g_ref):
    widen(pair_ref, 0, width, q_ref)
    widen(pair_ref, width, width, g_ref)
    squares = jnp.zeros(stats_ref.shape[1:], F32)
    prods = squares
    for channel in range(width):
        q_short = filtered(lagged(strided(q_ref, channel, width)), taps_ref, 0, channel)
        q_short_ref[channel] = q_short
        y_out = q_short * conv_ref[channel]
        squares = squares + y_out * y_out
        prods = prods + strided(g_ref, channel, width) * gain_ref[0, channel] * y_out
    stats_ref[0] = squares
    stats_ref[1] = prods


def norm_kernel(width, pair_ref, conv_ref, q_short_ref, stats_ref, taps_ref, gain_ref, out_ref, dconv_ref, short_ref,
                q_ref, g_ref, mixed_ref, grad_ref):
    rows = pair_ref.shape[0]
    widen(pair_ref, 0, width, q_ref)
    widen(pair_ref, width, width, g_ref)
    rms = jnp.sqrt(stats_ref[0] / D + EPS)
    inverse_rms = 1.0 / rms
    slope = stats_ref[1] / (D * rms * rms * rms)
    for channel in range(width):
        gain = gain_ref[0, channel]
        q_short = q_short_ref[channel]
        conv = conv_ref[channel]
        y_out = q_short * conv
        mixed_ref[pl.ds(channel, rows, stride=width), :] = y_out / rms * gain
        grad_y = strided(g_ref, channel, width) * gain * inverse_rms - y_out * slope
        dconv_ref[channel] = grad_y * q_short
        grad_q = grad_y * conv
        grad_ref[pl.ds(channel, rows, stride=width), :] = filtered(led(grad_q), taps_ref, 0, channel)
        for lag, block in enumerate(lagged(strided(q_ref, channel, width))):
            short_ref[lag * width + channel : lag * width + channel + 1, :] = jnp.sum(
                grad_q * block, axis=0, keepdims=True
            )
    out_ref[:, :width, :] = mixed_ref[...].reshape(rows, width, LANES).astype(BF16)
    out_ref[:, width:, :] = grad_ref[...].reshape(rows, width, LANES).astype(BF16)


def back_kernel(width, dconv_ref, pair_ref, spec_kv_ref, spec_filt_ref, taps_ref, first_ref, last_ref, twiddle_ref,
                inner_ref, outer_ref, out_ref, dfilt_ref, short_ref, k_ref, v_ref, grad_k_ref, grad_v_ref):
    rows = pair_ref.shape[0]
    widen(pair_ref, 0, width, k_ref)
    widen(pair_ref, width, width, v_ref)
    for start in range(0, width, STEP):
        part = slice(start * rows, (start + STEP) * rows)
        spec = forward(
            [dconv_ref[channel] for channel in range(start, start + STEP)], first_ref, twiddle_ref, inner_ref
        )
        dkv = inverse(times(spec_filt_ref[part, :], spec, True), rows, last_ref, twiddle_ref, outer_ref)
        dfilt = inverse(times(spec_kv_ref[part, :], spec, True), rows, last_ref, twiddle_ref, outer_ref)
        for index in range(STEP):
            channel = start + index
            dfilt_ref[pl.ds(channel, rows, stride=width), :] = dfilt[index]
            k_lags = lagged(strided(k_ref, channel, width))
            v_lags = lagged(strided(v_ref, channel, width))
            grad_k = dkv[index] * filtered(v_lags, taps_ref, 2, channel)
            grad_v = dkv[index] * filtered(k_lags, taps_ref, 1, channel)
            grad_k_ref[pl.ds(channel, rows, stride=width), :] = filtered(led(grad_k), taps_ref, 1, channel)
            grad_v_ref[pl.ds(channel, rows, stride=width), :] = filtered(led(grad_v), taps_ref, 2, channel)
            for lag in range(FILT):
                row = lag * width + channel
                short_ref[row : row + 1, :] = jnp.sum(grad_k * k_lags[lag], axis=0, keepdims=True)
                row += FILT * width
                short_ref[row : row + 1, :] = jnp.sum(grad_v * v_lags[lag], axis=0, keepdims=True)
    out_ref[:, :width, :] = grad_k_ref[...].reshape(rows, width, LANES).astype(BF16)
    out_ref[:, width:, :] = grad_v_ref[...].reshape(rows, width, LANES).astype(BF16)


def exchange(payload):
    return lax.all_to_all(payload, "context", split_axis=0, concat_axis=0, tiled=True)


def swap(half):
    return lax.ppermute(half, "dp", [(0, 1), (1, 0)])


def whole(half, side):
    other = swap(half)
    return jnp.where(
        side == 0, jnp.concatenate([half, other], 1), jnp.concatenate([other, half], 1)
    )


def shards(q_in, k_in, v_in, short_filt, long_filt, norm_gain, grad_out):
    rows = lax.axis_size("context")
    channels = q_in.shape[2]
    width = channels // rows
    size = rows * width
    place = lax.axis_index("context")
    side = lax.axis_index("dp")
    first, last, twiddle, inner, outer = (jnp.asarray(t) for t in tables(rows))
    shape = functools.partial(jax.ShapeDtypeStruct, dtype=F32)
    scratch = pltpu.VMEM((size, LANES), F32)

    taps = lax.dynamic_index_in_dim(short_filt.reshape(3 * FILT, rows, width), place, 1, keepdims=False)
    gain = lax.dynamic_index_in_dim(norm_gain.reshape(rows, width), place, 0)

    filt_own = lax.dynamic_index_in_dim(
        turn([long_filt], width).reshape(rows, 2, width // 2, LANES), side, 1, keepdims=False
    )
    filt_half = exchange(filt_own)
    kv_pair = exchange(turn([k_in[0], v_in[0]], width))
    qg_pair = exchange(turn([q_in[0], grad_out[0]], width))
    filt = whole(filt_half, side).reshape(size, LANES)

    conv, spec_kv, spec_filt = pl.pallas_call(
        functools.partial(conv_kernel, width),
        out_shape=[shape((width, rows, LANES)), shape((size, 2 * LANES)), shape((size, 2 * LANES))],
        in_specs=[VMEM, VMEM, SMEM] + [VMEM] * 5,
        out_specs=[VMEM] * 3,
        scratch_shapes=[scratch] * 2,
        compiler_params=PARAMS,
    )(kv_pair, filt, taps, first, last, twiddle, inner, outer)

    q_short, stats = pl.pallas_call(
        functools.partial(stats_kernel, width),
        out_shape=[shape((width, rows, LANES)), shape((2, rows, LANES))],
        in_specs=[VMEM, VMEM, SMEM, SMEM],
        out_specs=[VMEM] * 2,
        scratch_shapes=[scratch] * 2,
        compiler_params=PARAMS,
    )(qg_pair, conv, taps, gain)
    stats = lax.psum(stats, ("tensor", "context"))

    mixed_pair, dconv, short_q = pl.pallas_call(
        functools.partial(norm_kernel, width),
        out_shape=[
            jax.ShapeDtypeStruct((rows, 2 * width, LANES), BF16),
            shape((width, rows, LANES)),
            shape((FILT * width, LANES)),
        ],
        in_specs=[VMEM] * 4 + [SMEM] * 2,
        out_specs=[VMEM] * 3,
        scratch_shapes=[scratch] * 4,
        compiler_params=PARAMS,
    )(qg_pair, conv, q_short, stats, taps, gain)
    mixed_pair = exchange(mixed_pair)

    grad_pair, dfilt, short_kv = pl.pallas_call(
        functools.partial(back_kernel, width),
        out_shape=[
            jax.ShapeDtypeStruct((rows, 2 * width, LANES), BF16),
            shape((size, LANES)),
            shape((2 * FILT * width, LANES)),
        ],
        in_specs=[VMEM] * 4 + [SMEM] + [VMEM] * 5,
        out_specs=[VMEM] * 3,
        scratch_shapes=[scratch] * 4,
        compiler_params=PARAMS,
    )(dconv, kv_pair, spec_kv, spec_filt, taps, first, last, twiddle, inner, outer)
    grad_pair = exchange(grad_pair)

    scale = 1.0 / math.sqrt(lax.axis_size("dp") * rows * LANES)
    parts = dfilt.reshape(rows, 2, width // 2, LANES)
    own = lax.dynamic_index_in_dim(parts, side, 1, keepdims=False)
    other = lax.dynamic_index_in_dim(parts, 1 - side, 1, keepdims=False)
    dfilt = whole(exchange(own + swap(other)), side)
    (grad_long,) = unturn(dfilt, 1, scale)

    short = jnp.sum(jnp.concatenate([short_q, short_kv]), axis=1) * scale
    short = lax.all_gather(short, ("dp", "context")).reshape(2, rows, 3, FILT, width)
    grad_short = jnp.sum(short, axis=0).transpose(1, 2, 0, 3).reshape(3, FILT, channels)

    mixed, grad_q = unturn(mixed_pair, 2)
    grad_k, grad_v = unturn(grad_pair, 2)
    return (mixed[None], jnp.stack([grad_q, grad_k, grad_v])[:, None], grad_long, grad_short)


def solution(mesh):
    in_specs = (
        P("dp", "context", "tensor"),
        P("dp", "context", "tensor"),
        P("dp", "context", "tensor"),
        P(None, None, "tensor"),
        P("context", "tensor"),
        P("tensor"),
        P("dp", "context", "tensor"),
    )
    out_specs = (
        P("dp", "context", "tensor"),
        P(None, "dp", "context", "tensor"),
        P("context", "tensor"),
        P(None, None, "tensor"),
    )
    return jax.shard_map(shards, mesh=mesh, in_specs=in_specs, out_specs=out_specs, check_vma=False)
```

time: 1360 us -> 2770 us (2.04)
  waiting for transfers between devices: 759 us -> 2590 us
  blocking collectives: 350 us -> 71.6 us
  local copies, waits for them, and re-layouts: 81.6 us -> 10.3 us
  other arithmetic: 46.6 us -> 5.2 us
  matrix products: 37.2 us -> 0 us
  Pallas kernels: 0 us -> 35.2 us
    psum x2 -> x1, waiting for transfers between devices: 333 us -> 2190 us  [shards(): stats = lax.psum(stats, ('tensor', 'context'))]
    all_to_all x5 -> x4, waiting for transfers between devices: 421 us -> 69.5 us  [exchange(): lax.all_to_all(payload, 'context', split_axis=0, concat_axis=0, tiled=True)]
    unnamed x2 -> x3, waiting for transfers between devices: 0.03 us -> 323 us
    all_to_all x3 -> x2, blocking collectives: 341 us -> 71.6 us  [exchange(): lax.all_to_all(payload, 'context', split_axis=0, concat_axis=0, tiled=True)]
    dot_general x8 -> x0, matrix products: 37.2 us -> none  [the longest x2 11.8 us: forward_rows(): jnp.einsum('pqmb,nqjbx->npjmx', block_table(block_len, 1.0), moved, preci...]
    pallas_call x0 -> x10, Pallas kernels: none -> 35.2 us  [the longest x1 9.13 us: shards(): pl.pallas_call(functools.partial(back_kernel, width), out_shape=[jax.Shap...]
  transfers between devices with their start and end apart: 9 -> 9, of which waited for: 9 -> 7; matrix products, arithmetic and copies ran while one was open for 1% -> 0% of each run, Pallas kernels for 0% -> 1%
where the time goes in v1:
time: 2770 us
  waiting for transfers between devices  2590 us (94%)
  blocking collectives  71.6 us (3%)
  starting transfers between devices  40.9 us (1%)
  Pallas kernels  35.2 us (1%)
    psum x1, waiting for transfers between devices, shards(): stats = lax.psum(stats, ('tensor', 'context'))  2190 us
    unnamed x3, waiting for transfers between devices  323 us
    all_to_all x2, blocking collectives, exchange(): lax.all_to_all(payload, 'context', split_axis=0, concat_axis=0, tiled=True)  71.6 us
    all_to_all x4, waiting for transfers between devices, exchange(): lax.all_to_all(payload, 'context', split_axis=0, concat_axis=0, tiled=True)  69.5 us
  transfers between devices with their start and end apart: 9, of which 7 were waited for; matrix products, arithmetic and copies ran while one was open for 0% of the time, Pallas kernels for 1%

profile of v1, /device:TPU:1, one launch (start us, length us, event | category | flops | bytes accessed | tf_op | source)
XLA Modules:
  0.0 2767.6 jit_solution(1990021275504091420)
XLA Ops:
  7.2 2.0 shard_map.149
  9.2 1.7 dynamic-slice_bitcast_fusion.1
  10.9 19.8 all-to-all-start.2
  30.7 2.0 shard_map.148
  32.7 21.8 all-to-all-done.2
  54.5 4.2 all-to-all-start.1
  58.7 2.0 shard_map.147
  60.7 31.7 %all-to-all-done.1.pair_ref = bf16[64,32,128]{2,1,0:T(8,128)(2,1)S(1)} async-done(((bf16[64,32,128]{2,1,0:T(8,128)(2,1)}), bf16[64,32,128]{2,1,0:T(8,128)(2,1)S(1)}, u32[]{:S(2)}, u32[]{:S(2)}) %all-to-all-start.1) | async-done | bytes 524320 | tf_op jit(solution)/shard_map/all_to_all | solution.py:278
  92.4 5.0 all-to-all-start
  97.4 0.0 all-reduce.4.cloned.1.call-start
  97.4 2.5 collective-permute-start
  99.9 0.2 reshape.41
  100.2 0.6 copy.49
  100.8 0.1 reshape.42
  100.9 0.5 constant_dynamic-slice_fusion.gain_ref
  101.4 6.4 collective-permute-done
  107.9 0.8 maximum_select_fusion
  108.7 6.7 shard_map.150
  115.4 16.0 all-to-all-done.pair_ref
  131.4 0.8 copy-done.1
  132.2 3.0 shard_map.151
  135.2 2185.5 %all-reduce.4.cloned.1.call-done.stats_ref = f32[2,64,128]{2,1,0:T(8,128)} async-done(((f32[2,64,128]{2,1,0:T(8,128)}), f32[2,64,128]{2,1,0:T(8,128)}) %all-reduce.4.cloned.1.call-update) | async-done | bytes 65552 | tf_op jit(solution)/shard_map/psum | solution.py:331
  2320.6 4.3 shard_map.152
  2324.9 9.1 shard_map.154
  2334.1 1.0 dynamic-slice_bitcast_fusion
  2335.1 2.3 collective-permute-start.1
  2337.4 5.0 collective-permute-done.1
  2342.4 1.0 bitcast_add_fusion
  2343.4 33.7 %all_to_all.30 = f32[64,8,128]{2,1,0:T(8,128)S(1)} all-to-all(f32[64,8,128]{2,1,0:T(8,128)S(1)} %bitcast_add_fusion), channel_id=1, replica_groups=mesh['dp'=2,'tensor'=4,'context'=64] {'context'}, dimensions={0} | all-to-all | bytes 524288 | tf_op jit(solution)/shard_map/all_to_all | solution.py:278
  2377.0 37.9 %all_to_all.31.in_ref = bf16[64,32,128]{2,1,0:T(8,128)(2,1)} all-to-all(bf16[64,32,128]{2,1,0:T(8,128)(2,1)S(1)} %copy-done.4), channel_id=1, replica_groups=mesh['dp'=2,'tensor'=4,'context'=64] {'context'}, dimensions={0} | all-to-all | bytes 1048576 | tf_op jit(solution)/shard_map/all_to_all | solution.py:278
  2414.9 5.0 all-to-all-start.3
  2419.9 0.0 all-reduce.6.cloned.1.call-start
  2419.9 1.3 dynamic-slice
  2421.9 0.1 maximum_reduce_fusion
  2422.0 2.2 collective-permute-start.2
  2424.3 0.1 multiply_dynamic-update-slice_fusion
  2424.4 0.7 copy-done.3
  2425.1 323.2 %all-reduce.6.cloned.1.call-done = f32[43008]{0:T(1024)} async-done(((f32[43008]{0:T(1024)}), f32[43008]{0:T(1024)}) %all-reduce.6.cloned.1.call-update) | async-done | bytes 172048
  2748.3 1.4 reshape.44
  2749.7 0.2 reduce_sum.19
  2749.9 0.1 copy.42
  2750.0 1.0 reshape.45
  2751.0 0.8 maximum_select_fusion.1.in_ref
  2751.9 2.0 shard_map.156
  2753.9 2.0 shard_map.155
  2755.9 0.8 copy-done.2
  2756.7 2.0 shard_map.153
  2758.6 2.1 maximum_bitcast_fusion
  (21 shorter events, 0.1 us)
Async XLA Ops:
  10.9 43.6 %all-to-all-start.2 = ((f32[64,8,128]{2,1,0:T(8,128)}), f32[64,8,128]{2,1,0:T(8,128)S(1)}, u32[]{:S(2)}, u32[]{:S(2)}) async-start(f32[64,8,128]{2,1,0:T(8,128)} %dynamic-slice_bitcast_fusion.1), calls=%async_computation.2 | async-start | bytes 524288 | tf_op jit(solution)/shard_map/all_to_all | solution.py:278
  32.7 67.2 %copy-start.6 = (f32[3,7,1024]{2,1,0:T(8,128)S(1)}, f32[3,7,1024]{2,1,0:T(8,128)}, u32[]{:S(2)}) copy-start(f32[3,7,1024]{2,1,0:T(8,128)} %param.15) | copy-start | bytes 258052
  54.5 38.0 %all-to-all-start.1 = ((bf16[64,32,128]{2,1,0:T(8,128)(2,1)}), bf16[64,32,128]{2,1,0:T(8,128)(2,1)S(1)}, u32[]{:S(2)}, u32[]{:S(2)}) async-start(bf16[64,32,128]{2,1,0:T(8,128)(2,1)} %shard_map.148), calls=%async_computation.1 | async-start | bytes 1048576 | tf_op jit(solution)/shard_map/all_to_all | solution.py:278
  58.7 42.2 %copy-start.8 = (f32[1024]{0:T(1024)S(1)}, f32[1024]{0:T(1024)}, u32[]{:S(2)}) copy-start(f32[1024]{0:T(1024)} %param.17) | copy-start | bytes 12292
  92.4 16.3 copy-start
  92.4 39.0 %all-to-all-start = ((bf16[64,32,128]{2,1,0:T(8,128)(2,1)}), bf16[64,32,128]{2,1,0:T(8,128)(2,1)S(1)}, u32[]{:S(2)}, u32[]{:S(2)}) async-start(bf16[64,32,128]{2,1,0:T(8,128)(2,1)} %shard_map.147), calls=%async_computation | async-start | bytes 1048576 | tf_op jit(solution)/shard_map/all_to_all | solution.py:278
  97.4 2223.2 %all-reduce.4.cloned.1.call-start = ((), (), s32[]{:S(2)}) async-start(), calls=%async_computation.6 | async-start | bytes 131072 | tf_op jit(solution)/shard_map/psum | solution.py:331
  97.4 10.4 collective-permute-start
  131.4 0.8 copy-start.1
  2334.1 43.0 %copy-start.4 = (bf16[64,32,128]{2,1,0:T(8,128)(2,1)S(1)}, bf16[64,32,128]{2,1,0:T(8,128)(2,1)}, u32[]{:S(2)}) copy-start(bf16[64,32,128]{2,1,0:T(8,128)(2,1)} %get-tuple-element.28) | copy-start | bytes 1572868
  2335.1 86.8 %copy-start.5 = (f32[224,128]{1,0:T(8,128)S(1)}, f32[224,128]{1,0:T(8,128)}, u32[]{:S(2)}) copy-start(f32[224,128]{1,0:T(8,128)} %get-tuple-element.33) | copy-start | bytes 344068
  2335.1 86.8 %copy-start.7 = (f32[112,128]{1,0:T(8,128)S(1)}, f32[112,128]{1,0:T(8,128)}, u32[]{:S(2)}) copy-start(f32[112,128]{1,0:T(8,128)} %get-tuple-element.32) | copy-start | bytes 172036
  2335.1 7.2 collective-permute-start.1
  2414.9 341.0 %all-to-all-start.3 = ((bf16[64,32,128]{2,1,0:T(8,128)(2,1)}), bf16[64,32,128]{2,1,0:T(8,128)(2,1)S(1)}, u32[]{:S(2)}, u32[]{:S(2)}) async-start(bf16[64,32,128]{2,1,0:T(8,128)(2,1)} %get-tuple-element.22), calls=%async_computation.3 | async-start | bytes 1048576 | tf_op jit(solution)/shard_map/all_to_all | solution.py:278
  2419.9 328.4 %all-reduce.6.cloned.1.call-start = ((), (), s32[]{:S(2)}) async-start(), calls=%async_computation.7 | async-start | bytes 344064
  2422.0 329.0 %collective-permute-start.2 = (f32[64,8,128]{2,1,0:T(8,128)S(1)}, f32[64,8,128]{2,1,0:T(8,128)S(1)}, u32[]{:S(2)}, u32[]{:S(2)}) collective-permute-start(f32[64,8,128]{2,1,0:T(8,128)S(1)} %all_to_all.30), channel_id=1, source_target_pairs={{0,256},{256,0},{1,257},{257,1},{2,258},{258,2},{3,259},{259,3},{4... | collective-permute-start | bytes 786440 | tf_op jit(solution)/shard_map/ppermute | solution.py:282
  2424.4 0.7 copy-start.3
  2755.9 0.8 copy-start.2
Sparse Core Ops, SparseCore 0:
  135.3 2185.2 all-reduce.3
  2425.2 323.0 all-reduce.5

commit v2 on v1

v2 whole, which is shorter than its diff:
```python
import functools
import math

import jax
import jax.numpy as jnp
import numpy as np
from jax import lax
from jax.experimental import pallas as pl
from jax.experimental.pallas import tpu as pltpu
from jax.sharding import PartitionSpec as P

D = 4096
FILT = 7
EPS = 1e-06
LANES = 128
F32 = jnp.float32
BF16 = jnp.bfloat16
VMEM = pl.BlockSpec(memory_space=pltpu.VMEM)
SMEM = pl.BlockSpec(memory_space=pltpu.SMEM)
PARAMS = pltpu.CompilerParams(vmem_limit_bytes=56 * 2**20)


def halves(table):
    high = table.astype(jnp.bfloat16)
    low = (table - high.astype(np.float64)).astype(jnp.bfloat16)
    return high, low


@functools.cache
def tables(rows):
    size = rows * LANES
    row = np.arange(rows)
    lane = np.arange(LANES)
    angle = 2 * np.pi * np.outer(row + 0.25, row) / rows
    high, low = halves(np.concatenate([np.cos(angle), -np.sin(angle)], 0))
    first = np.concatenate([high, high, low], 1)
    high, low = halves(np.concatenate([np.cos(angle).T, -np.sin(angle).T], 1) / size)
    last = np.concatenate([high, high, low], 1)
    turn = 2 * np.pi * np.outer(row + 0.25, lane) / size
    twiddle = np.stack([np.cos(turn), -np.sin(turn)]).astype(np.float32)
    grid = 2 * np.pi * (np.outer(lane, lane) % LANES) / LANES
    cosine, sine = np.cos(grid), -np.sin(grid)
    high, low = halves(np.block([[cosine, sine], [-sine, cosine]]))
    inner = np.concatenate([high, high, low], 0)
    high, low = halves(np.block([[cosine, -sine], [sine, cosine]]))
    outer = np.concatenate([high, high, low], 0)
    return first, last, twiddle, inner, outer


def split(values):
    high = values.astype(BF16)
    return high, (values - high.astype(F32)).astype(BF16)


def dot(left, right):
    return jnp.dot(left, right, preferred_element_type=F32)


def forward(blocks, first_ref, twiddle_ref, inner_ref):
    rows = blocks[0].shape[0]
    real, imag = twiddle_ref[0], twiddle_ref[1]
    parts = []
    for pair in range(0, len(blocks), 2):
        high, low = split(jnp.concatenate(blocks[pair : pair + 2], 1))
        mixed = dot(first_ref[...], jnp.concatenate([high, low, high], 0))
        for side in range(2):
            lanes = slice(side * LANES, (side + 1) * LANES)
            re, im = mixed[:rows, lanes], mixed[rows:, lanes]
            parts.append(jnp.concatenate([re * real - im * imag, re * imag + im * real], 1))
    high, low = split(jnp.concatenate(parts, 0))
    return dot(jnp.concatenate([high, low, high], 1), inner_ref[...])


def inverse(spectra, rows, last_ref, twiddle_ref, outer_ref):
    real, imag = twiddle_ref[0], twiddle_ref[1]
    high, low = split(spectra)
    turned = dot(jnp.concatenate([high, low, high], 1), outer_ref[...])
    count = spectra.shape[0] // rows
    blocks = []
    for pair in range(0, count, 2):
        sides = []
        for block in (pair, pair + 1):
            re = turned[block * rows : (block + 1) * rows, :LANES]
            im = turned[block * rows : (block + 1) * rows, LANES:]
            sides.append(jnp.concatenate([re * real + im * imag, im * real - re * imag], 0))
        high, low = split(jnp.concatenate(sides, 1))
        out = dot(last_ref[...], jnp.concatenate([high, low, high], 0))
        blocks += [out[:, :LANES], out[:, LANES:]]
    return blocks


def times(left, right, conjugate):
    re_l, im_l = left[:, :LANES], left[:, LANES:]
    re_r, im_r = right[:, :LANES], right[:, LANES:]
    if conjugate:
        return jnp.concatenate([re_l * re_r + im_l * im_r, re_l * im_r - im_l * re_r], 1)
    return jnp.concatenate([re_l * re_r - im_l * im_r, re_l * im_r + im_l * re_r], 1)


def lagged(block):
    row = lax.broadcasted_iota(jnp.int32, block.shape, 0)
    lane = lax.broadcasted_iota(jnp.int32, block.shape, 1)
    above = jnp.where(row == 0, 0.0, pltpu.roll(block, 1, 0))
    return [block] + [
        pltpu.roll(jnp.where(lane >= LANES - lag, above, block), lag, 1) for lag in range(1, FILT)
    ]


def led(block):
    rows = block.shape[0]
    row = lax.broadcasted_iota(jnp.int32, block.shape, 0)
    lane = lax.broadcasted_iota(jnp.int32, block.shape, 1)
    below = jnp.where(row == rows - 1, 0.0, pltpu.roll(block, rows - 1, 0))
    return [block] + [
        pltpu.roll(jnp.where(lane < lag, below, block), LANES - lag, 1) for lag in range(1, FILT)
    ]


def filtered(shifted, taps_ref, branch, channel):
    total = shifted[0] * taps_ref[branch * FILT, channel]
    for lag in range(1, FILT):
        total = total + shifted[lag] * taps_ref[branch * FILT + lag, channel]
    return total


def strided(ref, start, count, step):
    return ref[pl.ds(start, count, stride=step), :]


def kernel_call(kernel, shapes, smem=(), scratch=(), count=0):
    return pl.pallas_call(
        kernel,
        out_shape=shapes,
        in_specs=[SMEM if index in smem else VMEM for index in range(count)],
        out_specs=[VMEM] * len(shapes),
        scratch_shapes=list(scratch),
        compiler_params=PARAMS,
    )


def f32(*dims):
    return jax.ShapeDtypeStruct(dims, F32)


def bf16(*dims):
    return jax.ShapeDtypeStruct(dims, BF16)


def pack_kernel(width, side_ref, k_ref, v_ref, filt_ref, out_ref):
    low_side = side_ref[0, 0] == 1
    for start in range(0, k_ref.shape[1], LANES):
        into = slice(start // width, (start + LANES) // width)
        for index, ref in enumerate((k_ref, v_ref, filt_ref)):
            block = ref[:, start : start + LANES].astype(F32).T
            if ref is filt_ref:
                block = block - jnp.where(low_side, block.astype(BF16).astype(F32), 0.0)
            out_ref[into, index * width : (index + 1) * width, :] = (
                block.astype(BF16).reshape(LANES // width, width, LANES)
            )


def shifted(values, lag):
    return values[lag : lag + LANES]


HALO = 8


def prepare_kernel(q_ref, halo_ref, grad_ref, taps_ref, gain_ref, q_short_ref, grad_z_ref):
    for start in range(0, q_ref.shape[1], LANES):
        lanes = slice(start, start + LANES)
        extended = jnp.concatenate([halo_ref[:, lanes], q_ref[:, lanes]], 0).astype(F32)
        total = jnp.zeros((LANES, LANES), F32)
        for lag in range(FILT):
            total = total + shifted(extended, HALO - lag) * taps_ref[lag : lag + 1, lanes]
        q_short_ref[lanes, :] = total.T
        grad_z_ref[lanes, :] = (grad_ref[:, lanes].astype(F32) * gain_ref[:, lanes]).T


def conv_kernel(width, groups, payload_ref, taps_ref, first_ref, last_ref, twiddle_ref, inner_ref, outer_ref,
                conv_ref, spec_kv_ref, spec_filt_ref, k_ref, v_ref, filt_ref):
    rows = payload_ref.shape[0] // groups
    span = rows * width
    for index, ref in enumerate((k_ref, v_ref)):
        ref[...] = payload_ref[:, index * width : (index + 1) * width, :].astype(F32).reshape(groups * span, LANES)
    parts = payload_ref[:, 2 * width : 3 * width, :].astype(F32)
    filt_ref[...] = (parts[:rows] + parts[rows:]).reshape(span, LANES)
    for start in range(0, width, 2):
        blocks = []
        for channel in (start, start + 1):
            for group in range(groups):
                place = group * span + channel
                k_short = filtered(lagged(strided(k_ref, place, rows, width)), taps_ref, 1, channel)
                v_short = filtered(lagged(strided(v_ref, place, rows, width)), taps_ref, 2, channel)
                blocks.append(k_short * v_short)
        blocks += [strided(filt_ref, channel, rows, width) for channel in (start, start + 1)]
        spec = forward(blocks, first_ref, twiddle_ref, inner_ref)
        pairs = 2 * groups * rows
        spec_kv, spec_filt = spec[:pairs], spec[pairs:]
        spec_kv_ref[start * groups * rows : (start + 2) * groups * rows, :] = spec_kv
        spec_filt_ref[start * rows : (start + 2) * rows, :] = spec_filt
        products = []
        for side in range(2):
            for group in range(groups):
                block = (side * groups + group) * rows
                products.append(
                    times(spec_kv[block : block + rows], spec_filt[side * rows : (side + 1) * rows], False)
                )
        convs = inverse(jnp.concatenate(products, 0), rows, last_ref, twiddle_ref, outer_ref)
        for side in range(2):
            for group in range(groups):
                conv_ref[pl.ds(group * span + start + side, rows, stride=width), :] = convs[side * groups + group]


def stats_kernel(conv_ref, q_short_ref, grad_z_ref, stats_ref):
    squares = jnp.zeros((LANES, LANES), F32)
    prods = squares
    for start in range(0, conv_ref.shape[0], LANES):
        lanes = slice(start, start + LANES)
        y_out = q_short_ref[lanes, :] * conv_ref[lanes, :]
        squares = squares + y_out * y_out
        prods = prods + grad_z_ref[lanes, :] * y_out
    stats_ref[0:1, :] = jnp.sum(squares, 0, keepdims=True)
    stats_ref[1:2, :] = jnp.sum(prods, 0, keepdims=True)


def scales(stats_ref):
    rms = jnp.sqrt(stats_ref[0:1, :] / D + EPS)
    return rms, stats_ref[1:2, :] / (D * rms * rms * rms)


def dconv_kernel(conv_ref, q_short_ref, grad_z_ref, stats_ref, dconv_ref):
    rms, slope = scales(stats_ref)
    inverse_rms = 1.0 / rms
    for start in range(0, conv_ref.shape[0], LANES):
        lanes = slice(start, start + LANES)
        q_short = q_short_ref[lanes, :]
        y_out = q_short * conv_ref[lanes, :]
        dconv_ref[lanes, :] = (grad_z_ref[lanes, :] * inverse_rms - y_out * slope) * q_short


def norm_kernel(conv_ref, q_short_ref, grad_z_ref, stats_ref, q_ref, halo_ref, gain_ref,
                mixed_ref, grad_ref, edge_ref, short_ref):
    rms, slope = scales(stats_ref)
    inverse_rms = 1.0 / rms
    for start in range(0, conv_ref.shape[0], LANES):
        lanes = slice(start, start + LANES)
        conv = conv_ref[lanes, :]
        y_out = q_short_ref[lanes, :] * conv
        mixed_ref[:, lanes] = ((y_out / rms).T * gain_ref[:, lanes]).astype(BF16)
        grad = ((grad_z_ref[lanes, :] * inverse_rms - y_out * slope) * conv).T
        grad_ref[:, lanes] = grad
        edge_ref[:, lanes] = grad[:HALO]
        extended = jnp.concatenate([halo_ref[:, lanes], q_ref[:, lanes]], 0).astype(F32)
        for lag in range(FILT):
            short_ref[lag : lag + 1, lanes] = jnp.sum(grad * shifted(extended, HALO - lag), 0, keepdims=True)


def grad_q_kernel(grad_ref, edge_ref, taps_ref, out_ref):
    for start in range(0, grad_ref.shape[1], LANES):
        lanes = slice(start, start + LANES)
        extended = jnp.concatenate([grad_ref[:, lanes], edge_ref[:, lanes]], 0)
        total = jnp.zeros((LANES, LANES), F32)
        for lag in range(FILT):
            total = total + shifted(extended, lag) * taps_ref[lag : lag + 1, lanes]
        out_ref[:, lanes] = total.astype(BF16)


def back_kernel(width, groups, scale, dconv_ref, payload_ref, spec_kv_ref, spec_filt_ref, taps_ref, first_ref, last_ref,
                twiddle_ref, inner_ref, outer_ref, out_ref, k_ref, v_ref, grad_k_ref, grad_v_ref, dfilt_ref, short_ref):
    rows = payload_ref.shape[0] // groups
    span = rows * width
    for index, ref in enumerate((k_ref, v_ref)):
        ref[...] = payload_ref[:, index * width : (index + 1) * width, :].astype(F32).reshape(groups * span, LANES)
    short_ref[...] = jnp.zeros(short_ref.shape, F32)
    for start in range(0, width, 2):
        blocks = []
        for channel in (start, start + 1):
            for group in range(groups):
                blocks.append(strided(dconv_ref, group * span + channel, rows, width))
        spec = forward(blocks, first_ref, twiddle_ref, inner_ref)
        spec_filt = spec_filt_ref[start * rows : (start + 2) * rows, :]
        spec_kv = spec_kv_ref[start * groups * rows : (start + 2) * groups * rows, :]
        products = []
        filters = []
        for side in range(2):
            total = 0.0
            for group in range(groups):
                block = (side * groups + group) * rows
                part = spec[block : block + rows]
                products.append(times(spec_filt[side * rows : (side + 1) * rows], part, True))
                total = total + times(spec_kv[block : block + rows], part, True)
            filters.append(total)
        results = inverse(jnp.concatenate(products + filters, 0), rows, last_ref, twiddle_ref, outer_ref)
        for side in range(2):
            channel = start + side
            dfilt_ref[pl.ds(channel, rows, stride=width), :] = results[2 * groups + side] * scale
            for group in range(groups):
                place = group * span + channel
                dkv = results[side * groups + group]
                k_lags = lagged(strided(k_ref, place, rows, width))
                v_lags = lagged(strided(v_ref, place, rows, width))
                grad_k = dkv * filtered(v_lags, taps_ref, 2, channel)
                grad_v = dkv * filtered(k_lags, taps_ref, 1, channel)
                grad_k_ref[pl.ds(place, rows, stride=width), :] = filtered(led(grad_k), taps_ref, 1, channel)
                grad_v_ref[pl.ds(place, rows, stride=width), :] = filtered(led(grad_v), taps_ref, 2, channel)
                for branch, (grad, lags) in enumerate(((grad_k, k_lags), (grad_v, v_lags))):
                    for lag in range(FILT):
                        row = (branch * FILT + lag) * width + channel
                        short_ref[row : row + 1, :] += jnp.sum(grad * lags[lag], axis=0, keepdims=True)
    peers = groups * rows
    out_ref[:, :width, :] = grad_k_ref[...].reshape(peers, width, LANES).astype(BF16)
    out_ref[:, width : 2 * width, :] = grad_v_ref[...].reshape(peers, width, LANES).astype(BF16)
    dfilt = dfilt_ref[...].reshape(rows, width, LANES).astype(BF16)
    short = jnp.sum(short_ref[...].T, axis=0, keepdims=True) * scale
    high = short.astype(BF16).astype(F32)
    row = lax.broadcasted_iota(jnp.int32, (width, LANES), 0)
    short = jnp.where(row == 0, high, jnp.where(row == 1, short - high, 0.0)).astype(BF16)
    short = jnp.broadcast_to(short[None], (rows, width, LANES))
    for group in range(groups):
        into = slice(group * rows, (group + 1) * rows)
        out_ref[into, 2 * width : 3 * width, :] = dfilt
        out_ref[into, 3 * width :, :] = short


def unpack_kernel(width, payload_ref, grad_q_ref, grads_ref, long_ref, short_ref):
    grads_ref[0, 0] = grad_q_ref[...]
    for start in range(0, grad_q_ref.shape[1], LANES):
        lanes = slice(start, start + LANES)
        source = slice(start // width, (start + LANES) // width)
        for index in range(3):
            block = payload_ref[source, index * width : (index + 1) * width, :].astype(F32)
            block = block.reshape(LANES, LANES).T
            if index < 2:
                grads_ref[1 + index, 0, :, lanes] = block.astype(BF16)
            else:
                long_ref[:, lanes] = block
    tail = payload_ref[:, 3 * width :, :].astype(F32)
    short_ref[...] = tail[:, 0, :] + tail[:, 1, :]


def encode(values, top):
    root = jnp.sqrt(jnp.sqrt(jnp.abs(values))) * (60000.0 / top**0.25)
    return jnp.where(values < 0, -root, root).astype(jnp.float16)


def decode(code, top):
    root = code.astype(F32) * (top**0.25 / 60000.0)
    square = root * root
    return jnp.where(root < 0, -square * square, square * square)


PEERS = ("dp", "context")


def exchange(payload):
    return lax.all_to_all(payload, PEERS, split_axis=0, concat_axis=0, tiled=True)


def total_over_peers(values):
    for axis in PEERS:
        size = lax.axis_size(axis)
        bit = 1
        while bit < size:
            values = values + lax.ppermute(values, axis, [(i, i ^ bit) for i in range(size)])
            bit *= 2
    return values


def passed_along(values, by):
    size = lax.axis_size("context")
    pairs = [(i, i + by) for i in range(size) if 0 <= i + by < size]
    return lax.ppermute(values, "context", pairs)


def shards(q_in, k_in, v_in, short_filt, long_filt, norm_gain, grad_out):
    rows = lax.axis_size("context")
    groups = lax.axis_size("dp")
    peers = rows * groups
    channels = q_in.shape[2]
    width = channels // peers
    size = peers * width
    place = lax.axis_index(PEERS)
    first, last, twiddle, inner, outer = (jnp.asarray(t) for t in tables(rows))
    scratch = pltpu.VMEM((size, LANES), F32)
    scale = 1.0 / math.sqrt(groups * rows * LANES)
    gain = norm_gain[None]
    taps_q = jnp.pad(short_filt[0], ((0, 1), (0, 0)))
    taps = lax.dynamic_index_in_dim(short_filt.reshape(3 * FILT, peers, width), place, 1, keepdims=False)

    side = lax.axis_index("dp").astype(jnp.int32).reshape(1, 1)
    (payload,) = kernel_call(
        functools.partial(pack_kernel, width), [bf16(peers, 3 * width, LANES)], smem=(0,), count=4
    )(side, k_in[0], v_in[0], long_filt)
    payload = exchange(payload)

    halo = passed_along(q_in[0, LANES - HALO :], 1)
    q_short, grad_z = kernel_call(prepare_kernel, [f32(channels, LANES)] * 2, count=5)(
        q_in[0], halo, grad_out[0], taps_q, gain
    )

    conv, spec_kv, spec_filt = kernel_call(
        functools.partial(conv_kernel, width, groups),
        [f32(size, LANES), f32(size, 2 * LANES), f32(rows * width, 2 * LANES)],
        smem=(1,),
        scratch=[scratch, scratch, pltpu.VMEM((rows * width, LANES), F32)],
        count=7,
    )(payload, taps, first, last, twiddle, inner, outer)

    conv = exchange(encode(conv, 6.4e7).reshape(peers, width, LANES))
    conv = decode(conv, 6.4e7).reshape(size, LANES)
    (stats,) = kernel_call(stats_kernel, [f32(2, LANES)], count=3)(conv, q_short, grad_z)
    stats = lax.psum(stats, "tensor")
    (dconv,) = kernel_call(dconv_kernel, [f32(size, LANES)], count=4)(conv, q_short, grad_z, stats)
    dconv = exchange(encode(dconv, 4.6e8).reshape(peers, width, LANES))

    mixed, grad_0, edge, short_q = kernel_call(
        norm_kernel,
        [bf16(LANES, channels), f32(LANES, channels), f32(HALO, channels), f32(FILT, channels)],
        count=7,
    )(conv, q_short, grad_z, stats, q_in[0], halo, gain)
    edge = passed_along(edge, -1)
    (grad_q,) = kernel_call(grad_q_kernel, [bf16(LANES, channels)], count=3)(grad_0, edge, taps_q)
    short_q = total_over_peers(short_q) * scale

    dconv = decode(dconv, 4.6e8).reshape(size, LANES)
    (back,) = kernel_call(
        functools.partial(back_kernel, width, groups, scale),
        [bf16(peers, 4 * width, LANES)],
        smem=(4,),
        scratch=[scratch] * 4 + [pltpu.VMEM((rows * width, LANES), F32), pltpu.VMEM((LANES, LANES), F32)],
        count=10,
    )(dconv, payload, spec_kv, spec_filt, taps, first, last, twiddle, inner, outer)
    back = exchange(back)
    grads, grad_long, short = kernel_call(
        functools.partial(unpack_kernel, width),
        [bf16(3, 1, LANES, channels), f32(LANES, channels), f32(peers, LANES)],
        count=2,
    )(back, grad_q)
    short = short[:, : 2 * FILT * width].reshape(peers, 2, FILT, width).transpose(1, 2, 0, 3)
    grad_short = jnp.concatenate([short_q[None], short.reshape(2, FILT, channels)])
    return (mixed[None], grads, grad_long, grad_short)


def solution(mesh):
    in_specs = (
        P("dp", "context", "tensor"),
        P("dp", "context", "tensor"),
        P("dp", "context", "tensor"),
        P(None, None, "tensor"),
        P("context", "tensor"),
        P("tensor"),
        P("dp", "context", "tensor"),
    )
    out_specs = (
        P("dp", "context", "tensor"),
        P(None, "dp", "context", "tensor"),
        P("context", "tensor"),
        P(None, None, "tensor"),
    )
    return jax.shard_map(shards, mesh=mesh, in_specs=in_specs, out_specs=out_specs, check_vma=False)
```

time: 2770 us -> 258 us (0.09)
  waiting for transfers between devices: 2590 us -> 81.8 us
  starting transfers between devices: 40.9 us -> 84.1 us
  blocking collectives: 71.6 us -> 41.2 us
    psum x1 -> x0, waiting for transfers between devices: 2190 us -> none  [shards(): stats = lax.psum(stats, ('tensor', 'context'))]
    unnamed x3 -> x0, waiting for transfers between devices: 323 us -> none
    all_to_all x2 -> x1, blocking collectives: 71.6 us -> 32 us  [exchange(): lax.all_to_all(payload, PEERS, split_axis=0, concat_axis=0, tiled=True)]
    ppermute x3 -> x9, starting transfers between devices: 6.95 us -> 44.1 us  [the longest x7 35.1 us: total_over_peers(): lax.ppermute(values, axis, [(i, i ^ bit) for i in range(size)])]
    all_to_all x4 -> x3, waiting for transfers between devices: 69.5 us -> 51.5 us  [exchange(): lax.all_to_all(payload, PEERS, split_axis=0, concat_axis=0, tiled=True)]
  transfers between devices with their start and end apart: 9 -> 12, of which waited for: 7 -> 8; matrix products, arithmetic and copies ran while one was open for 0% -> 1% of each run, Pallas kernels for 1% -> 3%
where the time goes in v2:
time: 258 us; the launch traced here: 254 us
  starting transfers between devices  84.1 us (33%)
  waiting for transfers between devices  81.8 us (32%)
  blocking collectives  41.2 us (16%)
  Pallas kernels  31.6 us (12%)
  local copies, waits for them, and re-layouts  8.22 us (3%)
  other arithmetic  6.23 us (2%)
    all_to_all x3, waiting for transfers between devices, exchange(): lax.all_to_all(payload, PEERS, split_axis=0, concat_axis=0, tiled=True)  51.5 us
    all_to_all x3, starting transfers between devices, exchange(): lax.all_to_all(payload, PEERS, split_axis=0, concat_axis=0, tiled=True)  40 us
    ppermute x7, starting transfers between devices, total_over_peers(): lax.ppermute(values, axis, [(i, i ^ bit) for i in range(size)])  35.1 us
    all_to_all x1, blocking collectives, exchange(): lax.all_to_all(payload, PEERS, split_axis=0, concat_axis=0, tiled=True)  32 us
    ppermute x7, waiting for transfers between devices, total_over_peers(): lax.ppermute(values, axis, [(i, i ^ bit) for i in range(size)])  30.1 us
    psum x1, blocking collectives, shards(): stats = lax.psum(stats, 'tensor')  9.16 us
    ppermute x2, starting transfers between devices, passed_along(): return lax.ppermute(values, 'context', pairs)  8.99 us
    pallas_call x1, Pallas kernels, shards(): kernel_call(functools.partial(back_kernel, width, groups, scale), [bf16(p...  7.91 us
  transfers between devices with their start and end apart: 12, of which 8 were waited for; matrix products, arithmetic and copies ran while one was open for 1% of the time, Pallas kernels for 3%

profile of v2, /device:TPU:1, one launch (start us, length us, event | category | flops | bytes accessed | tf_op | source)
XLA Modules:
  0.0 254.1 jit_solution(7062350558048437744)
XLA Ops:
  0.6 2.5 shard_map.147
  3.1 20.6 %all-to-all-start = ((bf16[128,24,128]{2,1,0:T(8,128)(2,1)}), bf16[128,24,128]{2,1,0:T(8,128)(2,1)S(1)}, u32[]{:S(2)}, u32[]{:S(2)}) async-start(bf16[128,24,128]{2,1,0:T(8,128)(2,1)} %shard_map.147), calls=%async_computation | async-start | bytes 1572864 | tf_op jit(solution)/shard_map/all_to_all | solution.py:357
  23.7 0.8 reshape.33
  24.5 0.6 copy.31
  25.1 40.3 %all-to-all-done.payload_ref = bf16[128,24,128]{2,1,0:T(8,128)(2,1)S(1)} async-done(((bf16[128,24,128]{2,1,0:T(8,128)(2,1)}), bf16[128,24,128]{2,1,0:T(8,128)(2,1)S(1)}, u32[]{:S(2)}, u32[]{:S(2)}) %all-to-all-start) | async-done | bytes 786464 | tf_op jit(solution)/shard_map/all_to_all | solution.py:357
  65.4 0.9 copy-done
  66.3 6.6 %shard_map.148 = (f32[1024,128]{1,0:T(8,128)}, f32[1024,256]{1,0:T(8,128)}, f32[512,256]{1,0:T(8,128)}) custom-call(bf16[128,24,128]{2,1,0:T(8,128)(2,1)} %copy-done, f32[21,8]{1,0:T(8,128)} %bitcast.39, bf16[128,192]{1,0:T(8,128)(2,1)} %constant.43.clone.first_ref, bf16[64,384]{1,0:T(8,128)(2,1)} %constant.44.clone.last_ref, ...), custom_call_target="tpu_custom_call" | custom-call | tf_op jit(solution)/shard_map/pallas_call | solution.py:402
  72.9 2.1 fusion.9
  75.0 9.7 %all-to-all-start.1 = ((f16[128,8,128]{2,1,0:T(8,128)(2,1)}), f16[128,8,128]{2,1,0:T(8,128)(2,1)S(1)}, u32[]{:S(2)}, u32[]{:S(2)}) async-start(f16[128,8,128]{2,1,0:T(8,128)(2,1)} %fusion.9), calls=%async_computation.1 | async-start | bytes 524288 | tf_op jit(solution)/shard_map/all_to_all | solution.py:357
  84.7 0.7 slice_bitcast_fusion.1
  85.4 5.0 %collective-permute-start = (bf16[8,1024]{1,0:T(8,128)(2,1)S(1)}, bf16[8,1024]{1,0:T(8,128)(2,1)S(1)}, u32[]{:S(2)}, u32[]{:S(2)}) collective-permute-start(bf16[8,1024]{1,0:T(8,128)(2,1)S(1)} %slice_bitcast_fusion.1), channel_id=1, source_target_pairs={{0,1},{1,2},{2,3},{3,4},{4,5},{5,6},{6,7},{7,8},{8,9},{9,10},{10,1... | collective-permute-start | bytes 49160 | tf_op jit(solution)/shard_map/ppermute | solution.py:373
  90.5 0.6 pad.4.taps_ref
  91.1 0.2 collective-permute-done.halo_ref
  91.3 0.6 copy-done.3
  91.9 2.6 %shard_map.149 = (f32[1024,128]{1,0:T(8,128)}, f32[1024,128]{1,0:T(8,128)}) custom-call(bf16[128,1024]{1,0:T(8,128)(2,1)} %bitcast.33, bf16[8,1024]{1,0:T(8,128)(2,1)} %copy-done.3, bf16[128,1024]{1,0:T(8,128)(2,1)} %bitcast.35, f32[8,1024]{1,0:T(8,128)} %pad.4.taps_ref, f32[1,1024]{1,0:T(1,128)} %bitcast.42), custom_call_target="tpu_custom_call" | custom-call | tf_op jit(solution)/shard_map/pallas_call | solution.py:398
  94.5 11.2 %all-to-all-done.1 = f16[128,8,128]{2,1,0:T(8,128)(2,1)S(1)} async-done(((f16[128,8,128]{2,1,0:T(8,128)(2,1)}), f16[128,8,128]{2,1,0:T(8,128)(2,1)S(1)}, u32[]{:S(2)}, u32[]{:S(2)}) %all-to-all-start.1) | async-done | bytes 262176 | tf_op jit(solution)/shard_map/all_to_all | solution.py:357
  105.7 0.9 fusion.2.conv_ref
  106.6 2.0 shard_map.150
  108.6 9.2 %psum.7.stats_ref = f32[2,128]{1,0:T(2,128)} all-reduce(f32[2,128]{1,0:T(2,128)} %shard_map.150), channel_id=1, replica_groups=mesh['dp'=2,'tensor'=4,'context'=64] {'tensor'}, use_global_device_ids=true, to_apply=%region_0.1 | all-reduce | flops 256 | bytes 2048 | tf_op jit(solution)/shard_map/psum | solution.py:413
  117.8 2.3 shard_map.152
  120.0 1.4 fusion.8
  121.4 32.0 %all_to_all.20 = f16[128,8,128]{2,1,0:T(8,128)(2,1)S(1)} all-to-all(f16[128,8,128]{2,1,0:T(8,128)(2,1)S(1)} %fusion.8), channel_id=1, replica_groups=mesh['dp'=2,'tensor'=4,'context'=64] {'dp','context'}, dimensions={0} | all-to-all | bytes 524288 | tf_op jit(solution)/shard_map/all_to_all | solution.py:357
  153.5 0.9 fusion.5.dconv_ref
  154.4 7.9 %shard_map.153 = bf16[128,32,128]{2,1,0:T(8,128)(2,1)} custom-call(f32[1024,128]{1,0:T(8,128)} %fusion.5.dconv_ref, bf16[128,24,128]{2,1,0:T(8,128)(2,1)} %copy-done, f32[1024,256]{1,0:T(8,128)} %get-tuple-element.20.spec_kv_ref, f32[512,256]{1,0:T(8,128)} %get-tuple-element.21.spec_filt_ref, f32[21,8]{1,0:T(8,128)} %bitcast.40, ...), custom_call_target="tpu_custom_call" | custom-call | tf_op jit(solution)/shard_map/pallas_call | solution.py:427
  162.3 9.8 %all-to-all-start.3 = ((bf16[128,32,128]{2,1,0:T(8,128)(2,1)}), bf16[128,32,128]{2,1,0:T(8,128)(2,1)S(1)}, u32[]{:S(2)}, u32[]{:S(2)}) async-start(bf16[128,32,128]{2,1,0:T(8,128)(2,1)} %shard_map.153), calls=%async_computation.3 | async-start | bytes 2097152 | tf_op jit(solution)/shard_map/all_to_all | solution.py:357
  172.1 2.9 %shard_map.151 = (bf16[128,1024]{1,0:T(8,128)(2,1)}, f32[128,1024]{1,0:T(8,128)}, f32[8,1024]{1,0:T(8,128)}, f32[7,1024]{1,0:T(8,128)}) custom-call(f32[1024,128]{1,0:T(8,128)} %fusion.2.conv_ref, f32[1024,128]{1,0:T(8,128)} %get-tuple-element.17.q_short_ref, f32[1024,128]{1,0:T(8,128)} %get-tuple-element.18.grad_z_ref, f32[2,128]{1,0:T(2,128)} %psum.7.stats_ref, ...), custom_call_target="tpu_custom_call" | custom-call | tf_op jit(solution)/shard_map/pallas_call | solution.py:417
  175.1 3.7 %collective-permute-start.2 = (f32[7,1024]{1,0:T(8,128)}, f32[7,1024]{1,0:T(8,128)S(1)}, u32[]{:S(2)}, u32[]{:S(2)}) collective-permute-start(f32[7,1024]{1,0:T(8,128)} %get-tuple-element.26), channel_id=1, source_target_pairs={{0,256},{256,0},{1,257},{257,1},{2,258},{258,2},{3,259},{259,3},{4... | collective-permute-start | bytes 86024 | tf_op jit(solution)/shard_map/ppermute | solution.py:365
  178.8 2.0 collective-permute-done.2
  180.7 0.8 add.34
  181.5 3.4 %collective-permute-start.3 = (f32[7,1024]{1,0:T(8,128)S(1)}, f32[7,1024]{1,0:T(8,128)S(1)}, u32[]{:S(2)}, u32[]{:S(2)}) collective-permute-start(f32[7,1024]{1,0:T(8,128)S(1)} %add.34), channel_id=1, source_target_pairs={{0,1},{1,0},{2,3},{3,2},{4,5},{5,4},{6,7},{7,6},{8,9},{9,8},{10,11... | collective-permute-start | bytes 86024 | tf_op jit(solution)/shard_map/ppermute | solution.py:365
  184.9 0.8 collective-permute-done.3
  185.7 4.1 %collective-permute-start.4 = (f32[7,1024]{1,0:T(8,128)S(1)}, f32[7,1024]{1,0:T(8,128)S(1)}, u32[]{:S(2)}, u32[]{:S(2)}) collective-permute-start(f32[7,1024]{1,0:T(8,128)S(1)} %add.35), channel_id=1, source_target_pairs={{0,2},{1,3},{2,0},{3,1},{4,6},{5,7},{6,4},{7,5},{8,10},{9,11},{10,... | collective-permute-start | bytes 86024 | tf_op jit(solution)/shard_map/ppermute | solution.py:365
  189.8 2.4 collective-permute-done.4
  192.2 2.6 %collective-permute-start.5 = (f32[7,1024]{1,0:T(8,128)S(1)}, f32[7,1024]{1,0:T(8,128)S(1)}, u32[]{:S(2)}, u32[]{:S(2)}) collective-permute-start(f32[7,1024]{1,0:T(8,128)S(1)} %add.36), channel_id=1, source_target_pairs={{0,4},{1,5},{2,6},{3,7},{4,0},{5,1},{6,2},{7,3},{8,12},{9,13},{10,... | collective-permute-start | bytes 86024 | tf_op jit(solution)/shard_map/ppermute | solution.py:365
  194.9 22.5 %collective-permute-done.5 = f32[7,1024]{1,0:T(8,128)S(1)} collective-permute-done((f32[7,1024]{1,0:T(8,128)S(1)}, f32[7,1024]{1,0:T(8,128)S(1)}, u32[]{:S(2)}, u32[]{:S(2)}) %collective-permute-start.5) | collective-permute-done | bytes 28704 | tf_op jit(solution)/shard_map/ppermute | solution.py:365
  217.4 3.4 %collective-permute-start.6 = (f32[7,1024]{1,0:T(8,128)S(1)}, f32[7,1024]{1,0:T(8,128)S(1)}, u32[]{:S(2)}, u32[]{:S(2)}) collective-permute-start(f32[7,1024]{1,0:T(8,128)S(1)} %add.37), channel_id=1, source_target_pairs={{0,8},{1,9},{2,10},{3,11},{4,12},{5,13},{6,14},{7,15},{8,0},{9,1},... | collective-permute-start | bytes 86024 | tf_op jit(solution)/shard_map/ppermute | solution.py:365
  220.7 2.5 collective-permute-done.6
  223.2 7.2 %collective-permute-start.7 = (f32[7,1024]{1,0:T(8,128)S(1)}, f32[7,1024]{1,0:T(8,128)S(1)}, u32[]{:S(2)}, u32[]{:S(2)}) collective-permute-start(f32[7,1024]{1,0:T(8,128)S(1)} %add.38), channel_id=1, source_target_pairs={{0,16},{1,17},{2,18},{3,19},{4,20},{5,21},{6,22},{7,23},{8,24},{9,... | collective-permute-start | bytes 86024 | tf_op jit(solution)/shard_map/ppermute | solution.py:365
  230.5 4.0 %collective-permute-start.1 = (f32[8,1024]{1,0:T(8,128)}, f32[8,1024]{1,0:T(8,128)S(1)}, u32[]{:S(2)}, u32[]{:S(2)}) collective-permute-start(f32[8,1024]{1,0:T(8,128)} %get-tuple-element.23), channel_id=1, source_target_pairs={{1,0},{2,1},{3,2},{4,3},{5,4},{6,5},{7,6},{8,7},{9,8},{10,9},{11,1... | collective-permute-start | bytes 98312 | tf_op jit(solution)/shard_map/ppermute | solution.py:373
  234.5 10.7 %collective-permute-start.8 = (f32[7,1024]{1,0:T(8,128)S(1)}, f32[7,1024]{1,0:T(8,128)S(1)}, u32[]{:S(2)}, u32[]{:S(2)}) collective-permute-start(f32[7,1024]{1,0:T(8,128)S(1)} %add.39), channel_id=1, source_target_pairs={{0,32},{1,33},{2,34},{3,35},{4,36},{5,37},{6,38},{7,39},{8,40},{9,... | collective-permute-start | bytes 86024 | tf_op jit(solution)/shard_map/ppermute | solution.py:365
  245.1 0.6 copy-done.4
  245.8 2.2 shard_map.154.grad_q_ref
  248.0 1.0 copy-done.1
  249.0 2.6 %shard_map.155 = (bf16[3,1,128,1024]{3,2,1,0:T(8,128)(2,1)}, f32[128,1024]{1,0:T(8,128)}, f32[128,128]{1,0:T(8,128)}) custom-call(bf16[128,32,128]{2,1,0:T(8,128)(2,1)} %copy-done.1, bf16[128,1024]{1,0:T(8,128)(2,1)} %shard_map.154.grad_q_ref), custom_call_target="tpu_custom_call" | custom-call | tf_op jit(solution)/shard_map/pallas_call | solution.py:435
  251.6 0.9 copy.25
  252.6 0.3 copy.26
  252.9 0.5 reshape.39
  253.4 0.7 copy.28
  (20 shorter events, 0.2 us)
Async XLA Ops:
  0.6 23.1 %copy-start.2 = (f32[3,7,1024]{2,1,0:T(8,128)S(1)}, f32[3,7,1024]{2,1,0:T(8,128)}, u32[]{:S(2)}) copy-start(f32[3,7,1024]{2,1,0:T(8,128)} %param.15) | copy-start | bytes 258052
  3.1 62.3 %all-to-all-start = ((bf16[128,24,128]{2,1,0:T(8,128)(2,1)}), bf16[128,24,128]{2,1,0:T(8,128)(2,1)S(1)}, u32[]{:S(2)}, u32[]{:S(2)}) async-start(bf16[128,24,128]{2,1,0:T(8,128)(2,1)} %shard_map.147), calls=%async_computation | async-start | bytes 1572864 | tf_op jit(solution)/shard_map/all_to_all | solution.py:357
  65.4 0.9 copy-start
  75.0 30.6 %all-to-all-start.1 = ((f16[128,8,128]{2,1,0:T(8,128)(2,1)}), f16[128,8,128]{2,1,0:T(8,128)(2,1)S(1)}, u32[]{:S(2)}, u32[]{:S(2)}) async-start(f16[128,8,128]{2,1,0:T(8,128)(2,1)} %fusion.9), calls=%async_computation.1 | async-start | bytes 524288 | tf_op jit(solution)/shard_map/all_to_all | solution.py:357
  85.4 5.9 %collective-permute-start = (bf16[8,1024]{1,0:T(8,128)(2,1)S(1)}, bf16[8,1024]{1,0:T(8,128)(2,1)S(1)}, u32[]{:S(2)}, u32[]{:S(2)}) collective-permute-start(bf16[8,1024]{1,0:T(8,128)(2,1)S(1)} %slice_bitcast_fusion.1), channel_id=1, source_target_pairs={{0,1},{1,2},{2,3},{3,4},{4,5},{5,6},{6,7},{7,8},{8,9},{9,10},{10,1... | collective-permute-start | bytes 49160 | tf_op jit(solution)/shard_map/ppermute | solution.py:373
  91.3 0.6 copy-start.3
  162.3 85.7 %all-to-all-start.3 = ((bf16[128,32,128]{2,1,0:T(8,128)(2,1)}), bf16[128,32,128]{2,1,0:T(8,128)(2,1)S(1)}, u32[]{:S(2)}, u32[]{:S(2)}) async-start(bf16[128,32,128]{2,1,0:T(8,128)(2,1)} %shard_map.153), calls=%async_computation.3 | async-start | bytes 2097152 | tf_op jit(solution)/shard_map/all_to_all | solution.py:357
  175.1 5.7 %collective-permute-start.2 = (f32[7,1024]{1,0:T(8,128)}, f32[7,1024]{1,0:T(8,128)S(1)}, u32[]{:S(2)}, u32[]{:S(2)}) collective-permute-start(f32[7,1024]{1,0:T(8,128)} %get-tuple-element.26), channel_id=1, source_target_pairs={{0,256},{256,0},{1,257},{257,1},{2,258},{258,2},{3,259},{259,3},{4... | collective-permute-start | bytes 86024 | tf_op jit(solution)/shard_map/ppermute | solution.py:365
  181.5 4.2 %collective-permute-start.3 = (f32[7,1024]{1,0:T(8,128)S(1)}, f32[7,1024]{1,0:T(8,128)S(1)}, u32[]{:S(2)}, u32[]{:S(2)}) collective-permute-start(f32[7,1024]{1,0:T(8,128)S(1)} %add.34), channel_id=1, source_target_pairs={{0,1},{1,0},{2,3},{3,2},{4,5},{5,4},{6,7},{7,6},{8,9},{9,8},{10,11... | collective-permute-start | bytes 86024 | tf_op jit(solution)/shard_map/ppermute | solution.py:365
  185.7 6.5 %collective-permute-start.4 = (f32[7,1024]{1,0:T(8,128)S(1)}, f32[7,1024]{1,0:T(8,128)S(1)}, u32[]{:S(2)}, u32[]{:S(2)}) collective-permute-start(f32[7,1024]{1,0:T(8,128)S(1)} %add.35), channel_id=1, source_target_pairs={{0,2},{1,3},{2,0},{3,1},{4,6},{5,7},{6,4},{7,5},{8,10},{9,11},{10,... | collective-permute-start | bytes 86024 | tf_op jit(solution)/shard_map/ppermute | solution.py:365
  192.2 25.1 %collective-permute-start.5 = (f32[7,1024]{1,0:T(8,128)S(1)}, f32[7,1024]{1,0:T(8,128)S(1)}, u32[]{:S(2)}, u32[]{:S(2)}) collective-permute-start(f32[7,1024]{1,0:T(8,128)S(1)} %add.36), channel_id=1, source_target_pairs={{0,4},{1,5},{2,6},{3,7},{4,0},{5,1},{6,2},{7,3},{8,12},{9,13},{10,... | collective-permute-start | bytes 86024 | tf_op jit(solution)/shard_map/ppermute | solution.py:365
  217.4 5.8 %collective-permute-start.6 = (f32[7,1024]{1,0:T(8,128)S(1)}, f32[7,1024]{1,0:T(8,128)S(1)}, u32[]{:S(2)}, u32[]{:S(2)}) collective-permute-start(f32[7,1024]{1,0:T(8,128)S(1)} %add.37), channel_id=1, source_target_pairs={{0,8},{1,9},{2,10},{3,11},{4,12},{5,13},{6,14},{7,15},{8,0},{9,1},... | collective-permute-start | bytes 86024 | tf_op jit(solution)/shard_map/ppermute | solution.py:365
  223.2 11.2 %collective-permute-start.7 = (f32[7,1024]{1,0:T(8,128)S(1)}, f32[7,1024]{1,0:T(8,128)S(1)}, u32[]{:S(2)}, u32[]{:S(2)}) collective-permute-start(f32[7,1024]{1,0:T(8,128)S(1)} %add.38), channel_id=1, source_target_pairs={{0,16},{1,17},{2,18},{3,19},{4,20},{5,21},{6,22},{7,23},{8,24},{9,... | collective-permute-start | bytes 86024 | tf_op jit(solution)/shard_map/ppermute | solution.py:365
  230.5 14.7 %collective-permute-start.1 = (f32[8,1024]{1,0:T(8,128)}, f32[8,1024]{1,0:T(8,128)S(1)}, u32[]{:S(2)}, u32[]{:S(2)}) collective-permute-start(f32[8,1024]{1,0:T(8,128)} %get-tuple-element.23), channel_id=1, source_target_pairs={{1,0},{2,1},{3,2},{4,3},{5,4},{6,5},{7,6},{8,7},{9,8},{10,9},{11,1... | collective-permute-start | bytes 98312 | tf_op jit(solution)/shard_map/ppermute | solution.py:373
  234.5 13.5 %collective-permute-start.8 = (f32[7,1024]{1,0:T(8,128)S(1)}, f32[7,1024]{1,0:T(8,128)S(1)}, u32[]{:S(2)}, u32[]{:S(2)}) collective-permute-start(f32[7,1024]{1,0:T(8,128)S(1)} %add.39), channel_id=1, source_target_pairs={{0,32},{1,33},{2,34},{3,35},{4,36},{5,37},{6,38},{7,39},{8,40},{9,... | collective-permute-start | bytes 86024 | tf_op jit(solution)/shard_map/ppermute | solution.py:365
  245.1 0.6 copy-start.4
  248.0 1.0 copy-start.1

commit v3 on v2

--- a/solution.py
+++ b/solution.py
@@ -17,7 +17,6 @@
 BF16 = jnp.bfloat16
 VMEM = pl.BlockSpec(memory_space=pltpu.VMEM)
 SMEM = pl.BlockSpec(memory_space=pltpu.SMEM)
-PARAMS = pltpu.CompilerParams(vmem_limit_bytes=56 * 2**20)
 
 
 def halves(table):
@@ -127,14 +126,14 @@
     return ref[pl.ds(start, count, stride=step), :]
 
 
-def kernel_call(kernel, shapes, smem=(), scratch=(), count=0):
+def kernel_call(kernel, shapes, smem=(), scratch=(), count=0, mib=6):
     return pl.pallas_call(
         kernel,
         out_shape=shapes,
         in_specs=[SMEM if index in smem else VMEM for index in range(count)],
         out_specs=[VMEM] * len(shapes),
         scratch_shapes=list(scratch),
-        compiler_params=PARAMS,
+        compiler_params=pltpu.CompilerParams(vmem_limit_bytes=mib * 2**20),
     )
 
 
@@ -220,13 +219,17 @@
         y_out = q_short_ref[lanes, :] * conv_ref[lanes, :]
         squares = squares + y_out * y_out
         prods = prods + grad_z_ref[lanes, :] * y_out
-    stats_ref[0:1, :] = jnp.sum(squares, 0, keepdims=True)
-    stats_ref[1:2, :] = jnp.sum(prods, 0, keepdims=True)
+    squares = jnp.sum(squares, 0, keepdims=True)
+    prods = jnp.sum(prods, 0, keepdims=True)
+    for peer in range(stats_ref.shape[0]):
+        stats_ref[peer, 0:1, :] = squares
+        stats_ref[peer, 1:2, :] = prods
 
 
 def scales(stats_ref):
-    rms = jnp.sqrt(stats_ref[0:1, :] / D + EPS)
-    return rms, stats_ref[1:2, :] / (D * rms * rms * rms)
+    stats = jnp.sum(stats_ref[...], axis=0)
+    rms = jnp.sqrt(stats[0:1] / D + EPS)
+    return rms, stats[1:2] / (D * rms * rms * rms)
 
 
 def dconv_kernel(conv_ref, q_short_ref, grad_z_ref, stats_ref, dconv_ref):
@@ -270,9 +273,11 @@
                 twiddle_ref, inner_ref, outer_ref, out_ref, k_ref, v_ref, grad_k_ref, grad_v_ref, dfilt_ref, short_ref):
     rows = payload_ref.shape[0] // groups
     span = rows * width
+    part_width = width // groups
     for index, ref in enumerate((k_ref, v_ref)):
         ref[...] = payload_ref[:, index * width : (index + 1) * width, :].astype(F32).reshape(groups * span, LANES)
     short_ref[...] = jnp.zeros(short_ref.shape, F32)
+    dfilt_ref[...] = jnp.zeros(dfilt_ref.shape, F32)
     for start in range(0, width, 2):
         blocks = []
         for channel in (start, start + 1):
@@ -294,7 +299,8 @@
         results = inverse(jnp.concatenate(products + filters, 0), rows, last_ref, twiddle_ref, outer_ref)
         for side in range(2):
             channel = start + side
-            dfilt_ref[pl.ds(channel, rows, stride=width), :] = results[2 * groups + side] * scale
+            target = channel // part_width * span + channel % part_width
+            dfilt_ref[pl.ds(target, rows, stride=width), :] = results[2 * groups + side] * scale
             for group in range(groups):
                 place = group * span + channel
                 dkv = results[side * groups + group]
@@ -311,32 +317,41 @@
     peers = groups * rows
     out_ref[:, :width, :] = grad_k_ref[...].reshape(peers, width, LANES).astype(BF16)
     out_ref[:, width : 2 * width, :] = grad_v_ref[...].reshape(peers, width, LANES).astype(BF16)
-    dfilt = dfilt_ref[...].reshape(rows, width, LANES).astype(BF16)
     short = jnp.sum(short_ref[...].T, axis=0, keepdims=True) * scale
     high = short.astype(BF16).astype(F32)
-    row = lax.broadcasted_iota(jnp.int32, (width, LANES), 0)
-    short = jnp.where(row == 0, high, jnp.where(row == 1, short - high, 0.0)).astype(BF16)
-    short = jnp.broadcast_to(short[None], (rows, width, LANES))
-    for group in range(groups):
-        into = slice(group * rows, (group + 1) * rows)
-        out_ref[into, 2 * width : 3 * width, :] = dfilt
-        out_ref[into, 3 * width :, :] = short
-
-
-def unpack_kernel(width, payload_ref, grad_q_ref, grads_ref, long_ref, short_ref):
+    for row, values in enumerate((high, short - high)):
+        dfilt_ref[pl.ds(part_width + row, peers, stride=width), :] = jnp.broadcast_to(values, (peers, LANES))
+    out_ref[:, 2 * width :, :] = dfilt_ref[...].reshape(peers, width, LANES).astype(BF16)
+
+
+def part_kernel(width, part_width, payload_ref, part_ref, short_ref, rows_ref, out_ref):
+    peers = payload_ref.shape[0]
+    rows_ref[...] = payload_ref[:, 2 * width :, :].astype(F32).reshape(peers * width, LANES)
+    for row in range(part_width):
+        out_ref[pl.ds(row, peers, stride=part_width), :] = strided(rows_ref, row, peers, width)
+    part_ref[...] = out_ref[...].astype(BF16)
+    short_ref[...] = strided(rows_ref, part_width, peers, width) + strided(rows_ref, part_width + 1, peers, width)
+
+
+def unpack_kernel(width, payload_ref, grad_q_ref, grads_ref):
     grads_ref[0, 0] = grad_q_ref[...]
     for start in range(0, grad_q_ref.shape[1], LANES):
-        lanes = slice(start, start + LANES)
         source = slice(start // width, (start + LANES) // width)
-        for index in range(3):
+        for index in range(2):
             block = payload_ref[source, index * width : (index + 1) * width, :].astype(F32)
-            block = block.reshape(LANES, LANES).T
-            if index < 2:
-                grads_ref[1 + index, 0, :, lanes] = block.astype(BF16)
-            else:
-                long_ref[:, lanes] = block
-    tail = payload_ref[:, 3 * width :, :].astype(F32)
-    short_ref[...] = tail[:, 0, :] + tail[:, 1, :]
+            grads_ref[1 + index, 0, :, start : start + LANES] = block.reshape(LANES, LANES).T.astype(BF16)
+
+
+def join_kernel(width, part_width, side_ref, own_ref, other_ref, long_ref, from_ref, rows_ref):
+    peers = long_ref.shape[1] // width
+    for order, ref in ((side_ref[0, 0], own_ref), (1 - side_ref[0, 0], other_ref)):
+        from_ref[...] = ref[...].astype(F32)
+        for row in range(part_width):
+            rows_ref[pl.ds(order * part_width + row, peers, stride=width), :] = strided(
+                from_ref, row, peers, part_width
+            )
+    for start in range(0, long_ref.shape[1], LANES):
+        long_ref[:, start : start + LANES] = rows_ref[start : start + LANES, :].T
 
 
 def encode(values, top):
@@ -357,14 +372,8 @@
     return lax.all_to_all(payload, PEERS, split_axis=0, concat_axis=0, tiled=True)
 
 
-def total_over_peers(values):
-    for axis in PEERS:
-        size = lax.axis_size(axis)
-        bit = 1
-        while bit < size:
-            values = values + lax.ppermute(values, axis, [(i, i ^ bit) for i in range(size)])
-            bit *= 2
-    return values
+def paired_sum(values, axis, bit):
+    return values + lax.ppermute(values, axis, [(i, i ^ bit) for i in range(lax.axis_size(axis))])
 
 
 def passed_along(values, by):
@@ -405,12 +414,13 @@
         smem=(1,),
         scratch=[scratch, scratch, pltpu.VMEM((rows * width, LANES), F32)],
         count=7,
+        mib=10,
     )(payload, taps, first, last, twiddle, inner, outer)
 
     conv = exchange(encode(conv, 6.4e7).reshape(peers, width, LANES))
     conv = decode(conv, 6.4e7).reshape(size, LANES)
-    (stats,) = kernel_call(stats_kernel, [f32(2, LANES)], count=3)(conv, q_short, grad_z)
-    stats = lax.psum(stats, "tensor")
+    (stats,) = kernel_call(stats_kernel, [f32(lax.axis_size("tensor"), 2, LANES)], count=3)(conv, q_short, grad_z)
+    stats = lax.all_to_all(stats, "tensor", split_axis=0, concat_axis=0, tiled=True)
     (dconv,) = kernel_call(dconv_kernel, [f32(size, LANES)], count=4)(conv, q_short, grad_z, stats)
     dconv = exchange(encode(dconv, 4.6e8).reshape(peers, width, LANES))
 
@@ -420,25 +430,45 @@
         count=7,
     )(conv, q_short, grad_z, stats, q_in[0], halo, gain)
     edge = passed_along(edge, -1)
+    for bit in range(groups.bit_length() - 1):
+        short_q = paired_sum(short_q, "dp", 1 << bit)
+    short_q = paired_sum(short_q, "context", 1)
+    dconv, mixed, grad_0, edge, short_q = lax.optimization_barrier((dconv, mixed, grad_0, edge, short_q))
     (grad_q,) = kernel_call(grad_q_kernel, [bf16(LANES, channels)], count=3)(grad_0, edge, taps_q)
-    short_q = total_over_peers(short_q) * scale
+    for bit in range(1, rows.bit_length() - 1):
+        short_q = paired_sum(short_q, "context", 1 << bit)
 
     dconv = decode(dconv, 4.6e8).reshape(size, LANES)
     (back,) = kernel_call(
         functools.partial(back_kernel, width, groups, scale),
-        [bf16(peers, 4 * width, LANES)],
+        [bf16(peers, 3 * width, LANES)],
         smem=(4,),
-        scratch=[scratch] * 4 + [pltpu.VMEM((rows * width, LANES), F32), pltpu.VMEM((LANES, LANES), F32)],
+        scratch=[scratch] * 5 + [pltpu.VMEM((LANES, LANES), F32)],
         count=10,
+        mib=10,
     )(dconv, payload, spec_kv, spec_filt, taps, first, last, twiddle, inner, outer)
     back = exchange(back)
-    grads, grad_long, short = kernel_call(
-        functools.partial(unpack_kernel, width),
-        [bf16(3, 1, LANES, channels), f32(LANES, channels), f32(peers, LANES)],
-        count=2,
+    part_width = width // groups
+    part_scratch = pltpu.VMEM((peers * part_width, LANES), F32)
+    part, short = kernel_call(
+        functools.partial(part_kernel, width, part_width),
+        [bf16(peers * part_width, LANES), f32(peers, LANES)],
+        scratch=[scratch, part_scratch],
+        count=1,
+    )(back)
+    other = lax.ppermute(part, "dp", [(i, i ^ 1) for i in range(groups)])
+    (grads,) = kernel_call(
+        functools.partial(unpack_kernel, width), [bf16(3, 1, LANES, channels)], count=2
     )(back, grad_q)
+    (grad_long,) = kernel_call(
+        functools.partial(join_kernel, width, part_width),
+        [f32(LANES, channels)],
+        smem=(0,),
+        scratch=[part_scratch, scratch],
+        count=3,
+    )(side, part, other)
     short = short[:, : 2 * FILT * width].reshape(peers, 2, FILT, width).transpose(1, 2, 0, 3)
-    grad_short = jnp.concatenate([short_q[None], short.reshape(2, FILT, channels)])
+    grad_short = jnp.concatenate([short_q[None] * scale, short.reshape(2, FILT, channels)])
     return (mixed[None], grads, grad_long, grad_short)
 
 

time: 258 us -> 244 us (0.946)
  blocking collectives: 41.2 us -> 7.96 us
  starting transfers between devices: 84.1 us -> 102 us
  Pallas kernels: 31.6 us -> 17.9 us
  waiting for transfers between devices: 81.8 us -> 91.1 us
  local copies, waits for them, and re-layouts: 8.22 us -> 15.7 us
    all_to_all x1, blocking collectives: 32 us -> 7.96 us  [shards(): lax.all_to_all(stats, 'tensor', split_axis=0, concat_axis=0, tiled=True)]
    all_to_all x3 -> x4, starting transfers between devices: 40 us -> 53.6 us  [exchange(): lax.all_to_all(payload, PEERS, split_axis=0, concat_axis=0, tiled=True)]
    psum x1 -> x0, blocking collectives: 9.16 us -> none  [shards(): stats = lax.psum(stats, 'tensor')]
    unnamed x11 -> x53, local copies, waits for them, and re-layouts: 3.77 us -> 12 us
    ppermute x7 -> x8, starting transfers between devices: 35.1 us -> 40.8 us  [the longest x7 36.6 us: paired_sum(): lax.ppermute(values, axis, [(i, i ^ bit) for i in range(lax.axis_size(axi...]
    all_to_all x3 -> x4, waiting for transfers between devices: 51.5 us -> 56.9 us  [exchange(): lax.all_to_all(payload, PEERS, split_axis=0, concat_axis=0, tiled=True)]
    ppermute x7 -> x8, waiting for transfers between devices: 30.1 us -> 32.1 us  [the longest x7 32.1 us: paired_sum(): lax.ppermute(values, axis, [(i, i ^ bit) for i in range(lax.axis_size(axi...]
  transfers between devices with their start and end apart: 12 -> 14, of which waited for: 8 -> 10; matrix products, arithmetic and copies ran while one was open for 1% -> 2% of each run, Pallas kernels for 3% -> 2%
where the time goes in v3:
time: 244 us; the launch traced here: 240 us
  starting transfers between devices  102 us (42%)
  waiting for transfers between devices  91.1 us (37%)
  Pallas kernels  17.9 us (7%)
  local copies, waits for them, and re-layouts  15.7 us (6%)
  blocking collectives  7.96 us (3%)
  other arithmetic  4.41 us (2%)
    all_to_all x4, waiting for transfers between devices, exchange(): lax.all_to_all(payload, PEERS, split_axis=0, concat_axis=0, tiled=True)  56.9 us
    all_to_all x4, starting transfers between devices, exchange(): lax.all_to_all(payload, PEERS, split_axis=0, concat_axis=0, tiled=True)  53.6 us
    ppermute x7, starting transfers between devices, paired_sum(): lax.ppermute(values, axis, [(i, i ^ bit) for i in range(lax.axis_size(axi...  36.6 us
    ppermute x7, waiting for transfers between devices, paired_sum(): lax.ppermute(values, axis, [(i, i ^ bit) for i in range(lax.axis_size(axi...  32.1 us
    unnamed x53, local copies, waits for them, and re-layouts  12 us
    all_to_all x1, blocking collectives, shards(): lax.all_to_all(stats, 'tensor', split_axis=0, concat_axis=0, tiled=True)  7.96 us
    ppermute x2, starting transfers between devices, passed_along(): return lax.ppermute(values, 'context', pairs)  7.59 us
    pallas_call x1, Pallas kernels, shards(): kernel_call(functools.partial(back_kernel, width, groups, scale), [bf16(p...  6.56 us
  transfers between devices with their start and end apart: 14, of which 10 were waited for; matrix products, arithmetic and copies ran while one was open for 2% of the time, Pallas kernels for 2%

profile of v3, /device:TPU:1, one launch (start us, length us, event | category | flops | bytes accessed | tf_op | source)
XLA Modules:
  0.0 240.1 jit_solution(7148579949870868448)
XLA Ops:
  0.6 1.0 copy-done.7
  1.7 0.9 copy-done.14
  2.6 0.9 copy-done.15
  3.6 1.2 shard_map.147
  4.8 20.7 %all-to-all-start = ((bf16[128,24,128]{2,1,0:T(8,128)(2,1)}), bf16[128,24,128]{2,1,0:T(8,128)(2,1)S(1)}, u32[]{:S(2)}, u32[]{:S(2)}) async-start(bf16[128,24,128]{2,1,0:T(8,128)(2,1)} %shard_map.147), calls=%async_computation | async-start | bytes 1572864 | tf_op jit(solution)/shard_map/all_to_all | solution.py:372
  25.6 1.9 reshape.34
  27.5 0.9 constant_dynamic-slice_fusion
  28.4 38.9 %all-to-all-done.payload_ref = bf16[128,24,128]{2,1,0:T(8,128)(2,1)S(1)} async-done(((bf16[128,24,128]{2,1,0:T(8,128)(2,1)}), bf16[128,24,128]{2,1,0:T(8,128)(2,1)S(1)}, u32[]{:S(2)}, u32[]{:S(2)}) %all-to-all-start) | async-done | bytes 786464 | tf_op jit(solution)/shard_map/all_to_all | solution.py:372
  67.3 5.1 %shard_map.148 = (f32[1024,128]{1,0:T(8,128)S(1)}, f32[1024,256]{1,0:T(8,128)S(1)}, f32[512,256]{1,0:T(8,128)S(1)}) custom-call(bf16[128,24,128]{2,1,0:T(8,128)(2,1)S(1)} %all-to-all-done.payload_ref, f32[21,8]{1,0:T(8,128)S(1)} %bitcast.38, bf16[128,192]{1,0:T(8,128)(2,1)S(1)} %copy-done.10, bf16[64,384]{1,0:T(8,128)(2,1)S(1)} %copy-done.16, ...), custom_call_target="tpu_custom_call" | custom-call | tf_op jit(solution)/shard_map/pallas_call | solution.py:411
  72.5 1.0 copy-done.3
  73.5 1.1 fusion.9
  74.5 10.1 %all-to-all-start.1 = ((f16[128,8,128]{2,1,0:T(8,128)(2,1)}), f16[128,8,128]{2,1,0:T(8,128)(2,1)}, u32[]{:S(2)}, u32[]{:S(2)}) async-start(f16[128,8,128]{2,1,0:T(8,128)(2,1)} %fusion.9), calls=%async_computation.1 | async-start | bytes 524288 | tf_op jit(solution)/shard_map/all_to_all | solution.py:372
  84.7 5.0 %collective-permute-start = (bf16[8,1024]{1,0:T(8,128)(2,1)S(1)}, bf16[8,1024]{1,0:T(8,128)(2,1)S(1)}, u32[]{:S(2)}, u32[]{:S(2)}) collective-permute-start(bf16[8,1024]{1,0:T(8,128)(2,1)S(1)} %slice_bitcast_fusion.1), channel_id=1, source_target_pairs={{0,1},{1,2},{2,3},{3,4},{4,5},{5,6},{6,7},{7,8},{8,9},{9,10},{10,1... | collective-permute-start | bytes 49160 | tf_op jit(solution)/shard_map/ppermute | solution.py:382
  89.8 0.8 collective-permute-done.halo_ref
  91.2 14.1 %all-to-all-done.1 = f16[128,8,128]{2,1,0:T(8,128)(2,1)} async-done(((f16[128,8,128]{2,1,0:T(8,128)(2,1)}), f16[128,8,128]{2,1,0:T(8,128)(2,1)}, u32[]{:S(2)}, u32[]{:S(2)}) %all-to-all-start.1) | async-done | bytes 262176 | tf_op jit(solution)/shard_map/all_to_all | solution.py:372
  105.3 1.1 fusion.2.conv_ref
  106.5 8.0 %all_to_all.25.stats_ref = f32[4,2,128]{2,1,0:T(2,128)S(1)} all-to-all(f32[4,2,128]{2,1,0:T(2,128)S(1)} %shard_map.150), channel_id=1, replica_groups=mesh['dp'=2,'tensor'=4,'context'=64] {'tensor'}, dimensions={0} | all-to-all | bytes 8192 | tf_op jit(solution)/shard_map/all_to_all | solution.py:423
  115.2 1.1 fusion.8
  116.3 10.9 %all-to-all-start.3 = ((f16[128,8,128]{2,1,0:T(8,128)(2,1)}), f16[128,8,128]{2,1,0:T(8,128)(2,1)}, u32[]{:S(2)}, u32[]{:S(2)}) async-start(f16[128,8,128]{2,1,0:T(8,128)(2,1)} %fusion.8), calls=%async_computation.3 | async-start | bytes 524288 | tf_op jit(solution)/shard_map/all_to_all | solution.py:372
  127.1 0.7 copy-done.20
  129.2 1.4 shard_map.152
  130.6 0.8 copy-done.5
  131.4 3.7 %collective-permute-start.2 = (f32[7,1024]{1,0:T(8,128)S(1)}, f32[7,1024]{1,0:T(8,128)S(1)}, u32[]{:S(2)}, u32[]{:S(2)}) collective-permute-start(f32[7,1024]{1,0:T(8,128)S(1)} %get-tuple-element.26), channel_id=1, source_target_pairs={{0,256},{256,0},{1,257},{257,1},{2,258},{258,2},{3,259},{259,3},{4... | collective-permute-start | bytes 86024 | tf_op jit(solution)/shard_map/ppermute | solution.py:376
  135.1 2.5 %collective-permute-start.1 = (f32[8,1024]{1,0:T(8,128)S(1)}, f32[8,1024]{1,0:T(8,128)S(1)}, u32[]{:S(2)}, u32[]{:S(2)}) collective-permute-start(f32[8,1024]{1,0:T(8,128)S(1)} %get-tuple-element.25), channel_id=1, source_target_pairs={{1,0},{2,1},{3,2},{4,3},{5,4},{6,5},{7,6},{8,7},{9,8},{10,9},{11,1... | collective-permute-start | bytes 98312 | tf_op jit(solution)/shard_map/ppermute | solution.py:382
  137.7 2.5 %collective-permute-start.3 = (f32[7,1024]{1,0:T(8,128)S(1)}, f32[7,1024]{1,0:T(8,128)S(1)}, u32[]{:S(2)}, u32[]{:S(2)}) collective-permute-start(f32[7,1024]{1,0:T(8,128)S(1)} %add.32), channel_id=1, source_target_pairs={{0,1},{1,0},{2,3},{3,2},{4,5},{5,4},{6,7},{7,6},{8,9},{9,8},{10,11... | collective-permute-start | bytes 86024 | tf_op jit(solution)/shard_map/ppermute | solution.py:376
  140.3 0.8 collective-permute-done.3
  141.1 1.2 collective-permute-done.1.edge_ref
  142.3 4.0 %all-to-all-done.3 = f16[128,8,128]{2,1,0:T(8,128)(2,1)} async-done(((f16[128,8,128]{2,1,0:T(8,128)(2,1)}), f16[128,8,128]{2,1,0:T(8,128)(2,1)}, u32[]{:S(2)}, u32[]{:S(2)}) %all-to-all-start.3) | async-done | bytes 262176 | tf_op jit(solution)/shard_map/all_to_all | solution.py:372
  146.3 1.1 fusion.5.dconv_ref
  147.4 1.2 copy-done.4
  148.6 1.0 copy-done.9
  149.6 0.8 copy-done.12
  150.5 0.7 copy-done.18
  151.2 6.6 %shard_map.153 = bf16[128,24,128]{2,1,0:T(8,128)(2,1)} custom-call(f32[1024,128]{1,0:T(8,128)S(1)} %fusion.5.dconv_ref, bf16[128,24,128]{2,1,0:T(8,128)(2,1)S(1)} %all-to-all-done.payload_ref, f32[1024,256]{1,0:T(8,128)S(1)} %copy-done.4, f32[512,256]{1,0:T(8,128)S(1)} %copy-done.9, f32[21,8]{1,0:T(8,128)S(1)} %bitcast.39, bf16[128,192]{1,0:T(8,128)(2,1)S(1)} %copy-done.10, ...), custom_call_target="tpu_custom_call" | custom-call | tf_op jit(solution)/shard_map/pallas_call | solution.py:442
  157.7 11.9 %all-to-all-start.4 = ((bf16[128,24,128]{2,1,0:T(8,128)(2,1)}), bf16[128,24,128]{2,1,0:T(8,128)(2,1)S(1)}, u32[]{:S(2)}, u32[]{:S(2)}) async-start(bf16[128,24,128]{2,1,0:T(8,128)(2,1)} %shard_map.153), calls=%async_computation.4 | async-start | bytes 1572864 | tf_op jit(solution)/shard_map/all_to_all | solution.py:372
  169.6 4.8 %collective-permute-start.5 = (f32[7,1024]{1,0:T(8,128)S(1)}, f32[7,1024]{1,0:T(8,128)S(1)}, u32[]{:S(2)}, u32[]{:S(2)}) collective-permute-start(f32[7,1024]{1,0:T(8,128)S(1)} %add.33), channel_id=1, source_target_pairs={{0,2},{1,3},{2,0},{3,1},{4,6},{5,7},{6,4},{7,5},{8,10},{9,11},{10,... | collective-permute-start | bytes 86024 | tf_op jit(solution)/shard_map/ppermute | solution.py:376
  174.4 1.7 collective-permute-done.5
  176.1 3.5 %collective-permute-start.6 = (f32[7,1024]{1,0:T(8,128)S(1)}, f32[7,1024]{1,0:T(8,128)S(1)}, u32[]{:S(2)}, u32[]{:S(2)}) collective-permute-start(f32[7,1024]{1,0:T(8,128)S(1)} %add.34), channel_id=1, source_target_pairs={{0,4},{1,5},{2,6},{3,7},{4,0},{5,1},{6,2},{7,3},{8,12},{9,13},{10,... | collective-permute-start | bytes 86024 | tf_op jit(solution)/shard_map/ppermute | solution.py:376
  179.6 24.6 %collective-permute-done.6 = f32[7,1024]{1,0:T(8,128)S(1)} collective-permute-done((f32[7,1024]{1,0:T(8,128)S(1)}, f32[7,1024]{1,0:T(8,128)S(1)}, u32[]{:S(2)}, u32[]{:S(2)}) %collective-permute-start.6) | collective-permute-done | bytes 28704 | tf_op jit(solution)/shard_map/ppermute | solution.py:376
  204.2 2.8 %collective-permute-start.7 = (f32[7,1024]{1,0:T(8,128)S(1)}, f32[7,1024]{1,0:T(8,128)S(1)}, u32[]{:S(2)}, u32[]{:S(2)}) collective-permute-start(f32[7,1024]{1,0:T(8,128)S(1)} %add.35), channel_id=1, source_target_pairs={{0,8},{1,9},{2,10},{3,11},{4,12},{5,13},{6,14},{7,15},{8,0},{9,1},... | collective-permute-start | bytes 86024 | tf_op jit(solution)/shard_map/ppermute | solution.py:376
  207.0 3.0 %collective-permute-done.7 = f32[7,1024]{1,0:T(8,128)S(1)} collective-permute-done((f32[7,1024]{1,0:T(8,128)S(1)}, f32[7,1024]{1,0:T(8,128)S(1)}, u32[]{:S(2)}, u32[]{:S(2)}) %collective-permute-start.7) | collective-permute-done | bytes 28704 | tf_op jit(solution)/shard_map/ppermute | solution.py:376
  210.0 6.6 %collective-permute-start.8 = (f32[7,1024]{1,0:T(8,128)S(1)}, f32[7,1024]{1,0:T(8,128)S(1)}, u32[]{:S(2)}, u32[]{:S(2)}) collective-permute-start(f32[7,1024]{1,0:T(8,128)S(1)} %add.36), channel_id=1, source_target_pairs={{0,16},{1,17},{2,18},{3,19},{4,20},{5,21},{6,22},{7,23},{8,24},{9,... | collective-permute-start | bytes 86024 | tf_op jit(solution)/shard_map/ppermute | solution.py:376
  216.6 2.0 collective-permute-done.8
  218.6 12.7 %collective-permute-start.9 = (f32[7,1024]{1,0:T(8,128)S(1)}, f32[7,1024]{1,0:T(8,128)S(1)}, u32[]{:S(2)}, u32[]{:S(2)}) collective-permute-start(f32[7,1024]{1,0:T(8,128)S(1)} %add.37), channel_id=1, source_target_pairs={{0,32},{1,33},{2,34},{3,35},{4,36},{5,37},{6,38},{7,39},{8,40},{9,... | collective-permute-start | bytes 86024 | tf_op jit(solution)/shard_map/ppermute | solution.py:376
  231.9 4.2 %collective-permute-start.4 = (bf16[512,128]{1,0:T(8,128)(2,1)S(1)}, bf16[512,128]{1,0:T(8,128)(2,1)S(1)}, u32[]{:S(2)}, u32[]{:S(2)}) collective-permute-start(bf16[512,128]{1,0:T(8,128)(2,1)S(1)} %get-tuple-element.33.own_ref), channel_id=1, source_target_pairs={{0,256},{256,0},{1,257},{257,1},{2,258},{258,2},{3,259},{259,3},{4... | collective-permute-start | bytes 393224 | tf_op jit(solution)/shard_map/ppermute | solution.py:459
  237.2 0.7 copy.28
  237.9 1.1 shard_map.155
  238.9 1.1 shard_map.157
  (67 shorter events, 4.4 us)
Async XLA Ops:
  0.6 1.0 copy-start.7
  1.7 0.9 copy-start.14
  2.6 0.9 copy-start.15
  3.6 22.0 %copy-start.25 = (f32[3,7,1024]{2,1,0:T(8,128)S(1)}, f32[3,7,1024]{2,1,0:T(8,128)}, u32[]{:S(2)}) copy-start(f32[3,7,1024]{2,1,0:T(8,128)} %param.15) | copy-start | bytes 258052
  4.8 62.4 %copy-start = (bf16[768,256]{1,0:T(8,128)(2,1)S(1)}, bf16[768,256]{1,0:T(8,128)(2,1)}, u32[]{:S(2)}) copy-start(bf16[768,256]{1,0:T(8,128)(2,1)} %constant.46.clone.inner_ref) | copy-start | bytes 1179652
  4.8 62.4 %copy-start.1 = (bf16[768,256]{1,0:T(8,128)(2,1)S(1)}, bf16[768,256]{1,0:T(8,128)(2,1)}, u32[]{:S(2)}) copy-start(bf16[768,256]{1,0:T(8,128)(2,1)} %constant.47.clone.outer_ref) | copy-start | bytes 1179652
  4.8 62.4 %copy-start.10 = (bf16[128,192]{1,0:T(8,128)(2,1)S(1)}, bf16[128,192]{1,0:T(8,128)(2,1)}, u32[]{:S(2)}) copy-start(bf16[128,192]{1,0:T(8,128)(2,1)} %constant.43.clone.first_ref) | copy-start | bytes 147460
  4.8 62.5 %copy-start.11 = (f32[2,64,128]{2,1,0:T(8,128)S(1)}, f32[2,64,128]{2,1,0:T(8,128)}, u32[]{:S(2)}) copy-start(f32[2,64,128]{2,1,0:T(8,128)} %constant.45.clone.twiddle_ref) | copy-start | bytes 196612
  4.8 62.5 %copy-start.16 = (bf16[64,384]{1,0:T(8,128)(2,1)S(1)}, bf16[64,384]{1,0:T(8,128)(2,1)}, u32[]{:S(2)}) copy-start(bf16[64,384]{1,0:T(8,128)(2,1)} %constant.44.clone.last_ref) | copy-start | bytes 147460
  4.8 62.4 %all-to-all-start = ((bf16[128,24,128]{2,1,0:T(8,128)(2,1)}), bf16[128,24,128]{2,1,0:T(8,128)(2,1)S(1)}, u32[]{:S(2)}, u32[]{:S(2)}) async-start(bf16[128,24,128]{2,1,0:T(8,128)(2,1)} %shard_map.147), calls=%async_computation | async-start | bytes 1572864 | tf_op jit(solution)/shard_map/all_to_all | solution.py:372
  28.4 46.2 %copy-start.17 = (f32[21,1,8]{2,0,1:T(8,128)}, f32[21,1,8]{2,0,1:T(8,128)S(1)}, u32[]{:S(2)}) copy-start(f32[21,1,8]{2,0,1:T(8,128)S(1)} %copy.31) | copy-start | bytes 2020
  67.3 17.4 %copy-start.2 = (bf16[1,128,1024]{2,1,0:T(8,128)(2,1)S(1)}, bf16[1,128,1024]{2,1,0:T(8,128)(2,1)}, u32[]{:S(2)}) copy-start(bf16[1,128,1024]{2,1,0:T(8,128)(2,1)} %param.12) | copy-start | bytes 786436
  67.3 23.3 %copy-start.13 = (bf16[1,128,1024]{2,1,0:T(8,128)(2,1)S(1)}, bf16[1,128,1024]{2,1,0:T(8,128)(2,1)}, u32[]{:S(2)}) copy-start(bf16[1,128,1024]{2,1,0:T(8,128)(2,1)} %param.18) | copy-start | bytes 786436
  67.3 23.3 %copy-start.23 = (f32[1024]{0:T(1024)S(1)}, f32[1024]{0:T(1024)}, u32[]{:S(2)}) copy-start(f32[1024]{0:T(1024)} %param.17) | copy-start | bytes 12292
  72.4 1.0 copy-start.3
  73.5 17.2 %copy-start.8 = (f32[512,256]{1,0:T(8,128)}, f32[512,256]{1,0:T(8,128)S(1)}, u32[]{:S(2)}) copy-start(f32[512,256]{1,0:T(8,128)S(1)} %get-tuple-element.30.spec_filt_ref) | copy-start | bytes 1572868
  74.5 30.8 %all-to-all-start.1 = ((f16[128,8,128]{2,1,0:T(8,128)(2,1)}), f16[128,8,128]{2,1,0:T(8,128)(2,1)}, u32[]{:S(2)}, u32[]{:S(2)}) async-start(f16[128,8,128]{2,1,0:T(8,128)(2,1)} %fusion.9), calls=%async_computation.1 | async-start | bytes 524288 | tf_op jit(solution)/shard_map/all_to_all | solution.py:372
  84.7 5.9 %collective-permute-start = (bf16[8,1024]{1,0:T(8,128)(2,1)S(1)}, bf16[8,1024]{1,0:T(8,128)(2,1)S(1)}, u32[]{:S(2)}, u32[]{:S(2)}) collective-permute-start(bf16[8,1024]{1,0:T(8,128)(2,1)S(1)} %slice_bitcast_fusion.1), channel_id=1, source_target_pairs={{0,1},{1,2},{2,3},{3,4},{4,5},{5,6},{6,7},{7,8},{8,9},{9,10},{10,1... | collective-permute-start | bytes 49160 | tf_op jit(solution)/shard_map/ppermute | solution.py:382
  90.6 0.6 copy-start.19
  114.6 0.6 copy-start.21
  116.3 30.0 %all-to-all-start.3 = ((f16[128,8,128]{2,1,0:T(8,128)(2,1)}), f16[128,8,128]{2,1,0:T(8,128)(2,1)}, u32[]{:S(2)}, u32[]{:S(2)}) async-start(f16[128,8,128]{2,1,0:T(8,128)(2,1)} %fusion.8), calls=%async_computation.3 | async-start | bytes 524288 | tf_op jit(solution)/shard_map/all_to_all | solution.py:372
  127.1 0.7 copy-start.20
  127.8 0.7 copy-start.22
  128.5 0.7 copy-start.24
  130.6 0.8 copy-start.5
  131.4 6.3 %collective-permute-start.2 = (f32[7,1024]{1,0:T(8,128)S(1)}, f32[7,1024]{1,0:T(8,128)S(1)}, u32[]{:S(2)}, u32[]{:S(2)}) collective-permute-start(f32[7,1024]{1,0:T(8,128)S(1)} %get-tuple-element.26), channel_id=1, source_target_pairs={{0,256},{256,0},{1,257},{257,1},{2,258},{258,2},{3,259},{259,3},{4... | collective-permute-start | bytes 86024 | tf_op jit(solution)/shard_map/ppermute | solution.py:376
  135.1 7.2 %collective-permute-start.1 = (f32[8,1024]{1,0:T(8,128)S(1)}, f32[8,1024]{1,0:T(8,128)S(1)}, u32[]{:S(2)}, u32[]{:S(2)}) collective-permute-start(f32[8,1024]{1,0:T(8,128)S(1)} %get-tuple-element.25), channel_id=1, source_target_pairs={{1,0},{2,1},{3,2},{4,3},{5,4},{6,5},{7,6},{8,7},{9,8},{10,9},{11,1... | collective-permute-start | bytes 98312 | tf_op jit(solution)/shard_map/ppermute | solution.py:382
  137.7 3.4 %collective-permute-start.3 = (f32[7,1024]{1,0:T(8,128)S(1)}, f32[7,1024]{1,0:T(8,128)S(1)}, u32[]{:S(2)}, u32[]{:S(2)}) collective-permute-start(f32[7,1024]{1,0:T(8,128)S(1)} %add.32), channel_id=1, source_target_pairs={{0,1},{1,0},{2,3},{3,2},{4,5},{5,4},{6,7},{7,6},{8,9},{9,8},{10,11... | collective-permute-start | bytes 86024 | tf_op jit(solution)/shard_map/ppermute | solution.py:376
  147.4 1.2 copy-start.4
  148.6 1.0 copy-start.9
  149.6 0.8 copy-start.12
  150.5 0.7 copy-start.18
  157.7 73.6 %copy-start.6 = (f32[128,1024]{1,0:T(8,128)S(1)}, f32[128,1024]{1,0:T(8,128)}, u32[]{:S(2)}) copy-start(f32[128,1024]{1,0:T(8,128)} %copy-done.5) | copy-start | bytes 1572868
  157.7 74.0 %all-to-all-start.4 = ((bf16[128,24,128]{2,1,0:T(8,128)(2,1)}), bf16[128,24,128]{2,1,0:T(8,128)(2,1)S(1)}, u32[]{:S(2)}, u32[]{:S(2)}) async-start(bf16[128,24,128]{2,1,0:T(8,128)(2,1)} %shard_map.153), calls=%async_computation.4 | async-start | bytes 1572864 | tf_op jit(solution)/shard_map/all_to_all | solution.py:372
  169.6 6.5 %collective-permute-start.5 = (f32[7,1024]{1,0:T(8,128)S(1)}, f32[7,1024]{1,0:T(8,128)S(1)}, u32[]{:S(2)}, u32[]{:S(2)}) collective-permute-start(f32[7,1024]{1,0:T(8,128)S(1)} %add.33), channel_id=1, source_target_pairs={{0,2},{1,3},{2,0},{3,1},{4,6},{5,7},{6,4},{7,5},{8,10},{9,11},{10,... | collective-permute-start | bytes 86024 | tf_op jit(solution)/shard_map/ppermute | solution.py:376
  176.1 28.0 %collective-permute-start.6 = (f32[7,1024]{1,0:T(8,128)S(1)}, f32[7,1024]{1,0:T(8,128)S(1)}, u32[]{:S(2)}, u32[]{:S(2)}) collective-permute-start(f32[7,1024]{1,0:T(8,128)S(1)} %add.34), channel_id=1, source_target_pairs={{0,4},{1,5},{2,6},{3,7},{4,0},{5,1},{6,2},{7,3},{8,12},{9,13},{10,... | collective-permute-start | bytes 86024 | tf_op jit(solution)/shard_map/ppermute | solution.py:376
  204.2 5.9 %collective-permute-start.7 = (f32[7,1024]{1,0:T(8,128)S(1)}, f32[7,1024]{1,0:T(8,128)S(1)}, u32[]{:S(2)}, u32[]{:S(2)}) collective-permute-start(f32[7,1024]{1,0:T(8,128)S(1)} %add.35), channel_id=1, source_target_pairs={{0,8},{1,9},{2,10},{3,11},{4,12},{5,13},{6,14},{7,15},{8,0},{9,1},... | collective-permute-start | bytes 86024 | tf_op jit(solution)/shard_map/ppermute | solution.py:376
  210.0 8.6 %collective-permute-start.8 = (f32[7,1024]{1,0:T(8,128)S(1)}, f32[7,1024]{1,0:T(8,128)S(1)}, u32[]{:S(2)}, u32[]{:S(2)}) collective-permute-start(f32[7,1024]{1,0:T(8,128)S(1)} %add.36), channel_id=1, source_target_pairs={{0,16},{1,17},{2,18},{3,19},{4,20},{5,21},{6,22},{7,23},{8,24},{9,... | collective-permute-start | bytes 86024 | tf_op jit(solution)/shard_map/ppermute | solution.py:376
  218.6 17.5 %collective-permute-start.9 = (f32[7,1024]{1,0:T(8,128)S(1)}, f32[7,1024]{1,0:T(8,128)S(1)}, u32[]{:S(2)}, u32[]{:S(2)}) collective-permute-start(f32[7,1024]{1,0:T(8,128)S(1)} %add.37), channel_id=1, source_target_pairs={{0,32},{1,33},{2,34},{3,35},{4,36},{5,37},{6,38},{7,39},{8,40},{9,... | collective-permute-start | bytes 86024 | tf_op jit(solution)/shard_map/ppermute | solution.py:376
  231.9 7.0 %collective-permute-start.4 = (bf16[512,128]{1,0:T(8,128)(2,1)S(1)}, bf16[512,128]{1,0:T(8,128)(2,1)S(1)}, u32[]{:S(2)}, u32[]{:S(2)}) collective-permute-start(bf16[512,128]{1,0:T(8,128)(2,1)S(1)} %get-tuple-element.33.own_ref), channel_id=1, source_target_pairs={{0,256},{256,0},{1,257},{257,1},{2,258},{258,2},{3,259},{259,3},{4... | collective-permute-start | bytes 393224 | tf_op jit(solution)/shard_map/ppermute | solution.py:459

commit v4 on v3

--- a/solution.py
+++ b/solution.py
@@ -176,39 +176,65 @@
         grad_z_ref[lanes, :] = (grad_ref[:, lanes].astype(F32) * gain_ref[:, lanes]).T
 
 
-def conv_kernel(width, groups, payload_ref, taps_ref, first_ref, last_ref, twiddle_ref, inner_ref, outer_ref,
-                conv_ref, spec_kv_ref, spec_filt_ref, k_ref, v_ref, filt_ref):
+def unpack_inputs(payload_ref, width, groups, k_ref, v_ref, filt_ref):
     rows = payload_ref.shape[0] // groups
     span = rows * width
     for index, ref in enumerate((k_ref, v_ref)):
         ref[...] = payload_ref[:, index * width : (index + 1) * width, :].astype(F32).reshape(groups * span, LANES)
-    parts = payload_ref[:, 2 * width : 3 * width, :].astype(F32)
-    filt_ref[...] = (parts[:rows] + parts[rows:]).reshape(span, LANES)
+    if filt_ref is not None:
+        parts = payload_ref[:, 2 * width : 3 * width, :].astype(F32)
+        filt_ref[...] = (parts[:rows] + parts[rows:]).reshape(span, LANES)
+    return rows, span
+
+
+def short_pair(k_ref, v_ref, taps_ref, place, rows, width, channel):
+    k_short = filtered(lagged(strided(k_ref, place, rows, width)), taps_ref, 1, channel)
+    v_short = filtered(lagged(strided(v_ref, place, rows, width)), taps_ref, 2, channel)
+    return k_short, v_short
+
+
+def conv_kernel(width, groups, payload_ref, taps_ref, first_ref, last_ref, twiddle_ref, inner_ref, outer_ref,
+                conv_ref, k_ref, v_ref, filt_ref):
+    rows, span = unpack_inputs(payload_ref, width, groups, k_ref, v_ref, filt_ref)
     for start in range(0, width, 2):
         blocks = []
         for channel in (start, start + 1):
             for group in range(groups):
-                place = group * span + channel
-                k_short = filtered(lagged(strided(k_ref, place, rows, width)), taps_ref, 1, channel)
-                v_short = filtered(lagged(strided(v_ref, place, rows, width)), taps_ref, 2, channel)
+                k_short, v_short = short_pair(k_ref, v_ref, taps_ref, group * span + channel, rows, width, channel)
                 blocks.append(k_short * v_short)
         blocks += [strided(filt_ref, channel, rows, width) for channel in (start, start + 1)]
         spec = forward(blocks, first_ref, twiddle_ref, inner_ref)
         pairs = 2 * groups * rows
-        spec_kv, spec_filt = spec[:pairs], spec[pairs:]
-        spec_kv_ref[start * groups * rows : (start + 2) * groups * rows, :] = spec_kv
-        spec_filt_ref[start * rows : (start + 2) * rows, :] = spec_filt
         products = []
         for side in range(2):
             for group in range(groups):
                 block = (side * groups + group) * rows
-                products.append(
-                    times(spec_kv[block : block + rows], spec_filt[side * rows : (side + 1) * rows], False)
-                )
+                filt = pairs + side * rows
+                products.append(times(spec[block : block + rows], spec[filt : filt + rows], False))
         convs = inverse(jnp.concatenate(products, 0), rows, last_ref, twiddle_ref, outer_ref)
         for side in range(2):
             for group in range(groups):
                 conv_ref[pl.ds(group * span + start + side, rows, stride=width), :] = convs[side * groups + group]
+
+
+def spectra_kernel(width, groups, payload_ref, taps_ref, first_ref, twiddle_ref, inner_ref,
+                   out_ref, k_ref, v_ref, filt_ref):
+    rows, span = unpack_inputs(payload_ref, width, groups, k_ref, v_ref, filt_ref)
+    for start in range(0, width, 2):
+        blocks = []
+        for channel in (start, start + 1):
+            for group in range(groups):
+                k_short, v_short = short_pair(k_ref, v_ref, taps_ref, group * span + channel, rows, width, channel)
+                below = (channel * groups + group) * rows + groups * span
+                out_ref[below : below + rows, :LANES] = k_short
+                out_ref[below : below + rows, LANES:] = v_short
+                blocks.append(k_short * v_short)
+        blocks += [strided(filt_ref, channel, rows, width) for channel in (start, start + 1)]
+        spec = forward(blocks, first_ref, twiddle_ref, inner_ref)
+        pairs = 2 * groups * rows
+        out_ref[start * groups * rows : (start + 2) * groups * rows, :] = spec[:pairs]
+        below = 2 * groups * span + start * rows
+        out_ref[below : below + 2 * rows, :] = spec[pairs:]
 
 
 def stats_kernel(conv_ref, q_short_ref, grad_z_ref, stats_ref):
@@ -269,13 +295,10 @@
         out_ref[:, lanes] = total.astype(BF16)
 
 
-def back_kernel(width, groups, scale, dconv_ref, payload_ref, spec_kv_ref, spec_filt_ref, taps_ref, first_ref, last_ref,
+def back_kernel(width, groups, scale, dconv_ref, payload_ref, saved_ref, taps_ref, first_ref, last_ref,
                 twiddle_ref, inner_ref, outer_ref, out_ref, k_ref, v_ref, grad_k_ref, grad_v_ref, dfilt_ref, short_ref):
-    rows = payload_ref.shape[0] // groups
-    span = rows * width
+    rows, span = unpack_inputs(payload_ref, width, groups, k_ref, v_ref, None)
     part_width = width // groups
-    for index, ref in enumerate((k_ref, v_ref)):
-        ref[...] = payload_ref[:, index * width : (index + 1) * width, :].astype(F32).reshape(groups * span, LANES)
     short_ref[...] = jnp.zeros(short_ref.shape, F32)
     dfilt_ref[...] = jnp.zeros(dfilt_ref.shape, F32)
     for start in range(0, width, 2):
@@ -284,8 +307,9 @@
             for group in range(groups):
                 blocks.append(strided(dconv_ref, group * span + channel, rows, width))
         spec = forward(blocks, first_ref, twiddle_ref, inner_ref)
-        spec_filt = spec_filt_ref[start * rows : (start + 2) * rows, :]
-        spec_kv = spec_kv_ref[start * groups * rows : (start + 2) * groups * rows, :]
+        below = 2 * groups * span + start * rows
+        spec_filt = saved_ref[below : below + 2 * rows, :]
+        spec_kv = saved_ref[start * groups * rows : (start + 2) * groups * rows, :]
         products = []
         filters = []
         for side in range(2):
@@ -306,8 +330,9 @@
                 dkv = results[side * groups + group]
                 k_lags = lagged(strided(k_ref, place, rows, width))
                 v_lags = lagged(strided(v_ref, place, rows, width))
-                grad_k = dkv * filtered(v_lags, taps_ref, 2, channel)
-                grad_v = dkv * filtered(k_lags, taps_ref, 1, channel)
+                below = (channel * groups + group) * rows + groups * span
+                grad_k = dkv * saved_ref[below : below + rows, LANES:]
+                grad_v = dkv * saved_ref[below : below + rows, :LANES]
                 grad_k_ref[pl.ds(place, rows, stride=width), :] = filtered(led(grad_k), taps_ref, 1, channel)
                 grad_v_ref[pl.ds(place, rows, stride=width), :] = filtered(led(grad_v), taps_ref, 2, channel)
                 for branch, (grad, lags) in enumerate(((grad_k, k_lags), (grad_v, v_lags))):
@@ -399,7 +424,7 @@
 
     side = lax.axis_index("dp").astype(jnp.int32).reshape(1, 1)
     (payload,) = kernel_call(
-        functools.partial(pack_kernel, width), [bf16(peers, 3 * width, LANES)], smem=(0,), count=4
+        functools.partial(pack_kernel, width), [bf16(peers, 3 * width, LANES)], smem=(0,), count=4, mib=56
     )(side, k_in[0], v_in[0], long_filt)
     payload = exchange(payload)
 
@@ -408,11 +433,12 @@
         q_in[0], halo, grad_out[0], taps_q, gain
     )
 
-    conv, spec_kv, spec_filt = kernel_call(
+    inputs = [scratch, scratch, pltpu.VMEM((rows * width, LANES), F32)]
+    (conv,) = kernel_call(
         functools.partial(conv_kernel, width, groups),
-        [f32(size, LANES), f32(size, 2 * LANES), f32(rows * width, 2 * LANES)],
+        [f32(size, LANES)],
         smem=(1,),
-        scratch=[scratch, scratch, pltpu.VMEM((rows * width, LANES), F32)],
+        scratch=inputs,
         count=7,
         mib=10,
     )(payload, taps, first, last, twiddle, inner, outer)
@@ -430,24 +456,36 @@
         count=7,
     )(conv, q_short, grad_z, stats, q_in[0], halo, gain)
     edge = passed_along(edge, -1)
-    for bit in range(groups.bit_length() - 1):
-        short_q = paired_sum(short_q, "dp", 1 << bit)
-    short_q = paired_sum(short_q, "context", 1)
-    dconv, mixed, grad_0, edge, short_q = lax.optimization_barrier((dconv, mixed, grad_0, edge, short_q))
-    (grad_q,) = kernel_call(grad_q_kernel, [bf16(LANES, channels)], count=3)(grad_0, edge, taps_q)
-    for bit in range(1, rows.bit_length() - 1):
-        short_q = paired_sum(short_q, "context", 1 << bit)
-
+    (saved,) = kernel_call(
+        functools.partial(spectra_kernel, width, groups),
+        [f32(2 * size + rows * width, 2 * LANES)],
+        smem=(1,),
+        scratch=inputs,
+        count=5,
+        mib=10,
+    )(payload, taps, first, twiddle, inner)
+    bits = [1 << bit for bit in reversed(range(rows.bit_length() - 1))]
+    early = len(bits) // 2
+    for bit in bits[:early]:
+        short_q = paired_sum(short_q, "context", bit)
+    dconv, mixed, grad_0, edge, short_q, saved = lax.optimization_barrier(
+        (dconv, mixed, grad_0, edge, short_q, saved)
+    )
     dconv = decode(dconv, 4.6e8).reshape(size, LANES)
     (back,) = kernel_call(
         functools.partial(back_kernel, width, groups, scale),
         [bf16(peers, 3 * width, LANES)],
-        smem=(4,),
+        smem=(3,),
         scratch=[scratch] * 5 + [pltpu.VMEM((LANES, LANES), F32)],
-        count=10,
+        count=9,
         mib=10,
-    )(dconv, payload, spec_kv, spec_filt, taps, first, last, twiddle, inner, outer)
+    )(dconv, payload, saved, taps, first, last, twiddle, inner, outer)
     back = exchange(back)
+    for bit in bits[early:]:
+        short_q = paired_sum(short_q, "context", bit)
+    for bit in range(groups.bit_length() - 1):
+        short_q = paired_sum(short_q, "dp", 1 << bit)
+    (grad_q,) = kernel_call(grad_q_kernel, [bf16(LANES, channels)], count=3)(grad_0, edge, taps_q)
     part_width = width // groups
     part_scratch = pltpu.VMEM((peers * part_width, LANES), F32)
     part, short = kernel_call(

time: 244 us -> 244 us (level); the launches traced: 240 us -> 243 us
  waiting for transfers between devices: 91.1 us -> 104 us
  starting transfers between devices: 102 us -> 95.3 us
  local copies, waits for them, and re-layouts: 15.7 us -> 9.54 us
  Pallas kernels: 17.9 us -> 21.3 us
    ppermute x7, waiting for transfers between devices: 32.1 us -> 47.9 us  [paired_sum(): lax.ppermute(values, axis, [(i, i ^ bit) for i in range(lax.axis_size(axi...]
    unnamed x53 -> x43, local copies, waits for them, and re-layouts: 12 us -> 5.83 us
    ppermute x7, starting transfers between devices: 36.6 us -> 30.8 us  [paired_sum(): lax.ppermute(values, axis, [(i, i ^ bit) for i in range(lax.axis_size(axi...]
    all_to_all x4, waiting for transfers between devices: 56.9 us -> 53.3 us  [exchange(): lax.all_to_all(payload, PEERS, split_axis=0, concat_axis=0, tiled=True)]
    pallas_call x0 -> x1, Pallas kernels: none -> 3.27 us  [shards(): kernel_call(functools.partial(spectra_kernel, width, groups), [f32(2 * si...]
  transfers between devices with their start and end apart: 14 -> 14, of which waited for: 10 -> 10; matrix products, arithmetic and copies ran while one was open for 2% -> 2% of each run, Pallas kernels for 2% -> 3%
where the time goes in v4:
time: 244 us; the launch traced here: 243 us
  waiting for transfers between devices  104 us (43%)
  starting transfers between devices  95.3 us (39%)
  Pallas kernels  21.3 us (9%)
  local copies, waits for them, and re-layouts  9.54 us (4%)
  blocking collectives  7.96 us (3%)
  other arithmetic  4.08 us (2%)
    all_to_all x4, starting transfers between devices, exchange(): lax.all_to_all(payload, PEERS, split_axis=0, concat_axis=0, tiled=True)  55 us
    all_to_all x4, waiting for transfers between devices, exchange(): lax.all_to_all(payload, PEERS, split_axis=0, concat_axis=0, tiled=True)  53.3 us
    ppermute x7, waiting for transfers between devices, paired_sum(): lax.ppermute(values, axis, [(i, i ^ bit) for i in range(lax.axis_size(axi...  47.9 us
    ppermute x7, starting transfers between devices, paired_sum(): lax.ppermute(values, axis, [(i, i ^ bit) for i in range(lax.axis_size(axi...  30.8 us
    all_to_all x1, blocking collectives, shards(): lax.all_to_all(stats, 'tensor', split_axis=0, concat_axis=0, tiled=True)  7.96 us
    ppermute x2, starting transfers between devices, passed_along(): return lax.ppermute(values, 'context', pairs)  7.54 us
    unnamed x43, local copies, waits for them, and re-layouts  5.83 us
    pallas_call x1, Pallas kernels, shards(): kernel_call(functools.partial(back_kernel, width, groups, scale), [bf16(p...  5.51 us
  transfers between devices with their start and end apart: 14, of which 10 were waited for; matrix products, arithmetic and copies ran while one was open for 2% of the time, Pallas kernels for 3%

profile of v4, /device:TPU:1, one launch (start us, length us, event | category | flops | bytes accessed | tf_op | source)
XLA Modules:
  0.0 242.9 jit_solution(3265526724637258613)
XLA Ops:
  0.6 2.5 %shard_map.147 = bf16[128,24,128]{2,1,0:T(8,128)(2,1)} custom-call(s32[1,1]{1,0:T(1,128)} %bitcast.side_ref, bf16[128,1024]{1,0:T(8,128)(2,1)} %bitcast.42, bf16[128,1024]{1,0:T(8,128)(2,1)} %bitcast.43, f32[128,1024]{1,0:T(8,128)} %filt_ref.1), custom_call_target="tpu_custom_call" | custom-call | tf_op jit(solution)/shard_map/pallas_call | solution.py:426
  3.1 20.7 %all-to-all-start = ((bf16[128,24,128]{2,1,0:T(8,128)(2,1)}), bf16[128,24,128]{2,1,0:T(8,128)(2,1)S(1)}, u32[]{:S(2)}, u32[]{:S(2)}) async-start(bf16[128,24,128]{2,1,0:T(8,128)(2,1)} %shard_map.147), calls=%async_computation | async-start | bytes 1572864 | tf_op jit(solution)/shard_map/all_to_all | solution.py:397
  23.9 1.9 reshape.34
  25.8 0.9 constant_dynamic-slice_fusion
  26.7 38.9 %all-to-all-done.payload_ref = bf16[128,24,128]{2,1,0:T(8,128)(2,1)S(1)} async-done(((bf16[128,24,128]{2,1,0:T(8,128)(2,1)}), bf16[128,24,128]{2,1,0:T(8,128)(2,1)S(1)}, u32[]{:S(2)}, u32[]{:S(2)}) %all-to-all-start) | async-done | bytes 786464 | tf_op jit(solution)/shard_map/all_to_all | solution.py:397
  65.6 5.1 %shard_map.148 = f32[1024,128]{1,0:T(8,128)S(1)} custom-call(bf16[128,24,128]{2,1,0:T(8,128)(2,1)S(1)} %all-to-all-done.payload_ref, f32[21,8]{1,0:T(8,128)S(1)} %bitcast.36, bf16[128,192]{1,0:T(8,128)(2,1)S(1)} %copy-done.8, bf16[64,384]{1,0:T(8,128)(2,1)S(1)} %copy-done.14, f32[2,64,128]{2,1,0:T(8,128)S(1)} %copy-done.7, bf16[768,256]{1,0:T(8,128)(2,1)S(1)} %copy-done, ...), custom_call_target="tpu_custom_call" | custom-call | tf_op jit(solution)/shard_map/pallas_call | solution.py:437
  70.7 1.1 fusion.9
  71.8 9.7 %all-to-all-start.1 = ((f16[128,8,128]{2,1,0:T(8,128)(2,1)}), f16[128,8,128]{2,1,0:T(8,128)(2,1)S(1)}, u32[]{:S(2)}, u32[]{:S(2)}) async-start(f16[128,8,128]{2,1,0:T(8,128)(2,1)} %fusion.9), calls=%async_computation.1 | async-start | bytes 524288 | tf_op jit(solution)/shard_map/all_to_all | solution.py:397
  81.5 5.0 %collective-permute-start = (bf16[8,1024]{1,0:T(8,128)(2,1)S(1)}, bf16[8,1024]{1,0:T(8,128)(2,1)S(1)}, u32[]{:S(2)}, u32[]{:S(2)}) collective-permute-start(bf16[8,1024]{1,0:T(8,128)(2,1)S(1)} %slice_bitcast_fusion.1), channel_id=1, source_target_pairs={{0,1},{1,2},{2,3},{3,4},{4,5},{5,6},{6,7},{7,8},{8,9},{9,10},{10,1... | collective-permute-start | bytes 49160 | tf_op jit(solution)/shard_map/ppermute | solution.py:407
  86.6 0.8 collective-permute-done.halo_ref
  87.4 0.6 shard_map.149
  88.0 14.5 %all-to-all-done.1 = f16[128,8,128]{2,1,0:T(8,128)(2,1)S(1)} async-done(((f16[128,8,128]{2,1,0:T(8,128)(2,1)}), f16[128,8,128]{2,1,0:T(8,128)(2,1)S(1)}, u32[]{:S(2)}, u32[]{:S(2)}) %all-to-all-start.1) | async-done | bytes 262176 | tf_op jit(solution)/shard_map/all_to_all | solution.py:397
  102.7 8.0 %all_to_all.25.stats_ref = f32[4,2,128]{2,1,0:T(2,128)S(1)} all-to-all(f32[4,2,128]{2,1,0:T(2,128)S(1)} %shard_map.150), channel_id=1, replica_groups=mesh['dp'=2,'tensor'=4,'context'=64] {'tensor'}, dimensions={0} | all-to-all | bytes 8192 | tf_op jit(solution)/shard_map/all_to_all | solution.py:449
  110.8 1.1 fusion.8
  111.9 10.9 %all-to-all-start.3 = ((f16[128,8,128]{2,1,0:T(8,128)(2,1)}), f16[128,8,128]{2,1,0:T(8,128)(2,1)}, u32[]{:S(2)}, u32[]{:S(2)}) async-start(f16[128,8,128]{2,1,0:T(8,128)(2,1)} %fusion.8), calls=%async_computation.3 | async-start | bytes 524288 | tf_op jit(solution)/shard_map/all_to_all | solution.py:397
  122.8 1.4 shard_map.152
  124.1 0.8 copy-done.9
  124.9 12.2 %collective-permute-start.2 = (f32[7,1024]{1,0:T(8,128)S(1)}, f32[7,1024]{1,0:T(8,128)S(1)}, u32[]{:S(2)}, u32[]{:S(2)}) collective-permute-start(f32[7,1024]{1,0:T(8,128)S(1)} %get-tuple-element.23), channel_id=1, source_target_pairs={{0,32},{1,33},{2,34},{3,35},{4,36},{5,37},{6,38},{7,39},{8,40},{9,... | collective-permute-start | bytes 86024 | tf_op jit(solution)/shard_map/ppermute | solution.py:401
  137.1 9.1 %collective-permute-done.2 = f32[7,1024]{1,0:T(8,128)S(1)} collective-permute-done((f32[7,1024]{1,0:T(8,128)S(1)}, f32[7,1024]{1,0:T(8,128)S(1)}, u32[]{:S(2)}, u32[]{:S(2)}) %collective-permute-start.2) | collective-permute-done | bytes 28704 | tf_op jit(solution)/shard_map/ppermute | solution.py:401
  146.2 1.9 collective-permute-start.3
  148.2 2.5 %collective-permute-start.1 = (f32[8,1024]{1,0:T(8,128)S(1)}, f32[8,1024]{1,0:T(8,128)S(1)}, u32[]{:S(2)}, u32[]{:S(2)}) collective-permute-start(f32[8,1024]{1,0:T(8,128)S(1)} %get-tuple-element.22), channel_id=1, source_target_pairs={{1,0},{2,1},{3,2},{4,3},{5,4},{6,5},{7,6},{8,7},{9,8},{10,9},{11,1... | collective-permute-start | bytes 98312 | tf_op jit(solution)/shard_map/ppermute | solution.py:407
  150.7 4.1 %collective-permute-done.3 = f32[7,1024]{1,0:T(8,128)S(1)} collective-permute-done((f32[7,1024]{1,0:T(8,128)S(1)}, f32[7,1024]{1,0:T(8,128)S(1)}, u32[]{:S(2)}, u32[]{:S(2)}) %collective-permute-start.3) | collective-permute-done | bytes 28704 | tf_op jit(solution)/shard_map/ppermute | solution.py:401
  154.8 1.9 collective-permute-start.4
  156.7 3.3 %shard_map.153.saved_ref = f32[2560,256]{1,0:T(8,128)S(1)} custom-call(bf16[128,24,128]{2,1,0:T(8,128)(2,1)S(1)} %all-to-all-done.payload_ref, f32[21,8]{1,0:T(8,128)S(1)} %bitcast.37, bf16[128,192]{1,0:T(8,128)(2,1)S(1)} %copy-done.8, f32[2,64,128]{2,1,0:T(8,128)S(1)} %copy-done.7, bf16[768,256]{1,0:T(8,128)(2,1)S(1)} %copy-done.1), custom_call_target="tpu_custom_call" | custom-call | tf_op jit(solution)/shard_map/pallas_call | solution.py:459
  160.0 0.3 collective-permute-done.4
  160.4 0.6 add.34
  161.0 0.6 copy-done.16
  161.6 1.1 fusion.5.dconv_ref
  162.7 1.0 copy-done.2
  163.7 1.0 copy-done.5
  164.7 0.8 copy-done.15
  165.5 5.5 %shard_map.154 = bf16[128,24,128]{2,1,0:T(8,128)(2,1)S(1)} custom-call(f32[1024,128]{1,0:T(8,128)S(1)} %fusion.5.dconv_ref, bf16[128,24,128]{2,1,0:T(8,128)(2,1)S(1)} %all-to-all-done.payload_ref, f32[2560,256]{1,0:T(8,128)S(1)} %shard_map.153.saved_ref, f32[21,8]{1,0:T(8,128)S(1)} %bitcast.38, bf16[128,192]{1,0:T(8,128)(2,1)S(1)} %copy-done.8, ...), custom_call_target="tpu_custom_call" | custom-call | tf_op jit(solution)/shard_map/pallas_call | solution.py:475
  171.0 0.9 copy-done.3
  171.9 13.8 %all-to-all-start.4 = ((bf16[128,24,128]{2,1,0:T(8,128)(2,1)}), bf16[128,24,128]{2,1,0:T(8,128)(2,1)S(1)}, u32[]{:S(2)}, u32[]{:S(2)}) async-start(bf16[128,24,128]{2,1,0:T(8,128)(2,1)} %copy-done.3), calls=%async_computation.4 | async-start | bytes 1572864 | tf_op jit(solution)/shard_map/all_to_all | solution.py:397
  185.7 3.3 %collective-permute-start.6 = (f32[7,1024]{1,0:T(8,128)S(1)}, f32[7,1024]{1,0:T(8,128)S(1)}, u32[]{:S(2)}, u32[]{:S(2)}) collective-permute-start(f32[7,1024]{1,0:T(8,128)S(1)} %copy-done.20), channel_id=1, source_target_pairs={{0,4},{1,5},{2,6},{3,7},{4,0},{5,1},{6,2},{7,3},{8,12},{9,13},{10,... | collective-permute-start | bytes 86024 | tf_op jit(solution)/shard_map/ppermute | solution.py:401
  189.0 31.2 %collective-permute-done.6 = f32[7,1024]{1,0:T(8,128)S(1)} collective-permute-done((f32[7,1024]{1,0:T(8,128)S(1)}, f32[7,1024]{1,0:T(8,128)S(1)}, u32[]{:S(2)}, u32[]{:S(2)}) %collective-permute-start.6) | collective-permute-done | bytes 28704 | tf_op jit(solution)/shard_map/ppermute | solution.py:401
  220.2 4.2 %collective-permute-start.7 = (f32[7,1024]{1,0:T(8,128)S(1)}, f32[7,1024]{1,0:T(8,128)S(1)}, u32[]{:S(2)}, u32[]{:S(2)}) collective-permute-start(f32[7,1024]{1,0:T(8,128)S(1)} %add.35), channel_id=1, source_target_pairs={{0,2},{1,3},{2,0},{3,1},{4,6},{5,7},{6,4},{7,5},{8,10},{9,11},{10,... | collective-permute-start | bytes 86024 | tf_op jit(solution)/shard_map/ppermute | solution.py:401
  224.4 2.3 collective-permute-done.7
  226.7 3.8 %collective-permute-start.8 = (f32[7,1024]{1,0:T(8,128)S(1)}, f32[7,1024]{1,0:T(8,128)S(1)}, u32[]{:S(2)}, u32[]{:S(2)}) collective-permute-start(f32[7,1024]{1,0:T(8,128)S(1)} %add.36), channel_id=1, source_target_pairs={{0,1},{1,0},{2,3},{3,2},{4,5},{5,4},{6,7},{7,6},{8,9},{9,8},{10,11... | collective-permute-start | bytes 86024 | tf_op jit(solution)/shard_map/ppermute | solution.py:401
  230.5 0.8 collective-permute-done.8
  231.4 3.5 %collective-permute-start.9 = (f32[7,1024]{1,0:T(8,128)S(1)}, f32[7,1024]{1,0:T(8,128)S(1)}, u32[]{:S(2)}, u32[]{:S(2)}) collective-permute-start(f32[7,1024]{1,0:T(8,128)S(1)} %add.37), channel_id=1, source_target_pairs={{0,256},{256,0},{1,257},{257,1},{2,258},{258,2},{3,259},{259,3},{4... | collective-permute-start | bytes 86024 | tf_op jit(solution)/shard_map/ppermute | solution.py:401
  234.9 0.5 shard_map.155.grad_q_ref
  235.5 1.9 collective-permute-start.5
  237.9 0.5 reshape.40
  238.4 0.7 copy.29
  239.1 1.1 shard_map.156
  240.2 1.6 collective-permute-done.5.other_ref
  241.8 1.1 shard_map.158
  (58 shorter events, 1.1 us)
Async XLA Ops:
  0.6 23.2 %copy-start.19 = (f32[3,7,1024]{2,1,0:T(8,128)S(1)}, f32[3,7,1024]{2,1,0:T(8,128)}, u32[]{:S(2)}) copy-start(f32[3,7,1024]{2,1,0:T(8,128)} %param.15) | copy-start | bytes 258052
  3.1 62.4 %copy-start = (bf16[768,256]{1,0:T(8,128)(2,1)S(1)}, bf16[768,256]{1,0:T(8,128)(2,1)}, u32[]{:S(2)}) copy-start(bf16[768,256]{1,0:T(8,128)(2,1)} %constant.46.clone.inner_ref) | copy-start | bytes 1179652
  3.1 62.4 %copy-start.4 = (bf16[768,256]{1,0:T(8,128)(2,1)S(1)}, bf16[768,256]{1,0:T(8,128)(2,1)}, u32[]{:S(2)}) copy-start(bf16[768,256]{1,0:T(8,128)(2,1)} %constant.47.clone.outer_ref) | copy-start | bytes 1179652
  3.1 62.4 %copy-start.7 = (f32[2,64,128]{2,1,0:T(8,128)S(1)}, f32[2,64,128]{2,1,0:T(8,128)}, u32[]{:S(2)}) copy-start(f32[2,64,128]{2,1,0:T(8,128)} %constant.45.clone.twiddle_ref) | copy-start | bytes 196612
  3.1 62.5 %copy-start.8 = (bf16[128,192]{1,0:T(8,128)(2,1)S(1)}, bf16[128,192]{1,0:T(8,128)(2,1)}, u32[]{:S(2)}) copy-start(bf16[128,192]{1,0:T(8,128)(2,1)} %constant.43.clone.first_ref) | copy-start | bytes 147460
  3.1 62.5 %copy-start.14 = (bf16[64,384]{1,0:T(8,128)(2,1)S(1)}, bf16[64,384]{1,0:T(8,128)(2,1)}, u32[]{:S(2)}) copy-start(bf16[64,384]{1,0:T(8,128)(2,1)} %constant.44.clone.last_ref) | copy-start | bytes 147460
  3.1 62.4 %all-to-all-start = ((bf16[128,24,128]{2,1,0:T(8,128)(2,1)}), bf16[128,24,128]{2,1,0:T(8,128)(2,1)S(1)}, u32[]{:S(2)}, u32[]{:S(2)}) async-start(bf16[128,24,128]{2,1,0:T(8,128)(2,1)} %shard_map.147), calls=%async_computation | async-start | bytes 1572864 | tf_op jit(solution)/shard_map/all_to_all | solution.py:397
  65.6 15.9 %copy-start.6 = (bf16[1,128,1024]{2,1,0:T(8,128)(2,1)S(1)}, bf16[1,128,1024]{2,1,0:T(8,128)(2,1)}, u32[]{:S(2)}) copy-start(bf16[1,128,1024]{2,1,0:T(8,128)(2,1)} %param.12) | copy-start | bytes 786436
  65.6 21.8 %copy-start.13 = (bf16[1,128,1024]{2,1,0:T(8,128)(2,1)S(1)}, bf16[1,128,1024]{2,1,0:T(8,128)(2,1)}, u32[]{:S(2)}) copy-start(bf16[1,128,1024]{2,1,0:T(8,128)(2,1)} %param.18) | copy-start | bytes 786436
  65.6 21.8 %copy-start.18 = (f32[1024]{0:T(1024)S(1)}, f32[1024]{0:T(1024)}, u32[]{:S(2)}) copy-start(f32[1024]{0:T(1024)} %param.17) | copy-start | bytes 12292
  71.8 30.7 %all-to-all-start.1 = ((f16[128,8,128]{2,1,0:T(8,128)(2,1)}), f16[128,8,128]{2,1,0:T(8,128)(2,1)S(1)}, u32[]{:S(2)}, u32[]{:S(2)}) async-start(f16[128,8,128]{2,1,0:T(8,128)(2,1)} %fusion.9), calls=%async_computation.1 | async-start | bytes 524288 | tf_op jit(solution)/shard_map/all_to_all | solution.py:397
  81.5 5.9 %collective-permute-start = (bf16[8,1024]{1,0:T(8,128)(2,1)S(1)}, bf16[8,1024]{1,0:T(8,128)(2,1)S(1)}, u32[]{:S(2)}, u32[]{:S(2)}) collective-permute-start(bf16[8,1024]{1,0:T(8,128)(2,1)S(1)} %slice_bitcast_fusion.1), channel_id=1, source_target_pairs={{0,1},{1,2},{2,3},{3,4},{4,5},{5,6},{6,7},{7,8},{8,9},{9,10},{10,1... | collective-permute-start | bytes 49160 | tf_op jit(solution)/shard_map/ppermute | solution.py:407
  86.6 1.4 copy-start.11
  111.9 49.7 %all-to-all-start.3 = ((f16[128,8,128]{2,1,0:T(8,128)(2,1)}), f16[128,8,128]{2,1,0:T(8,128)(2,1)}, u32[]{:S(2)}, u32[]{:S(2)}) async-start(f16[128,8,128]{2,1,0:T(8,128)(2,1)} %fusion.8), calls=%async_computation.3 | async-start | bytes 524288 | tf_op jit(solution)/shard_map/all_to_all | solution.py:397
  122.7 34.0 %copy-start.1 = (bf16[768,256]{1,0:T(8,128)(2,1)S(1)}, bf16[768,256]{1,0:T(8,128)(2,1)}, u32[]{:S(2)}) copy-start(bf16[768,256]{1,0:T(8,128)(2,1)} %constant.46.clone.inner_ref) | copy-start | bytes 1179652
  124.1 0.8 copy-start.9
  124.9 21.3 %collective-permute-start.2 = (f32[7,1024]{1,0:T(8,128)S(1)}, f32[7,1024]{1,0:T(8,128)S(1)}, u32[]{:S(2)}, u32[]{:S(2)}) collective-permute-start(f32[7,1024]{1,0:T(8,128)S(1)} %get-tuple-element.23), channel_id=1, source_target_pairs={{0,32},{1,33},{2,34},{3,35},{4,36},{5,37},{6,38},{7,39},{8,40},{9,... | collective-permute-start | bytes 86024 | tf_op jit(solution)/shard_map/ppermute | solution.py:401
  146.2 8.6 %collective-permute-start.3 = (f32[7,1024]{1,0:T(8,128)S(1)}, f32[7,1024]{1,0:T(8,128)S(1)}, u32[]{:S(2)}, u32[]{:S(2)}) collective-permute-start(f32[7,1024]{1,0:T(8,128)S(1)} %add.32), channel_id=1, source_target_pairs={{0,16},{1,17},{2,18},{3,19},{4,20},{5,21},{6,22},{7,23},{8,24},{9,... | collective-permute-start | bytes 86024 | tf_op jit(solution)/shard_map/ppermute | solution.py:401
  148.2 12.8 %collective-permute-start.1 = (f32[8,1024]{1,0:T(8,128)S(1)}, f32[8,1024]{1,0:T(8,128)S(1)}, u32[]{:S(2)}, u32[]{:S(2)}) collective-permute-start(f32[8,1024]{1,0:T(8,128)S(1)} %get-tuple-element.22), channel_id=1, source_target_pairs={{1,0},{2,1},{3,2},{4,3},{5,4},{6,5},{7,6},{8,7},{9,8},{10,9},{11,1... | collective-permute-start | bytes 98312 | tf_op jit(solution)/shard_map/ppermute | solution.py:407
  154.8 5.5 %collective-permute-start.4 = (f32[7,1024]{1,0:T(8,128)S(1)}, f32[7,1024]{1,0:T(8,128)S(1)}, u32[]{:S(2)}, u32[]{:S(2)}) collective-permute-start(f32[7,1024]{1,0:T(8,128)S(1)} %add.33), channel_id=1, source_target_pairs={{0,8},{1,9},{2,10},{3,11},{4,12},{5,13},{6,14},{7,15},{8,0},{9,1},... | collective-permute-start | bytes 86024 | tf_op jit(solution)/shard_map/ppermute | solution.py:401
  161.0 0.6 copy-start.16
  162.7 1.0 copy-start.2
  163.7 1.0 copy-start.5
  164.7 0.8 copy-start.15
  171.0 0.9 copy-start.3
  171.9 13.8 %copy-start.20 = (f32[7,1024]{1,0:T(8,128)S(1)}, f32[7,1024]{1,0:T(8,128)}, u32[]{:S(2)}) copy-start(f32[7,1024]{1,0:T(8,128)} %add.34) | copy-start | bytes 86020
  171.9 63.0 %copy-start.10 = (f32[128,1024]{1,0:T(8,128)S(1)}, f32[128,1024]{1,0:T(8,128)}, u32[]{:S(2)}) copy-start(f32[128,1024]{1,0:T(8,128)} %copy-done.9) | copy-start | bytes 1572868
  171.9 63.0 %copy-start.12 = (f32[8,1024]{1,0:T(8,128)S(1)}, f32[8,1024]{1,0:T(8,128)}, u32[]{:S(2)}) copy-start(f32[8,1024]{1,0:T(8,128)} %copy-done.11) | copy-start | bytes 98308
  171.9 63.0 %copy-start.17 = (f32[8,1024]{1,0:T(8,128)S(1)}, f32[8,1024]{1,0:T(8,128)}, u32[]{:S(2)}) copy-start(f32[8,1024]{1,0:T(8,128)} %copy-done.16) | copy-start | bytes 98308
  171.9 63.5 %all-to-all-start.4 = ((bf16[128,24,128]{2,1,0:T(8,128)(2,1)}), bf16[128,24,128]{2,1,0:T(8,128)(2,1)S(1)}, u32[]{:S(2)}, u32[]{:S(2)}) async-start(bf16[128,24,128]{2,1,0:T(8,128)(2,1)} %copy-done.3), calls=%async_computation.4 | async-start | bytes 1572864 | tf_op jit(solution)/shard_map/all_to_all | solution.py:397
  185.7 34.5 %collective-permute-start.6 = (f32[7,1024]{1,0:T(8,128)S(1)}, f32[7,1024]{1,0:T(8,128)S(1)}, u32[]{:S(2)}, u32[]{:S(2)}) collective-permute-start(f32[7,1024]{1,0:T(8,128)S(1)} %copy-done.20), channel_id=1, source_target_pairs={{0,4},{1,5},{2,6},{3,7},{4,0},{5,1},{6,2},{7,3},{8,12},{9,13},{10,... | collective-permute-start | bytes 86024 | tf_op jit(solution)/shard_map/ppermute | solution.py:401
  220.2 6.5 %collective-permute-start.7 = (f32[7,1024]{1,0:T(8,128)S(1)}, f32[7,1024]{1,0:T(8,128)S(1)}, u32[]{:S(2)}, u32[]{:S(2)}) collective-permute-start(f32[7,1024]{1,0:T(8,128)S(1)} %add.35), channel_id=1, source_target_pairs={{0,2},{1,3},{2,0},{3,1},{4,6},{5,7},{6,4},{7,5},{8,10},{9,11},{10,... | collective-permute-start | bytes 86024 | tf_op jit(solution)/shard_map/ppermute | solution.py:401
  226.7 4.7 %collective-permute-start.8 = (f32[7,1024]{1,0:T(8,128)S(1)}, f32[7,1024]{1,0:T(8,128)S(1)}, u32[]{:S(2)}, u32[]{:S(2)}) collective-permute-start(f32[7,1024]{1,0:T(8,128)S(1)} %add.36), channel_id=1, source_target_pairs={{0,1},{1,0},{2,3},{3,2},{4,5},{5,4},{6,7},{7,6},{8,9},{9,8},{10,11... | collective-permute-start | bytes 86024 | tf_op jit(solution)/shard_map/ppermute | solution.py:401
  231.4 6.0 %collective-permute-start.9 = (f32[7,1024]{1,0:T(8,128)S(1)}, f32[7,1024]{1,0:T(8,128)S(1)}, u32[]{:S(2)}, u32[]{:S(2)}) collective-permute-start(f32[7,1024]{1,0:T(8,128)S(1)} %add.37), channel_id=1, source_target_pairs={{0,256},{256,0},{1,257},{257,1},{2,258},{258,2},{3,259},{259,3},{4... | collective-permute-start | bytes 86024 | tf_op jit(solution)/shard_map/ppermute | solution.py:401
  235.5 6.3 %collective-permute-start.5 = (bf16[512,128]{1,0:T(8,128)(2,1)S(1)}, bf16[512,128]{1,0:T(8,128)(2,1)S(1)}, u32[]{:S(2)}, u32[]{:S(2)}) collective-permute-start(bf16[512,128]{1,0:T(8,128)(2,1)S(1)} %get-tuple-element.29.own_ref), channel_id=1, source_target_pairs={{0,256},{256,0},{1,257},{257,1},{2,258},{258,2},{3,259},{259,3},{4... | collective-permute-start | bytes 393224 | tf_op jit(solution)/shard_map/ppermute | solution.py:497

commit v5 on v4

--- a/solution.py
+++ b/solution.py
@@ -258,31 +258,40 @@
     return rms, stats[1:2] / (D * rms * rms * rms)
 
 
-def dconv_kernel(conv_ref, q_short_ref, grad_z_ref, stats_ref, dconv_ref):
+TAPS = 2 * HALO
+
+
+def dconv_kernel(width, conv_ref, q_short_ref, grad_z_ref, stats_ref, q_ref, halo_ref,
+                 dconv_ref, sums_ref, grad_ref, edge_ref, rows_ref):
     rms, slope = scales(stats_ref)
     inverse_rms = 1.0 / rms
     for start in range(0, conv_ref.shape[0], LANES):
         lanes = slice(start, start + LANES)
         q_short = q_short_ref[lanes, :]
-        y_out = q_short * conv_ref[lanes, :]
-        dconv_ref[lanes, :] = (grad_z_ref[lanes, :] * inverse_rms - y_out * slope) * q_short
-
-
-def norm_kernel(conv_ref, q_short_ref, grad_z_ref, stats_ref, q_ref, halo_ref, gain_ref,
-                mixed_ref, grad_ref, edge_ref, short_ref):
-    rms, slope = scales(stats_ref)
-    inverse_rms = 1.0 / rms
-    for start in range(0, conv_ref.shape[0], LANES):
-        lanes = slice(start, start + LANES)
         conv = conv_ref[lanes, :]
-        y_out = q_short_ref[lanes, :] * conv
-        mixed_ref[:, lanes] = ((y_out / rms).T * gain_ref[:, lanes]).astype(BF16)
-        grad = ((grad_z_ref[lanes, :] * inverse_rms - y_out * slope) * conv).T
+        grad_y = grad_z_ref[lanes, :] * inverse_rms - q_short * conv * slope
+        dconv_ref[lanes, :] = grad_y * q_short
+        grad = (grad_y * conv).T
         grad_ref[:, lanes] = grad
         edge_ref[:, lanes] = grad[:HALO]
         extended = jnp.concatenate([halo_ref[:, lanes], q_ref[:, lanes]], 0).astype(F32)
-        for lag in range(FILT):
-            short_ref[lag : lag + 1, lanes] = jnp.sum(grad * shifted(extended, HALO - lag), 0, keepdims=True)
+        sums = [
+            jnp.sum(grad * shifted(extended, HALO - lag), 0, keepdims=True) for lag in range(FILT)
+        ]
+        rows_ref[lanes, :] = jnp.concatenate(sums + [jnp.zeros((LANES - FILT, LANES), F32)], 0).T
+    peers = conv_ref.shape[0] // width
+    total = strided(rows_ref, 0, peers, width)
+    for channel in range(1, width):
+        total = total + pltpu.roll(strided(rows_ref, channel, peers, width), channel * TAPS, 1)
+    sums_ref[...] = total
+
+
+def mixed_kernel(conv_ref, q_short_ref, stats_ref, gain_ref, mixed_ref):
+    rms, _ = scales(stats_ref)
+    for start in range(0, conv_ref.shape[0], LANES):
+        lanes = slice(start, start + LANES)
+        y_out = q_short_ref[lanes, :] * conv_ref[lanes, :]
+        mixed_ref[:, lanes] = ((y_out / rms).T * gain_ref[:, lanes]).astype(BF16)
 
 
 def grad_q_kernel(grad_ref, edge_ref, taps_ref, out_ref):
@@ -295,7 +304,7 @@
         out_ref[:, lanes] = total.astype(BF16)
 
 
-def back_kernel(width, groups, scale, dconv_ref, payload_ref, saved_ref, taps_ref, first_ref, last_ref,
+def back_kernel(width, groups, scale, dconv_ref, sums_ref, payload_ref, saved_ref, taps_ref, first_ref, last_ref,
                 twiddle_ref, inner_ref, outer_ref, out_ref, k_ref, v_ref, grad_k_ref, grad_v_ref, dfilt_ref, short_ref):
     rows, span = unpack_inputs(payload_ref, width, groups, k_ref, v_ref, None)
     part_width = width // groups
@@ -337,15 +346,18 @@
                 grad_v_ref[pl.ds(place, rows, stride=width), :] = filtered(led(grad_v), taps_ref, 2, channel)
                 for branch, (grad, lags) in enumerate(((grad_k, k_lags), (grad_v, v_lags))):
                     for lag in range(FILT):
-                        row = (branch * FILT + lag) * width + channel
+                        row = channel * TAPS + branch * FILT + lag
                         short_ref[row : row + 1, :] += jnp.sum(grad * lags[lag], axis=0, keepdims=True)
     peers = groups * rows
     out_ref[:, :width, :] = grad_k_ref[...].reshape(peers, width, LANES).astype(BF16)
     out_ref[:, width : 2 * width, :] = grad_v_ref[...].reshape(peers, width, LANES).astype(BF16)
-    short = jnp.sum(short_ref[...].T, axis=0, keepdims=True) * scale
-    high = short.astype(BF16).astype(F32)
-    for row, values in enumerate((high, short - high)):
-        dfilt_ref[pl.ds(part_width + row, peers, stride=width), :] = jnp.broadcast_to(values, (peers, LANES))
+    short = (jnp.sum(short_ref[...].T, axis=0, keepdims=True), jnp.sum(sums_ref[...], axis=0, keepdims=True))
+    for index, values in enumerate(short):
+        values = values * scale
+        high = values.astype(BF16).astype(F32)
+        for row, part in enumerate((high, values - high)):
+            start = part_width + 2 * index + row
+            dfilt_ref[pl.ds(start, peers, stride=width), :] = jnp.broadcast_to(part, (peers, LANES))
     out_ref[:, 2 * width :, :] = dfilt_ref[...].reshape(peers, width, LANES).astype(BF16)
 
 
@@ -355,7 +367,20 @@
     for row in range(part_width):
         out_ref[pl.ds(row, peers, stride=part_width), :] = strided(rows_ref, row, peers, width)
     part_ref[...] = out_ref[...].astype(BF16)
-    short_ref[...] = strided(rows_ref, part_width, peers, width) + strided(rows_ref, part_width + 1, peers, width)
+    short_kv, short_q = (
+        strided(rows_ref, start, peers, width) + strided(rows_ref, start + 1, peers, width)
+        for start in (part_width, part_width + 2)
+    )
+    lane = lax.broadcasted_iota(jnp.int32, short_q.shape, 1)
+    for channel in range(width):
+        back = LANES - channel * TAPS
+        rows_ref[pl.ds(channel, peers, stride=width), :] = jnp.where(
+            lane < FILT, pltpu.roll(short_q, back % LANES, 1), pltpu.roll(short_kv, (back + FILT) % LANES, 1)
+        )
+    for start in range(0, short_ref.shape[2], LANES):
+        block = rows_ref[start : start + LANES, :].T
+        for branch in range(3):
+            short_ref[branch, :, start : start + LANES] = block[branch * FILT : (branch + 1) * FILT]
 
 
 def unpack_kernel(width, payload_ref, grad_q_ref, grads_ref):
@@ -395,10 +420,6 @@
 
 def exchange(payload):
     return lax.all_to_all(payload, PEERS, split_axis=0, concat_axis=0, tiled=True)
-
-
-def paired_sum(values, axis, bit):
-    return values + lax.ppermute(values, axis, [(i, i ^ bit) for i in range(lax.axis_size(axis))])
 
 
 def passed_along(values, by):
@@ -447,15 +468,19 @@
     conv = decode(conv, 6.4e7).reshape(size, LANES)
     (stats,) = kernel_call(stats_kernel, [f32(lax.axis_size("tensor"), 2, LANES)], count=3)(conv, q_short, grad_z)
     stats = lax.all_to_all(stats, "tensor", split_axis=0, concat_axis=0, tiled=True)
-    (dconv,) = kernel_call(dconv_kernel, [f32(size, LANES)], count=4)(conv, q_short, grad_z, stats)
-    dconv = exchange(encode(dconv, 4.6e8).reshape(peers, width, LANES))
-
-    mixed, grad_0, edge, short_q = kernel_call(
-        norm_kernel,
-        [bf16(LANES, channels), f32(LANES, channels), f32(HALO, channels), f32(FILT, channels)],
-        count=7,
-    )(conv, q_short, grad_z, stats, q_in[0], halo, gain)
+    dconv, sums, grad_0, edge = kernel_call(
+        functools.partial(dconv_kernel, width),
+        [f32(size, LANES), f32(peers, LANES), f32(LANES, channels), f32(HALO, channels)],
+        scratch=[scratch],
+        count=6,
+    )(conv, q_short, grad_z, stats, q_in[0], halo)
+    code = encode(dconv, 4.6e8).reshape(peers, width // 2, 2, LANES)
+    sums = jnp.pad(encode(sums, 1e18).reshape(peers, 1, 1, LANES), ((0, 0), (0, 0), (0, 1), (0, 0)))
+    code = exchange(jnp.concatenate([code, sums], 1))
+
     edge = passed_along(edge, -1)
+    (mixed,) = kernel_call(mixed_kernel, [bf16(LANES, channels)], count=4)(conv, q_short, stats, gain)
+    (grad_q,) = kernel_call(grad_q_kernel, [bf16(LANES, channels)], count=3)(grad_0, edge, taps_q)
     (saved,) = kernel_call(
         functools.partial(spectra_kernel, width, groups),
         [f32(2 * size + rows * width, 2 * LANES)],
@@ -464,33 +489,24 @@
         count=5,
         mib=10,
     )(payload, taps, first, twiddle, inner)
-    bits = [1 << bit for bit in reversed(range(rows.bit_length() - 1))]
-    early = len(bits) // 2
-    for bit in bits[:early]:
-        short_q = paired_sum(short_q, "context", bit)
-    dconv, mixed, grad_0, edge, short_q, saved = lax.optimization_barrier(
-        (dconv, mixed, grad_0, edge, short_q, saved)
-    )
-    dconv = decode(dconv, 4.6e8).reshape(size, LANES)
+    code, mixed, grad_q, saved = lax.optimization_barrier((code, mixed, grad_q, saved))
+
+    dconv = decode(code[:, : width // 2], 4.6e8).reshape(size, LANES)
+    sums = decode(code[:, width // 2, 0], 1e18)
     (back,) = kernel_call(
         functools.partial(back_kernel, width, groups, scale),
         [bf16(peers, 3 * width, LANES)],
-        smem=(3,),
+        smem=(4,),
         scratch=[scratch] * 5 + [pltpu.VMEM((LANES, LANES), F32)],
-        count=9,
+        count=10,
         mib=10,
-    )(dconv, payload, saved, taps, first, last, twiddle, inner, outer)
+    )(dconv, sums, payload, saved, taps, first, last, twiddle, inner, outer)
     back = exchange(back)
-    for bit in bits[early:]:
-        short_q = paired_sum(short_q, "context", bit)
-    for bit in range(groups.bit_length() - 1):
-        short_q = paired_sum(short_q, "dp", 1 << bit)
-    (grad_q,) = kernel_call(grad_q_kernel, [bf16(LANES, channels)], count=3)(grad_0, edge, taps_q)
     part_width = width // groups
     part_scratch = pltpu.VMEM((peers * part_width, LANES), F32)
-    part, short = kernel_call(
+    part, grad_short = kernel_call(
         functools.partial(part_kernel, width, part_width),
-        [bf16(peers * part_width, LANES), f32(peers, LANES)],
+        [bf16(peers * part_width, LANES), f32(3, FILT, channels)],
         scratch=[scratch, part_scratch],
         count=1,
     )(back)
@@ -505,8 +521,6 @@
         scratch=[part_scratch, scratch],
         count=3,
     )(side, part, other)
-    short = short[:, : 2 * FILT * width].reshape(peers, 2, FILT, width).transpose(1, 2, 0, 3)
-    grad_short = jnp.concatenate([short_q[None] * scale, short.reshape(2, FILT, channels)])
     return (mixed[None], grads, grad_long, grad_short)
 
 

time: 244 us -> 219 us (0.90)
  blocking collectives: 7.96 us -> 59.6 us
  starting transfers between devices: 95.3 us -> 51.3 us
  waiting for transfers between devices: 104 us -> 71.8 us
  local copies, waits for them, and re-layouts: 9.54 us -> 4.68 us
    all_to_all x0 -> x1, blocking collectives: none -> 51.6 us  [exchange(): lax.all_to_all(payload, PEERS, split_axis=0, concat_axis=0, tiled=True)]
    ppermute x7 -> x0, waiting for transfers between devices: 47.9 us -> none  [paired_sum(): lax.ppermute(values, axis, [(i, i ^ bit) for i in range(lax.axis_size(axi...]
    ppermute x7 -> x0, starting transfers between devices: 30.8 us -> none  [paired_sum(): lax.ppermute(values, axis, [(i, i ^ bit) for i in range(lax.axis_size(axi...]
    all_to_all x4 -> x3, waiting for transfers between devices: 53.3 us -> 68.3 us  [exchange(): lax.all_to_all(payload, PEERS, split_axis=0, concat_axis=0, tiled=True)]
    all_to_all x4 -> x3, starting transfers between devices: 55 us -> 41.2 us  [exchange(): lax.all_to_all(payload, PEERS, split_axis=0, concat_axis=0, tiled=True)]
    unnamed x43 -> x49, local copies, waits for them, and re-layouts: 5.83 us -> 2.73 us
  transfers between devices with their start and end apart: 14 -> 6, of which waited for: 10 -> 5; matrix products, arithmetic and copies ran while one was open for 2% -> 0% of each run, Pallas kernels for 3% -> 3%
where the time goes in v5:
time: 219 us; the launch traced here: 216 us
  waiting for transfers between devices  71.8 us (33%)
  blocking collectives  59.6 us (27%)
  starting transfers between devices  51.3 us (23%)
  Pallas kernels  23.3 us (11%)
  local copies, waits for them, and re-layouts  4.68 us (2%)
  other arithmetic  4.26 us (2%)
    all_to_all x3, waiting for transfers between devices, exchange(): lax.all_to_all(payload, PEERS, split_axis=0, concat_axis=0, tiled=True)  68.3 us
    all_to_all x1, blocking collectives, exchange(): lax.all_to_all(payload, PEERS, split_axis=0, concat_axis=0, tiled=True)  51.6 us
    all_to_all x3, starting transfers between devices, exchange(): lax.all_to_all(payload, PEERS, split_axis=0, concat_axis=0, tiled=True)  41.2 us
    ppermute x2, starting transfers between devices, passed_along(): return lax.ppermute(values, 'context', pairs)  8.15 us
    all_to_all x1, blocking collectives, shards(): lax.all_to_all(stats, 'tensor', split_axis=0, concat_axis=0, tiled=True)  7.96 us
    pallas_call x1, Pallas kernels, shards(): kernel_call(functools.partial(back_kernel, width, groups, scale), [bf16(p...  5.49 us
    pallas_call x1, Pallas kernels, shards(): kernel_call(functools.partial(conv_kernel, width, groups), [f32(size, LAN...  5.11 us
  transfers between devices with their start and end apart: 6, of which 5 were waited for; matrix products, arithmetic and copies ran while one was open for 0% of the time, Pallas kernels for 3%

profile of v5, /device:TPU:1, one launch (start us, length us, event | category | flops | bytes accessed | tf_op | source)
XLA Modules:
  0.0 215.9 jit_solution(8460898622537476818)
XLA Ops:
  0.6 2.5 %shard_map.147 = bf16[128,24,128]{2,1,0:T(8,128)(2,1)} custom-call(s32[1,1]{1,0:T(1,128)} %bitcast.side_ref, bf16[128,1024]{1,0:T(8,128)(2,1)} %bitcast.43, bf16[128,1024]{1,0:T(8,128)(2,1)} %bitcast.44, f32[128,1024]{1,0:T(8,128)} %filt_ref.1), custom_call_target="tpu_custom_call" | custom-call | tf_op jit(solution)/shard_map/pallas_call | solution.py:447
  3.1 0.0 copy-start.19
  3.1 20.7 %all-to-all-start = ((bf16[128,24,128]{2,1,0:T(8,128)(2,1)}), bf16[128,24,128]{2,1,0:T(8,128)(2,1)S(1)}, u32[]{:S(2)}, u32[]{:S(2)}) async-start(bf16[128,24,128]{2,1,0:T(8,128)(2,1)} %shard_map.147), calls=%async_computation | async-start | bytes 1572864 | tf_op jit(solution)/shard_map/all_to_all | solution.py:422
  23.9 0.8 reshape.36
  24.7 40.9 %all-to-all-done.payload_ref = bf16[128,24,128]{2,1,0:T(8,128)(2,1)S(1)} async-done(((bf16[128,24,128]{2,1,0:T(8,128)(2,1)}), bf16[128,24,128]{2,1,0:T(8,128)(2,1)S(1)}, u32[]{:S(2)}, u32[]{:S(2)}) %all-to-all-start) | async-done | bytes 786464 | tf_op jit(solution)/shard_map/all_to_all | solution.py:422
  65.6 0.0 copy-start.9
  65.6 0.0 copy-start.18
  65.6 0.0 copy-start.21
  65.6 5.1 %shard_map.148 = f32[1024,128]{1,0:T(8,128)S(1)} custom-call(bf16[128,24,128]{2,1,0:T(8,128)(2,1)S(1)} %all-to-all-done.payload_ref, f32[21,8]{1,0:T(8,128)S(1)} %bitcast.36, bf16[128,192]{1,0:T(8,128)(2,1)S(1)} %copy-done.13, bf16[64,384]{1,0:T(8,128)(2,1)S(1)} %copy-done.19, f32[2,64,128]{2,1,0:T(8,128)S(1)} %copy-done.12, bf16[768,256]{1,0:T(8,128)(2,1)S(1)} %copy-done.4, ...), custom_call_target="tpu_custom_call" | custom-call | tf_op jit(solution)/shard_map/pallas_call | solution.py:458
  70.7 1.1 fusion.6
  71.8 9.7 %all-to-all-start.1 = ((f16[128,8,128]{2,1,0:T(8,128)(2,1)}), f16[128,8,128]{2,1,0:T(8,128)(2,1)S(1)}, u32[]{:S(2)}, u32[]{:S(2)}) async-start(f16[128,8,128]{2,1,0:T(8,128)(2,1)} %fusion.6), calls=%async_computation.1 | async-start | bytes 524288 | tf_op jit(solution)/shard_map/all_to_all | solution.py:422
  81.5 5.0 %collective-permute-start = (bf16[8,1024]{1,0:T(8,128)(2,1)S(1)}, bf16[8,1024]{1,0:T(8,128)(2,1)S(1)}, u32[]{:S(2)}, u32[]{:S(2)}) collective-permute-start(bf16[8,1024]{1,0:T(8,128)(2,1)S(1)} %slice_bitcast_fusion.1), channel_id=1, source_target_pairs={{0,1},{1,2},{2,3},{3,4},{4,5},{5,6},{6,7},{7,8},{8,9},{9,10},{10,1... | collective-permute-start | bytes 49160 | tf_op jit(solution)/shard_map/ppermute | solution.py:428
  86.6 0.8 collective-permute-done.halo_ref
  87.4 0.6 shard_map.149
  88.0 14.5 %all-to-all-done.1 = f16[128,8,128]{2,1,0:T(8,128)(2,1)S(1)} async-done(((f16[128,8,128]{2,1,0:T(8,128)(2,1)}), f16[128,8,128]{2,1,0:T(8,128)(2,1)S(1)}, u32[]{:S(2)}, u32[]{:S(2)}) %all-to-all-start.1) | async-done | bytes 262176 | tf_op jit(solution)/shard_map/all_to_all | solution.py:422
  102.5 0.1 fusion.2.conv_ref
  102.6 0.0 copy-start
  102.6 0.1 shard_map.150
  102.8 8.0 %all_to_all.25.stats_ref = f32[4,2,128]{2,1,0:T(2,128)S(1)} all-to-all(f32[4,2,128]{2,1,0:T(2,128)S(1)} %shard_map.150), channel_id=1, replica_groups=mesh['dp'=2,'tensor'=4,'context'=64] {'tensor'}, dimensions={0} | all-to-all | bytes 8192 | tf_op jit(solution)/shard_map/all_to_all | solution.py:470
  110.7 1.5 shard_map.151
  112.2 0.8 copy-done.14
  113.0 0.4 fusion.3
  113.4 0.1 fusion.11
  113.4 0.1 copy.32
  113.5 1.1 fusion.5
  114.6 10.8 %all-to-all-start.3 = ((f16[128,5,2,128]{3,2,1,0:T(2,128)(2,1)}), f16[128,5,2,128]{3,2,1,0:T(2,128)(2,1)}, u32[]{:S(2)}, u32[]{:S(2)}) async-start(f16[128,5,2,128]{3,2,1,0:T(2,128)(2,1)} %fusion.5), calls=%async_computation.3 | async-start | bytes 655360 | tf_op jit(solution)/shard_map/all_to_all | solution.py:422
  125.5 0.0 copy-start.1
  125.5 0.0 copy-start.3
  125.5 3.1 %collective-permute-start.1 = (f32[8,1024]{1,0:T(8,128)}, f32[8,1024]{1,0:T(8,128)S(1)}, u32[]{:S(2)}, u32[]{:S(2)}) collective-permute-start(f32[8,1024]{1,0:T(8,128)} %get-tuple-element.21), channel_id=1, source_target_pairs={{1,0},{2,1},{3,2},{4,3},{5,4},{6,5},{7,6},{8,7},{9,8},{10,9},{11,1... | collective-permute-start | bytes 98312 | tf_op jit(solution)/shard_map/ppermute | solution.py:428
  128.6 0.0 copy-start.5
  128.6 1.0 copy-done.5
  129.6 3.3 %shard_map.154.saved_ref = f32[2560,256]{1,0:T(8,128)S(1)} custom-call(bf16[128,24,128]{2,1,0:T(8,128)(2,1)S(1)} %all-to-all-done.payload_ref, f32[21,8]{1,0:T(8,128)S(1)} %bitcast.37, bf16[128,192]{1,0:T(8,128)(2,1)S(1)} %copy-done.13, f32[2,64,128]{2,1,0:T(8,128)S(1)} %copy-done.12, bf16[768,256]{1,0:T(8,128)(2,1)S(1)} %copy-done.5), custom_call_target="tpu_custom_call" | custom-call | tf_op jit(solution)/shard_map/pallas_call | solution.py:484
  132.9 0.9 shard_map.152
  133.9 0.1 copy-done.15
  134.0 0.5 shard_map.153.grad_q_ref
  134.4 0.0 copy-start.10
  134.4 0.7 copy-done.10
  135.1 13.0 %all-to-all-done.3 = f16[128,5,2,128]{3,2,1,0:T(2,128)(2,1)} async-done(((f16[128,5,2,128]{3,2,1,0:T(2,128)(2,1)}), f16[128,5,2,128]{3,2,1,0:T(2,128)(2,1)}, u32[]{:S(2)}, u32[]{:S(2)}) %all-to-all-start.3) | async-done | bytes 327712 | tf_op jit(solution)/shard_map/all_to_all | solution.py:422
  148.1 1.1 copy.29
  149.2 1.5 compare_select_fusion.1
  150.8 5.5 %shard_map.155 = bf16[128,24,128]{2,1,0:T(8,128)(2,1)S(1)} custom-call(f32[1024,128]{1,0:T(8,128)S(1)} %bitcast.32, f32[128,128]{1,0:T(8,128)S(1)} %fusion.8.sums_ref, bf16[128,24,128]{2,1,0:T(8,128)(2,1)S(1)} %all-to-all-done.payload_ref, f32[2560,256]{1,0:T(8,128)S(1)} %shard_map.154.saved_ref, f32[21,8]{1,0:T(8,128)S(1)} %bitcast.38, ...), custom_call_target="tpu_custom_call" | custom-call | tf_op jit(solution)/shard_map/pallas_call | solution.py:496
  156.3 0.0 copy-start.11
  156.3 51.6 %all_to_all.26.payload_ref = bf16[128,24,128]{2,1,0:T(8,128)(2,1)S(1)} all-to-all(bf16[128,24,128]{2,1,0:T(8,128)(2,1)S(1)} %shard_map.155), channel_id=1, replica_groups=mesh['dp'=2,'tensor'=4,'context'=64] {'dp','context'}, dimensions={0} | all-to-all | bytes 1572864 | tf_op jit(solution)/shard_map/all_to_all | solution.py:422
  207.9 1.2 shard_map.157
  209.1 1.9 collective-permute-start.2
  211.0 1.1 shard_map.156
  212.1 2.7 %collective-permute-done.2.other_ref = bf16[512,128]{1,0:T(8,128)(2,1)S(1)} collective-permute-done((bf16[512,128]{1,0:T(8,128)(2,1)S(1)}, bf16[512,128]{1,0:T(8,128)(2,1)S(1)}, u32[]{:S(2)}, u32[]{:S(2)}) %collective-permute-start.2) | collective-permute-done | bytes 131104 | tf_op jit(solution)/shard_map/ppermute | solution.py:513
  214.8 1.1 shard_map.158
  (41 shorter events, 0.1 us)
Async XLA Ops:
  0.6 23.2 %copy-start.23 = (f32[3,7,1024]{2,1,0:T(8,128)S(1)}, f32[3,7,1024]{2,1,0:T(8,128)}, u32[]{:S(2)}) copy-start(f32[3,7,1024]{2,1,0:T(8,128)} %param.15) | copy-start | bytes 258052
  3.1 62.4 %copy-start.4 = (bf16[768,256]{1,0:T(8,128)(2,1)S(1)}, bf16[768,256]{1,0:T(8,128)(2,1)}, u32[]{:S(2)}) copy-start(bf16[768,256]{1,0:T(8,128)(2,1)} %constant.52.clone.inner_ref) | copy-start | bytes 1179652
  3.1 62.5 %copy-start.7 = (bf16[768,256]{1,0:T(8,128)(2,1)S(1)}, bf16[768,256]{1,0:T(8,128)(2,1)}, u32[]{:S(2)}) copy-start(bf16[768,256]{1,0:T(8,128)(2,1)} %constant.53.clone.outer_ref) | copy-start | bytes 1179652
  3.1 62.5 %copy-start.12 = (f32[2,64,128]{2,1,0:T(8,128)S(1)}, f32[2,64,128]{2,1,0:T(8,128)}, u32[]{:S(2)}) copy-start(f32[2,64,128]{2,1,0:T(8,128)} %constant.51.clone.twiddle_ref) | copy-start | bytes 196612
  3.1 62.5 %copy-start.13 = (bf16[128,192]{1,0:T(8,128)(2,1)S(1)}, bf16[128,192]{1,0:T(8,128)(2,1)}, u32[]{:S(2)}) copy-start(bf16[128,192]{1,0:T(8,128)(2,1)} %constant.49.clone.first_ref) | copy-start | bytes 147460
  3.1 62.5 %copy-start.19 = (bf16[64,384]{1,0:T(8,128)(2,1)S(1)}, bf16[64,384]{1,0:T(8,128)(2,1)}, u32[]{:S(2)}) copy-start(bf16[64,384]{1,0:T(8,128)(2,1)} %constant.50.clone.last_ref) | copy-start | bytes 147460
  3.1 62.4 %all-to-all-start = ((bf16[128,24,128]{2,1,0:T(8,128)(2,1)}), bf16[128,24,128]{2,1,0:T(8,128)(2,1)S(1)}, u32[]{:S(2)}, u32[]{:S(2)}) async-start(bf16[128,24,128]{2,1,0:T(8,128)(2,1)} %shard_map.147), calls=%async_computation | async-start | bytes 1572864 | tf_op jit(solution)/shard_map/all_to_all | solution.py:422
  65.6 15.9 %copy-start.9 = (bf16[1,128,1024]{2,1,0:T(8,128)(2,1)S(1)}, bf16[1,128,1024]{2,1,0:T(8,128)(2,1)}, u32[]{:S(2)}) copy-start(bf16[1,128,1024]{2,1,0:T(8,128)(2,1)} %param.12) | copy-start | bytes 786436
  65.6 21.8 %copy-start.18 = (bf16[1,128,1024]{2,1,0:T(8,128)(2,1)S(1)}, bf16[1,128,1024]{2,1,0:T(8,128)(2,1)}, u32[]{:S(2)}) copy-start(bf16[1,128,1024]{2,1,0:T(8,128)(2,1)} %param.18) | copy-start | bytes 786436
  65.6 21.8 %copy-start.21 = (f32[1024]{0:T(1024)S(1)}, f32[1024]{0:T(1024)}, u32[]{:S(2)}) copy-start(f32[1024]{0:T(1024)} %param.17) | copy-start | bytes 12292
  71.8 30.7 %all-to-all-start.1 = ((f16[128,8,128]{2,1,0:T(8,128)(2,1)}), f16[128,8,128]{2,1,0:T(8,128)(2,1)S(1)}, u32[]{:S(2)}, u32[]{:S(2)}) async-start(f16[128,8,128]{2,1,0:T(8,128)(2,1)} %fusion.6), calls=%async_computation.1 | async-start | bytes 524288 | tf_op jit(solution)/shard_map/all_to_all | solution.py:422
  81.5 5.9 %collective-permute-start = (bf16[8,1024]{1,0:T(8,128)(2,1)S(1)}, bf16[8,1024]{1,0:T(8,128)(2,1)S(1)}, u32[]{:S(2)}, u32[]{:S(2)}) collective-permute-start(bf16[8,1024]{1,0:T(8,128)(2,1)S(1)} %slice_bitcast_fusion.1), channel_id=1, source_target_pairs={{0,1},{1,2},{2,3},{3,4},{4,5},{5,6},{6,7},{7,8},{8,9},{9,10},{10,1... | collective-permute-start | bytes 49160 | tf_op jit(solution)/shard_map/ppermute | solution.py:428
  86.6 16.2 %copy-start.16 = (f32[8,1024]{1,0:T(8,128)}, f32[8,1024]{1,0:T(8,128)S(1)}, u32[]{:S(2)}) copy-start(f32[8,1024]{1,0:T(8,128)S(1)} %pad.8.taps_ref) | copy-start | bytes 98308
  88.0 24.2 %copy-start.2 = (f32[1024,128]{1,0:T(8,128)}, f32[1024,128]{1,0:T(8,128)S(1)}, u32[]{:S(2)}) copy-start(f32[1024,128]{1,0:T(8,128)S(1)} %get-tuple-element.16.q_short_ref) | copy-start | bytes 1572868
  102.6 9.6 %copy-start = (f32[1024,128]{1,0:T(8,128)}, f32[1024,128]{1,0:T(8,128)S(1)}, u32[]{:S(2)}) copy-start(f32[1024,128]{1,0:T(8,128)S(1)} %fusion.2.conv_ref) | copy-start | bytes 1572868
  112.2 0.8 copy-start.14
  114.6 33.4 %all-to-all-start.3 = ((f16[128,5,2,128]{3,2,1,0:T(2,128)(2,1)}), f16[128,5,2,128]{3,2,1,0:T(2,128)(2,1)}, u32[]{:S(2)}, u32[]{:S(2)}) async-start(f16[128,5,2,128]{3,2,1,0:T(2,128)(2,1)} %fusion.5), calls=%async_computation.3 | async-start | bytes 655360 | tf_op jit(solution)/shard_map/all_to_all | solution.py:422
  125.5 7.4 %copy-start.1 = (f32[1024,128]{1,0:T(8,128)S(1)}, f32[1024,128]{1,0:T(8,128)}, u32[]{:S(2)}) copy-start(f32[1024,128]{1,0:T(8,128)} %copy-done) | copy-start | bytes 1572868
  125.5 7.4 %copy-start.3 = (f32[1024,128]{1,0:T(8,128)S(1)}, f32[1024,128]{1,0:T(8,128)}, u32[]{:S(2)}) copy-start(f32[1024,128]{1,0:T(8,128)} %copy-done.2) | copy-start | bytes 1572868
  125.5 8.4 %collective-permute-start.1 = (f32[8,1024]{1,0:T(8,128)}, f32[8,1024]{1,0:T(8,128)S(1)}, u32[]{:S(2)}, u32[]{:S(2)}) collective-permute-start(f32[8,1024]{1,0:T(8,128)} %get-tuple-element.21), channel_id=1, source_target_pairs={{1,0},{2,1},{3,2},{4,3},{5,4},{6,5},{7,6},{8,7},{9,8},{10,9},{11,1... | collective-permute-start | bytes 98312 | tf_op jit(solution)/shard_map/ppermute | solution.py:428
  128.6 1.0 copy-start.5
  129.6 3.3 %copy-start.22 = (f32[1024]{0:T(1024)S(1)}, f32[1024]{0:T(1024)}, u32[]{:S(2)}) copy-start(f32[1024]{0:T(1024)} %param.17) | copy-start | bytes 12292
  129.6 4.3 %copy-start.17 = (f32[8,1024]{1,0:T(8,128)S(1)}, f32[8,1024]{1,0:T(8,128)}, u32[]{:S(2)}) copy-start(f32[8,1024]{1,0:T(8,128)} %copy-done.16) | copy-start | bytes 98308
  132.9 1.0 copy-start.15
  134.4 0.7 copy-start.10
  148.1 2.7 %copy-start.6 = (bf16[768,256]{1,0:T(8,128)(2,1)S(1)}, bf16[768,256]{1,0:T(8,128)(2,1)}, u32[]{:S(2)}) copy-start(bf16[768,256]{1,0:T(8,128)(2,1)} %constant.52.clone.inner_ref) | copy-start | bytes 1179652
  148.1 2.7 %copy-start.8 = (bf16[768,256]{1,0:T(8,128)(2,1)S(1)}, bf16[768,256]{1,0:T(8,128)(2,1)}, u32[]{:S(2)}) copy-start(bf16[768,256]{1,0:T(8,128)(2,1)} %constant.53.clone.outer_ref) | copy-start | bytes 1179652
  148.1 2.7 %copy-start.20 = (bf16[64,384]{1,0:T(8,128)(2,1)S(1)}, bf16[64,384]{1,0:T(8,128)(2,1)}, u32[]{:S(2)}) copy-start(bf16[64,384]{1,0:T(8,128)(2,1)} %constant.50.clone.last_ref) | copy-start | bytes 147460
  156.3 54.7 %copy-start.11 = (bf16[128,1024]{1,0:T(8,128)(2,1)S(1)}, bf16[128,1024]{1,0:T(8,128)(2,1)}, u32[]{:S(2)}) copy-start(bf16[128,1024]{1,0:T(8,128)(2,1)} %copy-done.10) | copy-start | bytes 786436
  209.1 5.7 %collective-permute-start.2 = (bf16[512,128]{1,0:T(8,128)(2,1)S(1)}, bf16[512,128]{1,0:T(8,128)(2,1)S(1)}, u32[]{:S(2)}, u32[]{:S(2)}) collective-permute-start(bf16[512,128]{1,0:T(8,128)(2,1)S(1)} %get-tuple-element.26.own_ref), channel_id=1, source_target_pairs={{0,256},{256,0},{1,257},{257,1},{2,258},{258,2},{3,259},{259,3},{4... | collective-permute-start | bytes 393224 | tf_op jit(solution)/shard_map/ppermute | solution.py:513

commit v6 on v5

v6 whole, which is shorter than its diff:
```python
import functools
import math

import jax
import jax.numpy as jnp
import numpy as np
from jax import lax
from jax.experimental import pallas as pl
from jax.experimental.pallas import tpu as pltpu
from jax.sharding import PartitionSpec as P

D = 4096
FILT = 7
EPS = 1e-06
LANES = 128
F32 = jnp.float32
BF16 = jnp.bfloat16
VMEM = pl.BlockSpec(memory_space=pltpu.VMEM)
SMEM = pl.BlockSpec(memory_space=pltpu.SMEM)


def halves(table):
    high = table.astype(jnp.bfloat16)
    low = (table - high.astype(np.float64)).astype(jnp.bfloat16)
    return high, low


@functools.cache
def tables(rows):
    size = rows * LANES
    row = np.arange(rows)
    lane = np.arange(LANES)
    angle = 2 * np.pi * np.outer(row + 0.25, row) / rows
    high, low = halves(np.concatenate([np.cos(angle), -np.sin(angle)], 0))
    first = np.concatenate([high, high, low], 1)
    high, low = halves(np.concatenate([np.cos(angle).T, np.sin(angle).T], 1) / size)
    last = np.concatenate([high, high, low], 1)
    turn = 2 * np.pi * np.outer(row + 0.25, lane) / size
    twiddle = np.concatenate([np.cos(turn), -np.sin(turn)], 1)
    twiddles = []
    for _ in range(3):
        twiddles.append(twiddle.astype(jnp.bfloat16))
        twiddle = twiddle - twiddles[-1].astype(np.float64)
    grid = 2 * np.pi * (np.outer(lane, lane) % LANES) / LANES
    cosine, sine = np.cos(grid), -np.sin(grid)
    inner = np.concatenate(halves(np.block([[cosine, sine], [-sine, cosine]])), 0)
    wide = lambda part: np.pad(part, ((0, 0), (0, 2 * LANES - part.shape[1])))
    return np.concatenate([inner, wide(first), wide(last[:, : 2 * LANES]), wide(last[:, 2 * LANES :])] + twiddles, 0)


class Tables:
    def __init__(self, ref, rows):
        self.ref, self.rows = ref, rows
        start = 4 * LANES + 4 * rows
        parts = [ref[start + index * rows : start + (index + 1) * rows, :].astype(F32) for index in range(3)]
        twiddle = parts[0] + parts[1] + parts[2]
        self.real, self.imag = twiddle[:, :LANES], twiddle[:, LANES:]

    def inner(self):
        high, low = self.ref[: 2 * LANES, :], self.ref[2 * LANES : 4 * LANES, :]
        return jnp.concatenate([high, high, low], 0)

    def first(self):
        return self.ref[4 * LANES : 4 * LANES + 2 * self.rows, : 3 * self.rows]

    def last(self):
        start, wide = 4 * LANES + 2 * self.rows, 6 * self.rows
        left = self.ref[start : start + self.rows, : min(wide, 2 * LANES)]
        if wide <= 2 * LANES:
            return left
        return jnp.concatenate([left, self.ref[start + self.rows : start + 2 * self.rows, : wide - 2 * LANES]], 1)

    def turned(self, real, imag):
        return real * self.real - imag * self.imag, real * self.imag + imag * self.real


def split(values):
    high = values.astype(BF16)
    return high, (values - high.astype(F32)).astype(BF16)


def dot(left, right):
    return jnp.dot(left, right, preferred_element_type=F32)


def along_lanes(values, table):
    high, low = split(values)
    return dot(jnp.concatenate([high, low, high], 1), table.inner())


def forward(blocks, table):
    rows = blocks[0].shape[0]
    parts = []
    for pair in range(0, len(blocks), 2):
        high, low = split(jnp.concatenate(blocks[pair : pair + 2], 1))
        mixed = dot(table.first(), jnp.concatenate([high, low, high], 0))
        for side in range(2):
            lanes = slice(side * LANES, (side + 1) * LANES)
            parts.append(jnp.concatenate(table.turned(mixed[:rows, lanes], mixed[rows:, lanes]), 1))
    return along_lanes(jnp.concatenate(parts, 0), table)


def inverse(conjugates, rows, table):
    values = along_lanes(conjugates, table)
    count = conjugates.shape[0] // rows
    blocks = []
    for pair in range(0, count, 2):
        sides = []
        for block in (pair, pair + 1):
            part = values[block * rows : (block + 1) * rows]
            sides.append(jnp.concatenate(table.turned(part[:, :LANES], part[:, LANES:]), 0))
        high, low = split(jnp.concatenate(sides, 1))
        out = dot(table.last(), jnp.concatenate([high, low, high], 0))
        blocks += [out[:, :LANES], out[:, LANES:]]
    return blocks


def times(left, right, conjugate):
    re_l, im_l = left[:, :LANES], left[:, LANES:]
    re_r, im_r = right[:, :LANES], right[:, LANES:]
    if conjugate:
        return jnp.concatenate([re_l * re_r + im_l * im_r, im_l * re_r - re_l * im_r], 1)
    return jnp.concatenate([re_l * re_r - im_l * im_r, -(re_l * im_r + im_l * re_r)], 1)


def lagged(values):
    above, block = values[:-1], values[1:]
    lane = lax.broadcasted_iota(jnp.int32, block.shape, 2)
    return [block] + [
        pltpu.roll(jnp.where(lane >= LANES - lag, above, block), lag, 2) for lag in range(1, FILT)
    ]


def led(values):
    block, below = values[:-1], values[1:]
    lane = lax.broadcasted_iota(jnp.int32, block.shape, 2)
    return [block] + [
        pltpu.roll(jnp.where(lane < lag, below, block), LANES - lag, 2) for lag in range(1, FILT)
    ]


def filtered(shifted, taps_ref, branch):
    total = shifted[0] * taps_ref[branch * FILT][None]
    for lag in range(1, FILT):
        total = total + shifted[lag] * taps_ref[branch * FILT + lag][None]
    return total


def strided(ref, start, count, step):
    return ref[pl.ds(start, count, stride=step), :]


def kernel_call(kernel, shapes, smem=(), scratch=(), count=0, mib=6):
    return pl.pallas_call(
        kernel,
        out_shape=shapes,
        in_specs=[SMEM if index in smem else VMEM for index in range(count)],
        out_specs=[VMEM] * len(shapes),
        scratch_shapes=list(scratch),
        compiler_params=pltpu.CompilerParams(vmem_limit_bytes=mib * 2**20),
    )


def f32(*dims):
    return jax.ShapeDtypeStruct(dims, F32)


def bf16(*dims):
    return jax.ShapeDtypeStruct(dims, BF16)


def pack_kernel(width, side_ref, k_ref, v_ref, filt_ref, out_ref):
    low_side = side_ref[0, 0] == 1
    for start in range(0, k_ref.shape[1], LANES):
        into = slice(start // width, (start + LANES) // width)
        for index, ref in enumerate((k_ref, v_ref, filt_ref)):
            block = ref[:, start : start + LANES].astype(F32).T
            if ref is filt_ref:
                block = block - jnp.where(low_side, block.astype(BF16).astype(F32), 0.0)
            out_ref[into, index * width : (index + 1) * width, :] = (
                block.astype(BF16).reshape(LANES // width, width, LANES)
            )


def shifted(values, lag):
    return values[lag : lag + LANES]


HALO = 8


def prepare_kernel(q_ref, halo_ref, grad_ref, taps_ref, gain_ref, q_short_ref, grad_z_ref):
    for start in range(0, q_ref.shape[1], LANES):
        lanes = slice(start, start + LANES)
        extended = jnp.concatenate([halo_ref[:, lanes], q_ref[:, lanes]], 0).astype(F32)
        total = jnp.zeros((LANES, LANES), F32)
        for lag in range(FILT):
            total = total + shifted(extended, HALO - lag) * taps_ref[lag : lag + 1, lanes]
        q_short_ref[lanes, :] = total.T
        grad_z_ref[lanes, :] = (grad_ref[:, lanes].astype(F32) * gain_ref[:, lanes]).T


STEP = 4
CHUNK = 8


def chunks(peers, groups):
    rows = peers // groups
    size = min(CHUNK, rows)
    for start in range(0, peers, size):
        yield start, size, start % rows == 0, (start + size) % rows == 0


def loaded(payload_ref, index, width, start, size, at_first):
    rows = slice(index * width, (index + 1) * width)
    if at_first:
        block = payload_ref[start : start + size, rows, :].astype(F32)
        return jnp.concatenate([jnp.zeros((1, width, LANES), F32), block], 0)
    return payload_ref[start - 1 : start + size, rows, :].astype(F32)


def make_inputs(payload_ref, taps_ref, width, groups, kv_ref, filt_ref):
    peers = payload_ref.shape[0]
    rows = peers // groups
    span = rows * width
    for start, size, at_first, _ in chunks(peers, groups):
        k_short = filtered(lagged(loaded(payload_ref, 0, width, start, size, at_first)), taps_ref, 1)
        v_short = filtered(lagged(loaded(payload_ref, 1, width, start, size, at_first)), taps_ref, 2)
        kv_ref[start * width : (start + size) * width, :] = (k_short * v_short).reshape(size * width, LANES)
    parts = payload_ref[:, 2 * width : 3 * width, :].astype(F32)
    filt_ref[...] = (parts[:rows] + parts[rows:]).reshape(span, LANES)
    return rows, span


def input_blocks(start, width, groups, rows, kv_ref, filt_ref):
    span = rows * width
    channels = range(start, start + STEP)
    blocks = [
        strided(kv_ref, group * span + channel, rows, width) for channel in channels for group in range(groups)
    ]
    return blocks + [strided(filt_ref, channel, rows, width) for channel in channels]


def conv_kernel(width, groups, payload_ref, taps_ref, table_ref,
                conv_ref, kv_ref, filt_ref):
    rows, span = make_inputs(payload_ref, taps_ref, width, groups, kv_ref, filt_ref)
    pairs = STEP * groups * rows
    table = Tables(table_ref, rows)
    for start in range(0, width, STEP):
        spec = forward(input_blocks(start, width, groups, rows, kv_ref, filt_ref), table)
        products = []
        for side in range(STEP):
            for group in range(groups):
                block = (side * groups + group) * rows
                filt = pairs + side * rows
                products.append(times(spec[block : block + rows], spec[filt : filt + rows], False))
        convs = inverse(jnp.concatenate(products, 0), rows, table)
        for side in range(STEP):
            for group in range(groups):
                conv_ref[pl.ds(group * span + start + side, rows, stride=width), :] = convs[side * groups + group]


def spectra_kernel(width, groups, payload_ref, taps_ref, table_ref, out_ref, kv_ref, filt_ref):
    rows, span = make_inputs(payload_ref, taps_ref, width, groups, kv_ref, filt_ref)
    pairs = STEP * groups * rows
    table = Tables(table_ref, rows)
    for start in range(0, width, STEP):
        spec = forward(input_blocks(start, width, groups, rows, kv_ref, filt_ref), table)
        out_ref[start * groups * rows : start * groups * rows + pairs, :] = spec[:pairs]
        below = groups * span + start * rows
        out_ref[below : below + STEP * rows, :] = spec[pairs:]


def stats_kernel(conv_ref, q_short_ref, grad_z_ref, stats_ref):
    squares = jnp.zeros((LANES, LANES), F32)
    prods = squares
    for start in range(0, conv_ref.shape[0], LANES):
        lanes = slice(start, start + LANES)
        y_out = q_short_ref[lanes, :] * conv_ref[lanes, :]
        squares = squares + y_out * y_out
        prods = prods + grad_z_ref[lanes, :] * y_out
    squares = jnp.sum(squares, 0, keepdims=True)
    prods = jnp.sum(prods, 0, keepdims=True)
    for peer in range(stats_ref.shape[0]):
        stats_ref[peer, 0:1, :] = squares
        stats_ref[peer, 1:2, :] = prods


def scales(stats_ref):
    stats = jnp.sum(stats_ref[...], axis=0)
    rms = jnp.sqrt(stats[0:1] / D + EPS)
    return rms, stats[1:2] / (D * rms * rms * rms)


TAPS = 2 * HALO
EXTRA = 2
SUMS_TOP = 1e18
CONV_TOP = 6.4e7
DCONV_TOP = 4.6e8


def dconv_kernel(width, conv_ref, q_short_ref, grad_z_ref, stats_ref, q_ref, halo_ref, out_ref, edge_ref, rows_ref):
    rms, slope = scales(stats_ref)
    inverse_rms = 1.0 / rms
    pitch = width + EXTRA
    for start in range(0, conv_ref.shape[0], LANES):
        lanes = slice(start, start + LANES)
        q_short = q_short_ref[lanes, :]
        conv = conv_ref[lanes, :]
        grad_y = grad_z_ref[lanes, :] * inverse_rms - q_short * conv * slope
        dconv = grad_y * q_short
        for peer in range(LANES // width):
            into = (start // width + peer) * pitch
            out_ref[into : into + width, :] = dconv[peer * width : (peer + 1) * width]
        grad = (grad_y * conv).T
        edge_ref[:, lanes] = grad[:HALO]
        extended = jnp.concatenate([halo_ref[:, lanes], q_ref[:, lanes]], 0).astype(F32)
        sums = [
            jnp.sum(grad * shifted(extended, HALO - lag), 0, keepdims=True) for lag in range(FILT)
        ]
        rows_ref[lanes, :] = jnp.concatenate(sums + [jnp.zeros((LANES - FILT, LANES), F32)], 0).T
    peers = conv_ref.shape[0] // width
    total = strided(rows_ref, 0, peers, width)
    for channel in range(1, width):
        total = total + pltpu.roll(strided(rows_ref, channel, peers, width), channel * TAPS, 1)
    out_ref[pl.ds(width, peers, stride=pitch), :] = total * (DCONV_TOP / SUMS_TOP)
    out_ref[pl.ds(width + 1, peers, stride=pitch), :] = jnp.zeros_like(total)


def mixed_kernel(conv_ref, q_short_ref, stats_ref, gain_ref, mixed_ref):
    rms, _ = scales(stats_ref)
    for start in range(0, conv_ref.shape[0], LANES):
        lanes = slice(start, start + LANES)
        y_out = q_short_ref[lanes, :] * conv_ref[lanes, :]
        mixed_ref[:, lanes] = ((y_out / rms).T * gain_ref[:, lanes]).astype(BF16)


def grad_q_kernel(conv_ref, q_short_ref, grad_z_ref, stats_ref, edge_ref, taps_ref, out_ref):
    rms, slope = scales(stats_ref)
    inverse_rms = 1.0 / rms
    for start in range(0, conv_ref.shape[0], LANES):
        lanes = slice(start, start + LANES)
        conv = conv_ref[lanes, :]
        grad = (grad_z_ref[lanes, :] * inverse_rms - q_short_ref[lanes, :] * conv * slope) * conv
        extended = jnp.concatenate([grad.T, edge_ref[:, lanes]], 0)
        total = jnp.zeros((LANES, LANES), F32)
        for lag in range(FILT):
            total = total + shifted(extended, lag) * taps_ref[lag : lag + 1, lanes]
        out_ref[:, lanes] = total.astype(BF16)


def back_kernel(width, groups, scale, dconv_ref, payload_ref, saved_ref, taps_ref, table_ref, out_ref, dkv_ref, grad_k_ref, grad_v_ref, dfilt_ref, short_ref):
    peers = payload_ref.shape[0]
    rows = peers // groups
    span = rows * width
    part_width = width // groups
    pitch = width + EXTRA
    dfilt_ref[...] = jnp.zeros(dfilt_ref.shape, F32)
    table = Tables(table_ref, rows)
    for start in range(0, width, STEP):
        blocks = []
        for channel in range(start, start + STEP):
            for group in range(groups):
                blocks.append(strided(dconv_ref, group * rows * pitch + channel, rows, pitch))
        spec = forward(blocks, table)
        below = groups * span + start * rows
        spec_filt = saved_ref[below : below + STEP * rows, :]
        spec_kv = saved_ref[start * groups * rows : (start + STEP) * groups * rows, :]
        products = []
        filters = []
        for side in range(STEP):
            total = 0.0
            for group in range(groups):
                block = (side * groups + group) * rows
                part = spec[block : block + rows]
                products.append(times(spec_filt[side * rows : (side + 1) * rows], part, True))
                total = total + times(spec_kv[block : block + rows], part, True)
            filters.append(total)
        results = inverse(jnp.concatenate(products + filters, 0), rows, table)
        for side in range(STEP):
            channel = start + side
            target = channel // part_width * span + channel % part_width
            dfilt_ref[pl.ds(target, rows, stride=width), :] = results[STEP * groups + side] * scale
            for group in range(groups):
                place = group * span + channel
                dkv_ref[pl.ds(place, rows, stride=width), :] = results[side * groups + group]
    totals = [0.0] * (2 * FILT)
    for start, size, at_first, _ in chunks(peers, groups):
        into = slice(start * width, (start + size) * width)
        dkv = dkv_ref[into, :].reshape(size, width, LANES)
        k_lags = lagged(loaded(payload_ref, 0, width, start, size, at_first))
        v_lags = lagged(loaded(payload_ref, 1, width, start, size, at_first))
        grad_k = dkv * filtered(v_lags, taps_ref, 2)
        grad_v = dkv * filtered(k_lags, taps_ref, 1)
        grad_k_ref[into, :] = grad_k.reshape(size * width, LANES)
        grad_v_ref[into, :] = grad_v.reshape(size * width, LANES)
        for branch, (grad, lags) in enumerate(((grad_k, k_lags), (grad_v, v_lags))):
            for lag in range(FILT):
                totals[branch * FILT + lag] = totals[branch * FILT + lag] + jnp.sum(grad * lags[lag], axis=0)
    for start, size, _, at_last in chunks(peers, groups):
        for index, ref in enumerate((grad_k_ref, grad_v_ref)):
            if at_last:
                values = ref[start * width : (start + size) * width, :]
                values = jnp.concatenate([values, jnp.zeros((width, LANES), F32)], 0)
            else:
                values = ref[start * width : (start + size + 1) * width, :]
            grads = filtered(led(values.reshape(size + 1, width, LANES)), taps_ref, 1 + index)
            out_ref[start : start + size, index * width : (index + 1) * width, :] = grads.astype(BF16)
    short_ref[...] = jnp.zeros(short_ref.shape, F32)
    for tap, total in enumerate(totals):
        short_ref[pl.ds(tap, width, stride=TAPS), :] = total
    sums = strided(dconv_ref, width, peers, pitch) * (SUMS_TOP / DCONV_TOP)
    short = (jnp.sum(short_ref[...].T, axis=0, keepdims=True), jnp.sum(sums, axis=0, keepdims=True))
    for index, values in enumerate(short):
        values = values * scale
        high = values.astype(BF16).astype(F32)
        for row, part in enumerate((high, values - high)):
            start = part_width + 2 * index + row
            dfilt_ref[pl.ds(start, peers, stride=width), :] = jnp.broadcast_to(part, (peers, LANES))
    out_ref[:, 2 * width :, :] = dfilt_ref[...].reshape(peers, width, LANES).astype(BF16)


def part_kernel(width, part_width, payload_ref, part_ref, short_ref, rows_ref, out_ref):
    peers = payload_ref.shape[0]
    rows_ref[...] = payload_ref[:, 2 * width :, :].astype(F32).reshape(peers * width, LANES)
    for row in range(part_width):
        out_ref[pl.ds(row, peers, stride=part_width), :] = strided(rows_ref, row, peers, width)
    part_ref[...] = out_ref[...].astype(BF16)
    short_kv, short_q = (
        strided(rows_ref, start, peers, width) + strided(rows_ref, start + 1, peers, width)
        for start in (part_width, part_width + 2)
    )
    lane = lax.broadcasted_iota(jnp.int32, short_q.shape, 1)
    for channel in range(width):
        back = LANES - channel * TAPS
        rows_ref[pl.ds(channel, peers, stride=width), :] = jnp.where(
            lane < FILT, pltpu.roll(short_q, back % LANES, 1), pltpu.roll(short_kv, (back + FILT) % LANES, 1)
        )
    for start in range(0, short_ref.shape[2], LANES):
        block = rows_ref[start : start + LANES, :].T
        for branch in range(3):
            short_ref[branch, :, start : start + LANES] = block[branch * FILT : (branch + 1) * FILT]


def unpack_kernel(width, payload_ref, grad_q_ref, grads_ref):
    grads_ref[0, 0] = grad_q_ref[...]
    for start in range(0, grad_q_ref.shape[1], LANES):
        source = slice(start // width, (start + LANES) // width)
        for index in range(2):
            block = payload_ref[source, index * width : (index + 1) * width, :].astype(F32)
            grads_ref[1 + index, 0, :, start : start + LANES] = block.reshape(LANES, LANES).T.astype(BF16)


def join_kernel(width, part_width, side_ref, own_ref, other_ref, long_ref, from_ref, rows_ref):
    peers = long_ref.shape[1] // width
    for order, ref in ((side_ref[0, 0], own_ref), (1 - side_ref[0, 0], other_ref)):
        from_ref[...] = ref[...].astype(F32)
        for row in range(part_width):
            rows_ref[pl.ds(order * part_width + row, peers, stride=width), :] = strided(
                from_ref, row, peers, part_width
            )
    for start in range(0, long_ref.shape[1], LANES):
        long_ref[:, start : start + LANES] = rows_ref[start : start + LANES, :].T


def encode(values, top):
    root = lax.rsqrt(lax.rsqrt(jnp.abs(values))) * (60000.0 / top**0.25)
    return jnp.where(values < 0, -root, root).astype(jnp.float16)


def decode(code, top):
    root = code.astype(F32) * (top**0.25 / 60000.0)
    square = root * root
    return jnp.where(root < 0, -square * square, square * square)


PEERS = ("dp", "context")


def exchange(payload):
    return lax.all_to_all(payload, PEERS, split_axis=0, concat_axis=0, tiled=True)


def passed_along(values, by):
    size = lax.axis_size("context")
    pairs = [(i, i + by) for i in range(size) if 0 <= i + by < size]
    return lax.ppermute(values, "context", pairs)


def shards(q_in, k_in, v_in, short_filt, long_filt, norm_gain, grad_out):
    rows = lax.axis_size("context")
    groups = lax.axis_size("dp")
    peers = rows * groups
    channels = q_in.shape[2]
    width = channels // peers
    size = peers * width
    place = lax.axis_index(PEERS)
    table = jnp.asarray(tables(rows))
    scratch = pltpu.VMEM((size, LANES), F32)
    scale = 1.0 / math.sqrt(groups * rows * LANES)
    gain = norm_gain[None]
    taps_q = jnp.pad(short_filt[0], ((0, 1), (0, 0)))
    taps = lax.dynamic_index_in_dim(short_filt.reshape(3 * FILT, peers, width), place, 1, keepdims=False)
    taps = jnp.broadcast_to(taps[:, :, None], (3 * FILT, width, LANES))

    side = lax.axis_index("dp").astype(jnp.int32).reshape(1, 1)
    (payload,) = kernel_call(
        functools.partial(pack_kernel, width), [bf16(peers, 3 * width, LANES)], smem=(0,), count=4, mib=56
    )(side, k_in[0], v_in[0], long_filt)
    payload = exchange(payload)

    halo = passed_along(q_in[0, LANES - HALO :], 1)
    q_short, grad_z = kernel_call(prepare_kernel, [f32(channels, LANES)] * 2, count=5)(
        q_in[0], halo, grad_out[0], taps_q, gain
    )

    inputs = [scratch, pltpu.VMEM((rows * width, LANES), F32)]
    (conv,) = kernel_call(
        functools.partial(conv_kernel, width, groups),
        [f32(size, LANES)],
        scratch=inputs,
        count=3,
        mib=10,
    )(payload, taps, table)

    conv = exchange(encode(conv, CONV_TOP).reshape(peers, width, LANES))
    conv = decode(conv, CONV_TOP).reshape(size, LANES)
    (stats,) = kernel_call(stats_kernel, [f32(lax.axis_size("tensor"), 2, LANES)], count=3)(conv, q_short, grad_z)
    stats = lax.all_to_all(stats, "tensor", split_axis=0, concat_axis=0, tiled=True)
    pitch = width + EXTRA
    dconv, edge = kernel_call(
        functools.partial(dconv_kernel, width),
        [f32(peers * pitch, LANES), f32(HALO, channels)],
        scratch=[scratch],
        count=6,
    )(conv, q_short, grad_z, stats, q_in[0], halo)
    code = exchange(encode(dconv, DCONV_TOP).reshape(peers, pitch // 2, 2, LANES))

    edge = passed_along(edge, -1)
    (mixed,) = kernel_call(mixed_kernel, [bf16(LANES, channels)], count=4)(conv, q_short, stats, gain)
    (grad_q,) = kernel_call(grad_q_kernel, [bf16(LANES, channels)], count=6)(
        conv, q_short, grad_z, stats, edge, taps_q
    )
    (saved,) = kernel_call(
        functools.partial(spectra_kernel, width, groups),
        [f32(size + rows * width, 2 * LANES)],
        scratch=inputs,
        count=3,
        mib=10,
    )(payload, taps, table)
    code, mixed, grad_q, saved = lax.optimization_barrier((code, mixed, grad_q, saved))

    dconv = decode(code, DCONV_TOP).reshape(peers * pitch, LANES)
    (back,) = kernel_call(
        functools.partial(back_kernel, width, groups, scale),
        [bf16(peers, 3 * width, LANES)],
        scratch=[scratch] * 4 + [pltpu.VMEM((LANES, LANES), F32)],
        count=5,
        mib=10,
    )(dconv, payload, saved, taps, table)
    back = exchange(back)
    part_width = width // groups
    part_scratch = pltpu.VMEM((peers * part_width, LANES), F32)
    part, grad_short = kernel_call(
        functools.partial(part_kernel, width, part_width),
        [bf16(peers * part_width, LANES), f32(3, FILT, channels)],
        scratch=[scratch, part_scratch],
        count=1,
    )(back)
    other = lax.ppermute(part, "dp", [(i, i ^ 1) for i in range(groups)])
    (grads,) = kernel_call(
        functools.partial(unpack_kernel, width), [bf16(3, 1, LANES, channels)], count=2
    )(back, grad_q)
    (grad_long,) = kernel_call(
        functools.partial(join_kernel, width, part_width),
        [f32(LANES, channels)],
        smem=(0,),
        scratch=[part_scratch, scratch],
        count=3,
    )(side, part, other)
    return (mixed[None], grads, grad_long, grad_short)


def solution(mesh):
    in_specs = (
        P("dp", "context", "tensor"),
        P("dp", "context", "tensor"),
        P("dp", "context", "tensor"),
        P(None, None, "tensor"),
        P("context", "tensor"),
        P("tensor"),
        P("dp", "context", "tensor"),
    )
    out_specs = (
        P("dp", "context", "tensor"),
        P(None, "dp", "context", "tensor"),
        P("context", "tensor"),
        P(None, None, "tensor"),
    )
    return jax.shard_map(shards, mesh=mesh, in_specs=in_specs, out_specs=out_specs, check_vma=False)
```

time: 219 us -> 216 us (0.986)
  transfers between devices with their start and end apart: 6 -> 6, of which waited for: 5 -> 6; matrix products, arithmetic and copies ran while one was open for 0% -> 0% of each run, Pallas kernels for 3% -> 3%
where the time goes in v6:
time: 216 us; the launch traced here: 213 us
  waiting for transfers between devices  73 us (34%)
  blocking collectives  59.7 us (28%)
  starting transfers between devices  51.1 us (24%)
  Pallas kernels  21.4 us (10%)
  local copies, waits for them, and re-layouts  3.67 us (2%)
  other arithmetic  3.64 us (2%)
    all_to_all x3, waiting for transfers between devices, exchange(): lax.all_to_all(payload, PEERS, split_axis=0, concat_axis=0, tiled=True)  69.2 us
    all_to_all x1, blocking collectives, exchange(): lax.all_to_all(payload, PEERS, split_axis=0, concat_axis=0, tiled=True)  51.8 us
    all_to_all x3, starting transfers between devices, exchange(): lax.all_to_all(payload, PEERS, split_axis=0, concat_axis=0, tiled=True)  41.2 us
    ppermute x2, starting transfers between devices, passed_along(): return lax.ppermute(values, 'context', pairs)  8.02 us
    all_to_all x1, blocking collectives, shards(): lax.all_to_all(stats, 'tensor', split_axis=0, concat_axis=0, tiled=True)  7.95 us
    pallas_call x1, Pallas kernels, shards(): kernel_call(functools.partial(back_kernel, width, groups, scale), [bf16(p...  5.5 us
  transfers between devices with their start and end apart: 6, of which 6 were waited for; matrix products, arithmetic and copies ran while one was open for 0% of the time, Pallas kernels for 3%

profile of v6, /device:TPU:1, one launch (start us, length us, event | category | flops | bytes accessed | tf_op | source)
XLA Modules:
  0.0 213.5 jit_solution(13584589586916782581)
XLA Ops:
  0.6 0.0 copy-start.10
  0.6 2.5 %shard_map.111 = bf16[128,24,128]{2,1,0:T(8,128)(2,1)} custom-call(s32[1,1]{1,0:T(1,128)} %bitcast.side_ref, bf16[128,1024]{1,0:T(8,128)(2,1)} %bitcast.28, bf16[128,1024]{1,0:T(8,128)(2,1)} %bitcast.29, f32[128,1024]{1,0:T(8,128)} %filt_ref.1), custom_call_target="tpu_custom_call" | custom-call | tf_op jit(solution)/shard_map/pallas_call | solution.py:507
  3.1 20.7 %all-to-all-start = ((bf16[128,24,128]{2,1,0:T(8,128)(2,1)}), bf16[128,24,128]{2,1,0:T(8,128)(2,1)S(1)}, u32[]{:S(2)}, u32[]{:S(2)}) async-start(bf16[128,24,128]{2,1,0:T(8,128)(2,1)} %shard_map.111), calls=%async_computation | async-start | bytes 1572864 | tf_op jit(solution)/shard_map/all_to_all | solution.py:481
  23.8 0.0 copy-done.10
  23.8 0.8 reshape.29
  24.6 40.9 %all-to-all-done.payload_ref = bf16[128,24,128]{2,1,0:T(8,128)(2,1)S(1)} async-done(((bf16[128,24,128]{2,1,0:T(8,128)(2,1)}), bf16[128,24,128]{2,1,0:T(8,128)(2,1)S(1)}, u32[]{:S(2)}, u32[]{:S(2)}) %all-to-all-start) | async-done | bytes 786464 | tf_op jit(solution)/shard_map/all_to_all | solution.py:481
  65.5 0.1 broadcast_in_dim.15.taps_ref
  65.6 0.0 copy-done.2
  65.6 0.0 copy-start.5
  65.6 0.0 copy-start.8
  65.6 0.0 copy-start.9
  65.6 4.2 %shard_map.112 = f32[1024,128]{1,0:T(8,128)S(1)} custom-call(bf16[128,24,128]{2,1,0:T(8,128)(2,1)S(1)} %all-to-all-done.payload_ref, f32[21,8,128]{2,1,0:T(8,128)S(1)} %broadcast_in_dim.15.taps_ref, bf16[960,256]{1,0:T(8,128)(2,1)S(1)} %copy-done.2), custom_call_target="tpu_custom_call" | custom-call | tf_op jit(solution)/shard_map/pallas_call | solution.py:518
  69.8 0.9 fusion.5
  70.7 9.7 %all-to-all-start.1 = ((f16[128,8,128]{2,1,0:T(8,128)(2,1)}), f16[128,8,128]{2,1,0:T(8,128)(2,1)S(1)}, u32[]{:S(2)}, u32[]{:S(2)}) async-start(f16[128,8,128]{2,1,0:T(8,128)(2,1)} %fusion.5), calls=%async_computation.1 | async-start | bytes 524288 | tf_op jit(solution)/shard_map/all_to_all | solution.py:481
  80.4 0.0 copy-done.5
  80.4 5.0 %collective-permute-start = (bf16[8,1024]{1,0:T(8,128)(2,1)S(1)}, bf16[8,1024]{1,0:T(8,128)(2,1)S(1)}, u32[]{:S(2)}, u32[]{:S(2)}) collective-permute-start(bf16[8,1024]{1,0:T(8,128)(2,1)S(1)} %slice_bitcast_fusion.1), channel_id=1, source_target_pairs={{0,1},{1,2},{2,3},{3,4},{4,5},{5,6},{6,7},{7,8},{8,9},{9,10},{10,1... | collective-permute-start | bytes 49160 | tf_op jit(solution)/shard_map/ppermute | solution.py:487
  85.5 0.8 collective-permute-done.halo_ref
  86.3 0.6 shard_map.113
  86.9 14.5 %all-to-all-done.1 = f16[128,8,128]{2,1,0:T(8,128)(2,1)S(1)} async-done(((f16[128,8,128]{2,1,0:T(8,128)(2,1)}), f16[128,8,128]{2,1,0:T(8,128)(2,1)S(1)}, u32[]{:S(2)}, u32[]{:S(2)}) %all-to-all-start.1) | async-done | bytes 262176 | tf_op jit(solution)/shard_map/all_to_all | solution.py:481
  101.4 0.1 fusion.3.conv_ref
  101.5 0.1 shard_map.114
  101.6 8.0 %all_to_all.25.stats_ref = f32[4,2,128]{2,1,0:T(2,128)S(1)} all-to-all(f32[4,2,128]{2,1,0:T(2,128)S(1)} %shard_map.114), channel_id=1, replica_groups=mesh['dp'=2,'tensor'=4,'context'=64] {'tensor'}, dimensions={0} | all-to-all | bytes 8192 | tf_op jit(solution)/shard_map/all_to_all | solution.py:529
  109.6 1.5 shard_map.115
  111.1 1.0 fusion
  112.0 10.8 %all-to-all-start.3 = ((f16[128,5,2,128]{3,2,1,0:T(2,128)(2,1)}), f16[128,5,2,128]{3,2,1,0:T(2,128)(2,1)}, u32[]{:S(2)}, u32[]{:S(2)}) async-start(f16[128,5,2,128]{3,2,1,0:T(2,128)(2,1)} %bitcast.12), calls=%async_computation.3 | async-start | bytes 655360 | tf_op jit(solution)/shard_map/all_to_all | solution.py:481
  122.9 3.0 %collective-permute-start.1 = (f32[8,1024]{1,0:T(8,128)}, f32[8,1024]{1,0:T(8,128)S(1)}, u32[]{:S(2)}, u32[]{:S(2)}) collective-permute-start(f32[8,1024]{1,0:T(8,128)} %get-tuple-element.17), channel_id=1, source_target_pairs={{1,0},{2,1},{3,2},{4,3},{5,4},{6,5},{7,6},{8,7},{9,8},{10,9},{11,1... | collective-permute-start | bytes 98312 | tf_op jit(solution)/shard_map/ppermute | solution.py:487
  125.9 0.0 copy-start.3
  125.9 1.0 copy-done.3
  126.9 2.2 %shard_map.118.saved_ref = f32[1536,256]{1,0:T(8,128)S(1)} custom-call(bf16[128,24,128]{2,1,0:T(8,128)(2,1)S(1)} %all-to-all-done.payload_ref, f32[21,8,128]{2,1,0:T(8,128)S(1)} %broadcast_in_dim.15.taps_ref, bf16[960,256]{1,0:T(8,128)(2,1)S(1)} %copy-done.3), custom_call_target="tpu_custom_call" | custom-call | tf_op jit(solution)/shard_map/pallas_call | solution.py:544
  129.1 0.0 copy-start.1
  129.1 0.9 shard_map.116
  130.0 0.3 collective-permute-done.1.edge_ref
  130.3 0.6 shard_map.117.grad_q_ref
  130.9 0.0 copy-start.6
  130.9 0.7 copy-done.6
  131.6 13.9 %all-to-all-done.3 = f16[128,5,2,128]{3,2,1,0:T(2,128)(2,1)} async-done(((f16[128,5,2,128]{3,2,1,0:T(2,128)(2,1)}), f16[128,5,2,128]{3,2,1,0:T(2,128)(2,1)}, u32[]{:S(2)}, u32[]{:S(2)}) %all-to-all-start.3) | async-done | bytes 327712 | tf_op jit(solution)/shard_map/all_to_all | solution.py:481
  145.5 1.6 compare_select_fusion
  147.1 0.0 copy-start.4
  147.1 1.0 copy-done.4
  148.2 5.5 %shard_map.119 = bf16[128,24,128]{2,1,0:T(8,128)(2,1)S(1)} custom-call(f32[1280,128]{1,0:T(8,128)S(1)} %bitcast.21, bf16[128,24,128]{2,1,0:T(8,128)(2,1)S(1)} %all-to-all-done.payload_ref, f32[1536,256]{1,0:T(8,128)S(1)} %shard_map.118.saved_ref, f32[21,8,128]{2,1,0:T(8,128)S(1)} %broadcast_in_dim.15.taps_ref, bf16[960,256]{1,0:T(8,128)(2,1)S(1)} %copy-done.4), custom_call_target="tpu_custom_call" | custom-call | tf_op jit(solution)/shard_map/pallas_call | solution.py:554
  153.7 0.0 copy-start.7
  153.7 51.8 %all_to_all.26.payload_ref = bf16[128,24,128]{2,1,0:T(8,128)(2,1)S(1)} all-to-all(bf16[128,24,128]{2,1,0:T(8,128)(2,1)S(1)} %shard_map.119), channel_id=1, replica_groups=mesh['dp'=2,'tensor'=4,'context'=64] {'dp','context'}, dimensions={0} | all-to-all | bytes 1572864 | tf_op jit(solution)/shard_map/all_to_all | solution.py:481
  205.4 1.2 shard_map.121
  206.6 1.9 collective-permute-start.2
  208.5 0.0 copy-done.7
  208.6 1.1 shard_map.120
  209.6 2.7 %collective-permute-done.2.other_ref = bf16[512,128]{1,0:T(8,128)(2,1)S(1)} collective-permute-done((bf16[512,128]{1,0:T(8,128)(2,1)S(1)}, bf16[512,128]{1,0:T(8,128)(2,1)S(1)}, u32[]{:S(2)}, u32[]{:S(2)}) %collective-permute-start.2) | collective-permute-done | bytes 131104 | tf_op jit(solution)/shard_map/ppermute | solution.py:570
  212.3 1.1 shard_map.122
  (11 shorter events, 0.1 us)
Async XLA Ops:
  0.6 23.2 %copy-start.10 = (f32[3,7,1024]{2,1,0:T(8,128)S(1)}, f32[3,7,1024]{2,1,0:T(8,128)}, u32[]{:S(2)}) copy-start(f32[3,7,1024]{2,1,0:T(8,128)} %param.11) | copy-start | bytes 258052
  3.1 62.5 %copy-start.2 = (bf16[960,256]{1,0:T(8,128)(2,1)S(1)}, bf16[960,256]{1,0:T(8,128)(2,1)}, u32[]{:S(2)}) copy-start(bf16[960,256]{1,0:T(8,128)(2,1)} %constant.35.clone.table_ref) | copy-start | bytes 1474564
  3.1 62.4 %all-to-all-start = ((bf16[128,24,128]{2,1,0:T(8,128)(2,1)}), bf16[128,24,128]{2,1,0:T(8,128)(2,1)S(1)}, u32[]{:S(2)}, u32[]{:S(2)}) async-start(bf16[128,24,128]{2,1,0:T(8,128)(2,1)} %shard_map.111), calls=%async_computation | async-start | bytes 1572864 | tf_op jit(solution)/shard_map/all_to_all | solution.py:481
  65.6 14.8 %copy-start.5 = (bf16[1,128,1024]{2,1,0:T(8,128)(2,1)S(1)}, bf16[1,128,1024]{2,1,0:T(8,128)(2,1)}, u32[]{:S(2)}) copy-start(bf16[1,128,1024]{2,1,0:T(8,128)(2,1)} %param.8) | copy-start | bytes 786436
  65.6 20.7 %copy-start.8 = (bf16[1,128,1024]{2,1,0:T(8,128)(2,1)S(1)}, bf16[1,128,1024]{2,1,0:T(8,128)(2,1)}, u32[]{:S(2)}) copy-start(bf16[1,128,1024]{2,1,0:T(8,128)(2,1)} %param.14) | copy-start | bytes 786436
  65.6 20.7 %copy-start.9 = (f32[1024]{0:T(1024)S(1)}, f32[1024]{0:T(1024)}, u32[]{:S(2)}) copy-start(f32[1024]{0:T(1024)} %param.13) | copy-start | bytes 12292
  70.7 30.7 %all-to-all-start.1 = ((f16[128,8,128]{2,1,0:T(8,128)(2,1)}), f16[128,8,128]{2,1,0:T(8,128)(2,1)S(1)}, u32[]{:S(2)}, u32[]{:S(2)}) async-start(f16[128,8,128]{2,1,0:T(8,128)(2,1)} %fusion.5), calls=%async_computation.1 | async-start | bytes 524288 | tf_op jit(solution)/shard_map/all_to_all | solution.py:481
  80.4 5.9 %collective-permute-start = (bf16[8,1024]{1,0:T(8,128)(2,1)S(1)}, bf16[8,1024]{1,0:T(8,128)(2,1)S(1)}, u32[]{:S(2)}, u32[]{:S(2)}) collective-permute-start(bf16[8,1024]{1,0:T(8,128)(2,1)S(1)} %slice_bitcast_fusion.1), channel_id=1, source_target_pairs={{0,1},{1,2},{2,3},{3,4},{4,5},{5,6},{6,7},{7,8},{8,9},{9,10},{10,1... | collective-permute-start | bytes 49160 | tf_op jit(solution)/shard_map/ppermute | solution.py:487
  86.9 24.2 %copy-start = (f32[1024,128]{1,0:T(8,128)}, f32[1024,128]{1,0:T(8,128)S(1)}, u32[]{:S(2)}) copy-start(f32[1024,128]{1,0:T(8,128)S(1)} %get-tuple-element.15.grad_z_ref) | copy-start | bytes 1572868
  112.0 33.4 %all-to-all-start.3 = ((f16[128,5,2,128]{3,2,1,0:T(2,128)(2,1)}), f16[128,5,2,128]{3,2,1,0:T(2,128)(2,1)}, u32[]{:S(2)}, u32[]{:S(2)}) async-start(f16[128,5,2,128]{3,2,1,0:T(2,128)(2,1)} %bitcast.12), calls=%async_computation.3 | async-start | bytes 655360 | tf_op jit(solution)/shard_map/all_to_all | solution.py:481
  122.9 7.4 %collective-permute-start.1 = (f32[8,1024]{1,0:T(8,128)}, f32[8,1024]{1,0:T(8,128)S(1)}, u32[]{:S(2)}, u32[]{:S(2)}) collective-permute-start(f32[8,1024]{1,0:T(8,128)} %get-tuple-element.17), channel_id=1, source_target_pairs={{1,0},{2,1},{3,2},{4,3},{5,4},{6,5},{7,6},{8,7},{9,8},{10,9},{11,1... | collective-permute-start | bytes 98312 | tf_op jit(solution)/shard_map/ppermute | solution.py:487
  125.9 1.0 copy-start.3
  129.1 1.3 copy-start.1
  130.9 0.7 copy-start.6
  147.1 1.0 copy-start.4
  153.7 54.9 %copy-start.7 = (bf16[128,1024]{1,0:T(8,128)(2,1)S(1)}, bf16[128,1024]{1,0:T(8,128)(2,1)}, u32[]{:S(2)}) copy-start(bf16[128,1024]{1,0:T(8,128)(2,1)} %copy-done.6) | copy-start | bytes 786436
  206.6 5.7 %collective-permute-start.2 = (bf16[512,128]{1,0:T(8,128)(2,1)S(1)}, bf16[512,128]{1,0:T(8,128)(2,1)S(1)}, u32[]{:S(2)}, u32[]{:S(2)}) collective-permute-start(bf16[512,128]{1,0:T(8,128)(2,1)S(1)} %get-tuple-element.22.own_ref), channel_id=1, source_target_pairs={{0,256},{256,0},{1,257},{257,1},{2,258},{258,2},{3,259},{259,3},{4... | collective-permute-start | bytes 393224 | tf_op jit(solution)/shard_map/ppermute | solution.py:570

commit v7 on v6

--- a/solution.py
+++ b/solution.py
@@ -281,15 +281,13 @@
         prods = prods + grad_z_ref[lanes, :] * y_out
     squares = jnp.sum(squares, 0, keepdims=True)
     prods = jnp.sum(prods, 0, keepdims=True)
-    for peer in range(stats_ref.shape[0]):
-        stats_ref[peer, 0:1, :] = squares
-        stats_ref[peer, 1:2, :] = prods
+    stats_ref[0:1, :] = squares
+    stats_ref[1:2, :] = prods
 
 
 def scales(stats_ref):
-    stats = jnp.sum(stats_ref[...], axis=0)
-    rms = jnp.sqrt(stats[0:1] / D + EPS)
-    return rms, stats[1:2] / (D * rms * rms * rms)
+    rms = jnp.sqrt(stats_ref[0:1, :] / D + EPS)
+    return rms, stats_ref[1:2, :] / (D * rms * rms * rms)
 
 
 TAPS = 2 * HALO
@@ -470,8 +468,7 @@
 
 def decode(code, top):
     root = code.astype(F32) * (top**0.25 / 60000.0)
-    square = root * root
-    return jnp.where(root < 0, -square * square, square * square)
+    return root * jnp.abs(root) * (root * root)
 
 
 PEERS = ("dp", "context")
@@ -504,8 +501,15 @@
     taps = jnp.broadcast_to(taps[:, :, None], (3 * FILT, width, LANES))
 
     side = lax.axis_index("dp").astype(jnp.int32).reshape(1, 1)
-    (payload,) = kernel_call(
-        functools.partial(pack_kernel, width), [bf16(peers, 3 * width, LANES)], smem=(0,), count=4, mib=56
+    steps = min(4, channels // LANES)
+    columns = pl.BlockSpec((LANES, channels // steps), lambda step: (0, step))
+    payload = pl.pallas_call(
+        functools.partial(pack_kernel, width),
+        grid=(steps,),
+        out_shape=bf16(peers, 3 * width, LANES),
+        in_specs=[SMEM] + [columns] * 3,
+        out_specs=pl.BlockSpec((peers // steps, 3 * width, LANES), lambda step: (step, 0, 0)),
+        compiler_params=pltpu.CompilerParams(vmem_limit_bytes=56 * 2**20),
     )(side, k_in[0], v_in[0], long_filt)
     payload = exchange(payload)
 
@@ -525,8 +529,12 @@
 
     conv = exchange(encode(conv, CONV_TOP).reshape(peers, width, LANES))
     conv = decode(conv, CONV_TOP).reshape(size, LANES)
-    (stats,) = kernel_call(stats_kernel, [f32(lax.axis_size("tensor"), 2, LANES)], count=3)(conv, q_short, grad_z)
-    stats = lax.all_to_all(stats, "tensor", split_axis=0, concat_axis=0, tiled=True)
+    (stats,) = kernel_call(stats_kernel, [f32(2, LANES)], count=3)(conv, q_short, grad_z)
+    peer = 1
+    while peer < lax.axis_size("tensor"):
+        pairs = [(index, index ^ peer) for index in range(lax.axis_size("tensor"))]
+        stats = stats + lax.ppermute(stats, "tensor", pairs)
+        peer *= 2
     pitch = width + EXTRA
     dconv, edge = kernel_call(
         functools.partial(dconv_kernel, width),
@@ -534,7 +542,7 @@
         scratch=[scratch],
         count=6,
     )(conv, q_short, grad_z, stats, q_in[0], halo)
-    code = exchange(encode(dconv, DCONV_TOP).reshape(peers, pitch // 2, 2, LANES))
+    code = exchange(encode(dconv, DCONV_TOP).reshape(peers, pitch // 2, 2, LANES)).reshape(peers * pitch, LANES)
 
     edge = passed_along(edge, -1)
     (mixed,) = kernel_call(mixed_kernel, [bf16(LANES, channels)], count=4)(conv, q_short, stats, gain)
@@ -550,7 +558,7 @@
     )(payload, taps, table)
     code, mixed, grad_q, saved = lax.optimization_barrier((code, mixed, grad_q, saved))
 
-    dconv = decode(code, DCONV_TOP).reshape(peers * pitch, LANES)
+    dconv = decode(code, DCONV_TOP)
     (back,) = kernel_call(
         functools.partial(back_kernel, width, groups, scale),
         [bf16(peers, 3 * width, LANES)],

time: 216 us -> 221 us (1.023)
  starting transfers between devices: 51.1 us -> 59.8 us
  blocking collectives: 59.7 us -> 51.7 us
  waiting for transfers between devices: 73 us -> 75.4 us
    all_to_all x1 -> x0, blocking collectives: 7.95 us -> none  [shards(): lax.all_to_all(stats, 'tensor', split_axis=0, concat_axis=0, tiled=True)]
    ppermute x0 -> x2, starting transfers between devices: none -> 7.76 us  [shards(): stats = stats + lax.ppermute(stats, 'tensor', pairs)]
    ppermute x0 -> x2, waiting for transfers between devices: none -> 2.34 us  [shards(): stats = stats + lax.ppermute(stats, 'tensor', pairs)]
  transfers between devices with their start and end apart: 6 -> 8, of which waited for: 6 -> 8; matrix products, arithmetic and copies ran while one was open for 0% -> 0% of each run, Pallas kernels for 3% -> 2%
where the time goes in v7:
time: 221 us; the launch traced here: 217 us
  waiting for transfers between devices  75.4 us (34%)
  starting transfers between devices  59.8 us (27%)
  blocking collectives  51.7 us (23%)
  Pallas kernels  22.6 us (10%)
  local copies, waits for them, and re-layouts  3.67 us (2%)
  other arithmetic  3.07 us (1%)
    all_to_all x3, waiting for transfers between devices, exchange(): lax.all_to_all(payload, PEERS, split_axis=0, concat_axis=0, tiled=True)  69.2 us
    all_to_all x1, blocking collectives, exchange(): lax.all_to_all(payload, PEERS, split_axis=0, concat_axis=0, tiled=True)  51.7 us
    all_to_all x3, starting transfers between devices, exchange(): lax.all_to_all(payload, PEERS, split_axis=0, concat_axis=0, tiled=True)  42.1 us
    ppermute x2, starting transfers between devices, passed_along(): return lax.ppermute(values, 'context', pairs)  8.02 us
    ppermute x2, starting transfers between devices, shards(): stats = stats + lax.ppermute(stats, 'tensor', pairs)  7.76 us
    pallas_call x1, Pallas kernels, shards(): kernel_call(functools.partial(back_kernel, width, groups, scale), [bf16(p...  5.5 us
  transfers between devices with their start and end apart: 8, of which 8 were waited for; matrix products, arithmetic and copies ran while one was open for 0% of the time, Pallas kernels for 2%

profile of v7, /device:TPU:1, one launch (start us, length us, event | category | flops | bytes accessed | tf_op | source)
XLA Modules:
  0.0 217.1 jit_solution(4696534375658169606)
XLA Ops:
  0.6 3.6 %shard_map.111 = bf16[128,24,128]{2,1,0:T(8,128)(2,1)} custom-call(s32[1,1]{1,0:T(1,128)} %bitcast.side_ref, bf16[128,1024]{1,0:T(8,128)(2,1)} %bitcast.26, bf16[128,1024]{1,0:T(8,128)(2,1)} %bitcast.27, f32[128,1024]{1,0:T(8,128)} %filt_ref.1), custom_call_target="tpu_custom_call" | custom-call | tf_op jit(solution)/shard_map/pallas_call | solution.py:506
  4.3 20.7 %all-to-all-start = ((bf16[128,24,128]{2,1,0:T(8,128)(2,1)}), bf16[128,24,128]{2,1,0:T(8,128)(2,1)S(1)}, u32[]{:S(2)}, u32[]{:S(2)}) async-start(bf16[128,24,128]{2,1,0:T(8,128)(2,1)} %shard_map.111), calls=%async_computation | async-start | bytes 1572864 | tf_op jit(solution)/shard_map/all_to_all | solution.py:478
  25.0 0.8 reshape.29
  25.8 40.9 %all-to-all-done.payload_ref = bf16[128,24,128]{2,1,0:T(8,128)(2,1)S(1)} async-done(((bf16[128,24,128]{2,1,0:T(8,128)(2,1)}), bf16[128,24,128]{2,1,0:T(8,128)(2,1)S(1)}, u32[]{:S(2)}, u32[]{:S(2)}) %all-to-all-start) | async-done | bytes 786464 | tf_op jit(solution)/shard_map/all_to_all | solution.py:478
  66.7 0.1 broadcast_in_dim.15.taps_ref
  66.8 0.0 copy-start.5
  66.8 0.0 copy-start.8
  66.8 0.0 copy-start.9
  66.8 4.2 %shard_map.112 = f32[1024,128]{1,0:T(8,128)S(1)} custom-call(bf16[128,24,128]{2,1,0:T(8,128)(2,1)S(1)} %all-to-all-done.payload_ref, f32[21,8,128]{2,1,0:T(8,128)S(1)} %broadcast_in_dim.15.taps_ref, bf16[960,256]{1,0:T(8,128)(2,1)S(1)} %copy-done.2), custom_call_target="tpu_custom_call" | custom-call | tf_op jit(solution)/shard_map/pallas_call | solution.py:522
  71.0 0.9 fusion.5
  71.9 9.7 %all-to-all-start.1 = ((f16[128,8,128]{2,1,0:T(8,128)(2,1)}), f16[128,8,128]{2,1,0:T(8,128)(2,1)S(1)}, u32[]{:S(2)}, u32[]{:S(2)}) async-start(f16[128,8,128]{2,1,0:T(8,128)(2,1)} %fusion.5), calls=%async_computation.1 | async-start | bytes 524288 | tf_op jit(solution)/shard_map/all_to_all | solution.py:478
  81.6 0.0 copy-done.5
  81.6 5.0 %collective-permute-start = (bf16[8,1024]{1,0:T(8,128)(2,1)S(1)}, bf16[8,1024]{1,0:T(8,128)(2,1)S(1)}, u32[]{:S(2)}, u32[]{:S(2)}) collective-permute-start(bf16[8,1024]{1,0:T(8,128)(2,1)S(1)} %slice_bitcast_fusion.1), channel_id=1, source_target_pairs={{0,1},{1,2},{2,3},{3,4},{4,5},{5,6},{6,7},{7,8},{8,9},{9,10},{10,1... | collective-permute-start | bytes 49160 | tf_op jit(solution)/shard_map/ppermute | solution.py:484
  86.7 0.8 collective-permute-done.halo_ref
  87.5 0.0 copy-done.8
  87.5 0.6 shard_map.113
  88.1 14.5 %all-to-all-done.1 = f16[128,8,128]{2,1,0:T(8,128)(2,1)S(1)} async-done(((f16[128,8,128]{2,1,0:T(8,128)(2,1)}), f16[128,8,128]{2,1,0:T(8,128)(2,1)S(1)}, u32[]{:S(2)}, u32[]{:S(2)}) %all-to-all-start.1) | async-done | bytes 262176 | tf_op jit(solution)/shard_map/all_to_all | solution.py:478
  102.6 0.1 fusion.4.conv_ref
  102.7 0.1 shard_map.114
  102.8 3.1 %collective-permute-start.1 = (f32[2,128]{1,0:T(2,128)S(1)}, f32[2,128]{1,0:T(2,128)S(1)}, u32[]{:S(2)}, u32[]{:S(2)}) collective-permute-start(f32[2,128]{1,0:T(2,128)S(1)} %shard_map.114), channel_id=1, source_target_pairs={{0,64},{64,0},{128,192},{192,128},{1,65},{65,1},{129,193},{193,129... | collective-permute-start | bytes 3080 | tf_op jit(solution)/shard_map/ppermute | solution.py:536
  105.9 1.2 collective-permute-done.1
  107.1 4.6 %collective-permute-start.2 = (f32[2,128]{1,0:T(2,128)S(1)}, f32[2,128]{1,0:T(2,128)S(1)}, u32[]{:S(2)}, u32[]{:S(2)}) collective-permute-start(f32[2,128]{1,0:T(2,128)S(1)} %add.17), channel_id=1, source_target_pairs={{0,128},{64,192},{128,0},{192,64},{1,129},{65,193},{129,1},{193,65... | collective-permute-start | bytes 3080 | tf_op jit(solution)/shard_map/ppermute | solution.py:536
  111.8 1.2 collective-permute-done.2
  112.9 1.5 shard_map.115
  114.4 1.0 fusion
  115.4 11.7 %all-to-all-start.2 = ((f16[128,5,2,128]{3,2,1,0:T(2,128)(2,1)}), f16[128,5,2,128]{3,2,1,0:T(2,128)(2,1)}, u32[]{:S(2)}, u32[]{:S(2)}) async-start(f16[128,5,2,128]{3,2,1,0:T(2,128)(2,1)} %bitcast.12), calls=%async_computation.2 | async-start | bytes 655360 | tf_op jit(solution)/shard_map/all_to_all | solution.py:478
  127.1 3.0 %collective-permute-start.3 = (f32[8,1024]{1,0:T(8,128)}, f32[8,1024]{1,0:T(8,128)S(1)}, u32[]{:S(2)}, u32[]{:S(2)}) collective-permute-start(f32[8,1024]{1,0:T(8,128)} %get-tuple-element.17), channel_id=1, source_target_pairs={{1,0},{2,1},{3,2},{4,3},{5,4},{6,5},{7,6},{8,7},{9,8},{10,9},{11,1... | collective-permute-start | bytes 98312 | tf_op jit(solution)/shard_map/ppermute | solution.py:484
  130.1 0.0 copy-start.3
  130.1 1.0 copy-done.3
  131.1 2.1 shard_map.118.saved_ref
  133.3 0.0 copy-start.1
  133.3 0.9 shard_map.116
  134.2 0.3 collective-permute-done.3.edge_ref
  134.5 0.6 shard_map.117.grad_q_ref
  135.1 0.0 copy-start.6
  135.1 0.7 copy-done.6
  135.8 13.9 %all-to-all-done.2 = f16[128,5,2,128]{3,2,1,0:T(2,128)(2,1)} async-done(((f16[128,5,2,128]{3,2,1,0:T(2,128)(2,1)}), f16[128,5,2,128]{3,2,1,0:T(2,128)(2,1)}, u32[]{:S(2)}, u32[]{:S(2)}) %all-to-all-start.2) | async-done | bytes 327712 | tf_op jit(solution)/shard_map/all_to_all | solution.py:478
  149.7 1.1 fusion.1.dconv_ref
  150.8 0.0 copy-start.4
  150.8 1.0 copy-done.4
  151.8 5.5 %shard_map.119 = bf16[128,24,128]{2,1,0:T(8,128)(2,1)S(1)} custom-call(f32[1280,128]{1,0:T(8,128)S(1)} %fusion.1.dconv_ref, bf16[128,24,128]{2,1,0:T(8,128)(2,1)S(1)} %all-to-all-done.payload_ref, f32[1536,256]{1,0:T(8,128)S(1)} %shard_map.118.saved_ref, f32[21,8,128]{2,1,0:T(8,128)S(1)} %broadcast_in_dim.15.taps_ref, bf16[960,256]{1,0:T(8,128)(2,1)S(1)} %copy-done.4), custom_call_target="tpu_custom_call" | custom-call | tf_op jit(solution)/shard_map/pallas_call | solution.py:562
  157.3 0.0 copy-start.7
  157.3 51.7 %all_to_all.20.payload_ref = bf16[128,24,128]{2,1,0:T(8,128)(2,1)S(1)} all-to-all(bf16[128,24,128]{2,1,0:T(8,128)(2,1)S(1)} %shard_map.119), channel_id=1, replica_groups=mesh['dp'=2,'tensor'=4,'context'=64] {'dp','context'}, dimensions={0} | all-to-all | bytes 1572864 | tf_op jit(solution)/shard_map/all_to_all | solution.py:478
  209.1 1.2 shard_map.121
  210.3 1.9 collective-permute-start.4
  212.2 1.1 shard_map.120
  213.3 2.7 %collective-permute-done.4.other_ref = bf16[512,128]{1,0:T(8,128)(2,1)S(1)} collective-permute-done((bf16[512,128]{1,0:T(8,128)(2,1)S(1)}, bf16[512,128]{1,0:T(8,128)(2,1)S(1)}, u32[]{:S(2)}, u32[]{:S(2)}) %collective-permute-start.4) | collective-permute-done | bytes 131104 | tf_op jit(solution)/shard_map/ppermute | solution.py:578
  216.0 1.1 shard_map.122
  (16 shorter events, 0.1 us)
Async XLA Ops:
  0.6 24.4 %copy-start.10 = (f32[3,7,1024]{2,1,0:T(8,128)S(1)}, f32[3,7,1024]{2,1,0:T(8,128)}, u32[]{:S(2)}) copy-start(f32[3,7,1024]{2,1,0:T(8,128)} %param.11) | copy-start | bytes 258052
  4.3 62.5 %copy-start.2 = (bf16[960,256]{1,0:T(8,128)(2,1)S(1)}, bf16[960,256]{1,0:T(8,128)(2,1)}, u32[]{:S(2)}) copy-start(bf16[960,256]{1,0:T(8,128)(2,1)} %constant.33.clone.table_ref) | copy-start | bytes 1474564
  4.3 62.4 %all-to-all-start = ((bf16[128,24,128]{2,1,0:T(8,128)(2,1)}), bf16[128,24,128]{2,1,0:T(8,128)(2,1)S(1)}, u32[]{:S(2)}, u32[]{:S(2)}) async-start(bf16[128,24,128]{2,1,0:T(8,128)(2,1)} %shard_map.111), calls=%async_computation | async-start | bytes 1572864 | tf_op jit(solution)/shard_map/all_to_all | solution.py:478
  66.8 14.8 %copy-start.5 = (bf16[1,128,1024]{2,1,0:T(8,128)(2,1)S(1)}, bf16[1,128,1024]{2,1,0:T(8,128)(2,1)}, u32[]{:S(2)}) copy-start(bf16[1,128,1024]{2,1,0:T(8,128)(2,1)} %param.8) | copy-start | bytes 786436
  66.8 20.7 %copy-start.8 = (bf16[1,128,1024]{2,1,0:T(8,128)(2,1)S(1)}, bf16[1,128,1024]{2,1,0:T(8,128)(2,1)}, u32[]{:S(2)}) copy-start(bf16[1,128,1024]{2,1,0:T(8,128)(2,1)} %param.14) | copy-start | bytes 786436
  66.8 20.7 %copy-start.9 = (f32[1024]{0:T(1024)S(1)}, f32[1024]{0:T(1024)}, u32[]{:S(2)}) copy-start(f32[1024]{0:T(1024)} %param.13) | copy-start | bytes 12292
  71.9 30.7 %all-to-all-start.1 = ((f16[128,8,128]{2,1,0:T(8,128)(2,1)}), f16[128,8,128]{2,1,0:T(8,128)(2,1)S(1)}, u32[]{:S(2)}, u32[]{:S(2)}) async-start(f16[128,8,128]{2,1,0:T(8,128)(2,1)} %fusion.5), calls=%async_computation.1 | async-start | bytes 524288 | tf_op jit(solution)/shard_map/all_to_all | solution.py:478
  81.6 5.9 %collective-permute-start = (bf16[8,1024]{1,0:T(8,128)(2,1)S(1)}, bf16[8,1024]{1,0:T(8,128)(2,1)S(1)}, u32[]{:S(2)}, u32[]{:S(2)}) collective-permute-start(bf16[8,1024]{1,0:T(8,128)(2,1)S(1)} %slice_bitcast_fusion.1), channel_id=1, source_target_pairs={{0,1},{1,2},{2,3},{3,4},{4,5},{5,6},{6,7},{7,8},{8,9},{9,10},{10,1... | collective-permute-start | bytes 49160 | tf_op jit(solution)/shard_map/ppermute | solution.py:484
  88.1 26.3 %copy-start = (f32[1024,128]{1,0:T(8,128)}, f32[1024,128]{1,0:T(8,128)S(1)}, u32[]{:S(2)}) copy-start(f32[1024,128]{1,0:T(8,128)S(1)} %get-tuple-element.15.grad_z_ref) | copy-start | bytes 1572868
  102.8 4.3 %collective-permute-start.1 = (f32[2,128]{1,0:T(2,128)S(1)}, f32[2,128]{1,0:T(2,128)S(1)}, u32[]{:S(2)}, u32[]{:S(2)}) collective-permute-start(f32[2,128]{1,0:T(2,128)S(1)} %shard_map.114), channel_id=1, source_target_pairs={{0,64},{64,0},{128,192},{192,128},{1,65},{65,1},{129,193},{193,129... | collective-permute-start | bytes 3080 | tf_op jit(solution)/shard_map/ppermute | solution.py:536
  107.1 5.8 %collective-permute-start.2 = (f32[2,128]{1,0:T(2,128)S(1)}, f32[2,128]{1,0:T(2,128)S(1)}, u32[]{:S(2)}, u32[]{:S(2)}) collective-permute-start(f32[2,128]{1,0:T(2,128)S(1)} %add.17), channel_id=1, source_target_pairs={{0,128},{64,192},{128,0},{192,64},{1,129},{65,193},{129,1},{193,65... | collective-permute-start | bytes 3080 | tf_op jit(solution)/shard_map/ppermute | solution.py:536
  115.4 34.3 %all-to-all-start.2 = ((f16[128,5,2,128]{3,2,1,0:T(2,128)(2,1)}), f16[128,5,2,128]{3,2,1,0:T(2,128)(2,1)}, u32[]{:S(2)}, u32[]{:S(2)}) async-start(f16[128,5,2,128]{3,2,1,0:T(2,128)(2,1)} %bitcast.12), calls=%async_computation.2 | async-start | bytes 655360 | tf_op jit(solution)/shard_map/all_to_all | solution.py:478
  127.1 7.4 %collective-permute-start.3 = (f32[8,1024]{1,0:T(8,128)}, f32[8,1024]{1,0:T(8,128)S(1)}, u32[]{:S(2)}, u32[]{:S(2)}) collective-permute-start(f32[8,1024]{1,0:T(8,128)} %get-tuple-element.17), channel_id=1, source_target_pairs={{1,0},{2,1},{3,2},{4,3},{5,4},{6,5},{7,6},{8,7},{9,8},{10,9},{11,1... | collective-permute-start | bytes 98312 | tf_op jit(solution)/shard_map/ppermute | solution.py:484
  130.1 1.0 copy-start.3
  133.3 1.3 copy-start.1
  135.1 0.7 copy-start.6
  150.8 1.0 copy-start.4
  157.3 54.9 %copy-start.7 = (bf16[128,1024]{1,0:T(8,128)(2,1)S(1)}, bf16[128,1024]{1,0:T(8,128)(2,1)}, u32[]{:S(2)}) copy-start(bf16[128,1024]{1,0:T(8,128)(2,1)} %copy-done.6) | copy-start | bytes 786436
  210.3 5.7 %collective-permute-start.4 = (bf16[512,128]{1,0:T(8,128)(2,1)S(1)}, bf16[512,128]{1,0:T(8,128)(2,1)S(1)}, u32[]{:S(2)}, u32[]{:S(2)}) collective-permute-start(bf16[512,128]{1,0:T(8,128)(2,1)S(1)} %get-tuple-element.22.own_ref), channel_id=1, source_target_pairs={{0,256},{256,0},{1,257},{257,1},{2,258},{258,2},{3,259},{259,3},{4... | collective-permute-start | bytes 393224 | tf_op jit(solution)/shard_map/ppermute | solution.py:578

commit v8 on v6

--- a/solution.py
+++ b/solution.py
@@ -420,12 +420,18 @@
     out_ref[:, 2 * width :, :] = dfilt_ref[...].reshape(peers, width, LANES).astype(BF16)
 
 
-def part_kernel(width, part_width, payload_ref, part_ref, short_ref, rows_ref, out_ref):
+def part_kernel(width, part_width, payload_ref, part_ref, rows_ref, out_ref):
     peers = payload_ref.shape[0]
     rows_ref[...] = payload_ref[:, 2 * width :, :].astype(F32).reshape(peers * width, LANES)
     for row in range(part_width):
         out_ref[pl.ds(row, peers, stride=part_width), :] = strided(rows_ref, row, peers, width)
     part_ref[...] = out_ref[...].astype(BF16)
+
+
+def unpack_kernel(width, part_width, payload_ref, grad_q_ref, grads_ref, short_ref, rows_ref):
+    peers = payload_ref.shape[0]
+    grads_ref[0, 0] = grad_q_ref[...]
+    rows_ref[...] = payload_ref[:, 2 * width :, :].astype(F32).reshape(peers * width, LANES)
     short_kv, short_q = (
         strided(rows_ref, start, peers, width) + strided(rows_ref, start + 1, peers, width)
         for start in (part_width, part_width + 2)
@@ -436,19 +442,15 @@
         rows_ref[pl.ds(channel, peers, stride=width), :] = jnp.where(
             lane < FILT, pltpu.roll(short_q, back % LANES, 1), pltpu.roll(short_kv, (back + FILT) % LANES, 1)
         )
-    for start in range(0, short_ref.shape[2], LANES):
-        block = rows_ref[start : start + LANES, :].T
-        for branch in range(3):
-            short_ref[branch, :, start : start + LANES] = block[branch * FILT : (branch + 1) * FILT]
-
-
-def unpack_kernel(width, payload_ref, grad_q_ref, grads_ref):
-    grads_ref[0, 0] = grad_q_ref[...]
     for start in range(0, grad_q_ref.shape[1], LANES):
+        lanes = slice(start, start + LANES)
         source = slice(start // width, (start + LANES) // width)
         for index in range(2):
             block = payload_ref[source, index * width : (index + 1) * width, :].astype(F32)
-            grads_ref[1 + index, 0, :, start : start + LANES] = block.reshape(LANES, LANES).T.astype(BF16)
+            grads_ref[1 + index, 0, :, lanes] = block.reshape(LANES, LANES).T.astype(BF16)
+        block = rows_ref[lanes, :].T
+        for branch in range(3):
+            short_ref[branch, :, lanes] = block[branch * FILT : (branch + 1) * FILT]
 
 
 def join_kernel(width, part_width, side_ref, own_ref, other_ref, long_ref, from_ref, rows_ref):
@@ -470,8 +472,7 @@
 
 def decode(code, top):
     root = code.astype(F32) * (top**0.25 / 60000.0)
-    square = root * root
-    return jnp.where(root < 0, -square * square, square * square)
+    return root * jnp.abs(root) * (root * root)
 
 
 PEERS = ("dp", "context")
@@ -534,7 +535,7 @@
         scratch=[scratch],
         count=6,
     )(conv, q_short, grad_z, stats, q_in[0], halo)
-    code = exchange(encode(dconv, DCONV_TOP).reshape(peers, pitch // 2, 2, LANES))
+    code = exchange(encode(dconv, DCONV_TOP).reshape(peers, pitch // 2, 2, LANES)).reshape(peers * pitch, LANES)
 
     edge = passed_along(edge, -1)
     (mixed,) = kernel_call(mixed_kernel, [bf16(LANES, channels)], count=4)(conv, q_short, stats, gain)
@@ -550,7 +551,7 @@
     )(payload, taps, table)
     code, mixed, grad_q, saved = lax.optimization_barrier((code, mixed, grad_q, saved))
 
-    dconv = decode(code, DCONV_TOP).reshape(peers * pitch, LANES)
+    dconv = decode(code, DCONV_TOP)
     (back,) = kernel_call(
         functools.partial(back_kernel, width, groups, scale),
         [bf16(peers, 3 * width, LANES)],
@@ -561,15 +562,18 @@
     back = exchange(back)
     part_width = width // groups
     part_scratch = pltpu.VMEM((peers * part_width, LANES), F32)
-    part, grad_short = kernel_call(
+    (part,) = kernel_call(
         functools.partial(part_kernel, width, part_width),
-        [bf16(peers * part_width, LANES), f32(3, FILT, channels)],
+        [bf16(peers * part_width, LANES)],
         scratch=[scratch, part_scratch],
         count=1,
     )(back)
     other = lax.ppermute(part, "dp", [(i, i ^ 1) for i in range(groups)])
-    (grads,) = kernel_call(
-        functools.partial(unpack_kernel, width), [bf16(3, 1, LANES, channels)], count=2
+    grads, grad_short = kernel_call(
+        functools.partial(unpack_kernel, width, part_width),
+        [bf16(3, 1, LANES, channels), f32(3, FILT, channels)],
+        scratch=[scratch],
+        count=2,
     )(back, grad_q)
     (grad_long,) = kernel_call(
         functools.partial(join_kernel, width, part_width),

time: 216 us -> 215 us (level)
  no operation moved by 1% of the time
where the time goes in v8:
time: 215 us; the launch traced here: 212 us
  waiting for transfers between devices  72.5 us (34%)
  blocking collectives  59.7 us (28%)
  starting transfers between devices  51.1 us (24%)
  Pallas kernels  20.8 us (10%)
  local copies, waits for them, and re-layouts  3.67 us (2%)
  other arithmetic  3.06 us (1%)
    all_to_all x3, waiting for transfers between devices, exchange(): lax.all_to_all(payload, PEERS, split_axis=0, concat_axis=0, tiled=True)  69.2 us
    all_to_all x1, blocking collectives, exchange(): lax.all_to_all(payload, PEERS, split_axis=0, concat_axis=0, tiled=True)  51.8 us
    all_to_all x3, starting transfers between devices, exchange(): lax.all_to_all(payload, PEERS, split_axis=0, concat_axis=0, tiled=True)  41.2 us
    ppermute x2, starting transfers between devices, passed_along(): return lax.ppermute(values, 'context', pairs)  8.02 us
    all_to_all x1, blocking collectives, shards(): lax.all_to_all(stats, 'tensor', split_axis=0, concat_axis=0, tiled=True)  7.95 us
    pallas_call x1, Pallas kernels, shards(): kernel_call(functools.partial(back_kernel, width, groups, scale), [bf16(p...  5.5 us
  transfers between devices with their start and end apart: 6, of which 6 were waited for; matrix products, arithmetic and copies ran while one was open for 0% of the time, Pallas kernels for 3%

profile of v8, /device:TPU:1, one launch (start us, length us, event | category | flops | bytes accessed | tf_op | source)
XLA Modules:
  0.0 211.8 jit_solution(5063161584434192248)
XLA Ops:
  0.6 0.0 copy-start.10
  0.6 2.5 %shard_map.111 = bf16[128,24,128]{2,1,0:T(8,128)(2,1)} custom-call(s32[1,1]{1,0:T(1,128)} %bitcast.side_ref, bf16[128,1024]{1,0:T(8,128)(2,1)} %bitcast.27, bf16[128,1024]{1,0:T(8,128)(2,1)} %bitcast.28, f32[128,1024]{1,0:T(8,128)} %filt_ref.1), custom_call_target="tpu_custom_call" | custom-call | tf_op jit(solution)/shard_map/pallas_call | solution.py:508
  3.1 20.7 %all-to-all-start = ((bf16[128,24,128]{2,1,0:T(8,128)(2,1)}), bf16[128,24,128]{2,1,0:T(8,128)(2,1)S(1)}, u32[]{:S(2)}, u32[]{:S(2)}) async-start(bf16[128,24,128]{2,1,0:T(8,128)(2,1)} %shard_map.111), calls=%async_computation | async-start | bytes 1572864 | tf_op jit(solution)/shard_map/all_to_all | solution.py:482
  23.8 0.0 copy-done.10
  23.8 0.8 reshape.29
  24.6 40.9 %all-to-all-done.payload_ref = bf16[128,24,128]{2,1,0:T(8,128)(2,1)S(1)} async-done(((bf16[128,24,128]{2,1,0:T(8,128)(2,1)}), bf16[128,24,128]{2,1,0:T(8,128)(2,1)S(1)}, u32[]{:S(2)}, u32[]{:S(2)}) %all-to-all-start) | async-done | bytes 786464 | tf_op jit(solution)/shard_map/all_to_all | solution.py:482
  65.5 0.1 broadcast_in_dim.15.taps_ref
  65.6 0.0 copy-done.2
  65.6 0.0 copy-start.5
  65.6 0.0 copy-start.8
  65.6 0.0 copy-start.9
  65.6 4.2 %shard_map.112 = f32[1024,128]{1,0:T(8,128)S(1)} custom-call(bf16[128,24,128]{2,1,0:T(8,128)(2,1)S(1)} %all-to-all-done.payload_ref, f32[21,8,128]{2,1,0:T(8,128)S(1)} %broadcast_in_dim.15.taps_ref, bf16[960,256]{1,0:T(8,128)(2,1)S(1)} %copy-done.2), custom_call_target="tpu_custom_call" | custom-call | tf_op jit(solution)/shard_map/pallas_call | solution.py:519
  69.8 0.9 fusion.5
  70.7 9.7 %all-to-all-start.1 = ((f16[128,8,128]{2,1,0:T(8,128)(2,1)}), f16[128,8,128]{2,1,0:T(8,128)(2,1)S(1)}, u32[]{:S(2)}, u32[]{:S(2)}) async-start(f16[128,8,128]{2,1,0:T(8,128)(2,1)} %fusion.5), calls=%async_computation.1 | async-start | bytes 524288 | tf_op jit(solution)/shard_map/all_to_all | solution.py:482
  80.4 0.0 copy-done.5
  80.4 5.0 %collective-permute-start = (bf16[8,1024]{1,0:T(8,128)(2,1)S(1)}, bf16[8,1024]{1,0:T(8,128)(2,1)S(1)}, u32[]{:S(2)}, u32[]{:S(2)}) collective-permute-start(bf16[8,1024]{1,0:T(8,128)(2,1)S(1)} %slice_bitcast_fusion.1), channel_id=1, source_target_pairs={{0,1},{1,2},{2,3},{3,4},{4,5},{5,6},{6,7},{7,8},{8,9},{9,10},{10,1... | collective-permute-start | bytes 49160 | tf_op jit(solution)/shard_map/ppermute | solution.py:488
  85.5 0.8 collective-permute-done.halo_ref
  86.3 0.6 shard_map.113
  86.9 14.5 %all-to-all-done.1 = f16[128,8,128]{2,1,0:T(8,128)(2,1)S(1)} async-done(((f16[128,8,128]{2,1,0:T(8,128)(2,1)}), f16[128,8,128]{2,1,0:T(8,128)(2,1)S(1)}, u32[]{:S(2)}, u32[]{:S(2)}) %all-to-all-start.1) | async-done | bytes 262176 | tf_op jit(solution)/shard_map/all_to_all | solution.py:482
  101.4 0.1 fusion.4.conv_ref
  101.5 0.1 shard_map.114
  101.6 8.0 %all_to_all.25.stats_ref = f32[4,2,128]{2,1,0:T(2,128)S(1)} all-to-all(f32[4,2,128]{2,1,0:T(2,128)S(1)} %shard_map.114), channel_id=1, replica_groups=mesh['dp'=2,'tensor'=4,'context'=64] {'tensor'}, dimensions={0} | all-to-all | bytes 8192 | tf_op jit(solution)/shard_map/all_to_all | solution.py:530
  109.6 1.5 shard_map.115
  111.0 1.0 fusion
  112.0 10.8 %all-to-all-start.3 = ((f16[128,5,2,128]{3,2,1,0:T(2,128)(2,1)}), f16[128,5,2,128]{3,2,1,0:T(2,128)(2,1)}, u32[]{:S(2)}, u32[]{:S(2)}) async-start(f16[128,5,2,128]{3,2,1,0:T(2,128)(2,1)} %bitcast.12), calls=%async_computation.3 | async-start | bytes 655360 | tf_op jit(solution)/shard_map/all_to_all | solution.py:482
  122.8 3.0 %collective-permute-start.1 = (f32[8,1024]{1,0:T(8,128)}, f32[8,1024]{1,0:T(8,128)S(1)}, u32[]{:S(2)}, u32[]{:S(2)}) collective-permute-start(f32[8,1024]{1,0:T(8,128)} %get-tuple-element.17), channel_id=1, source_target_pairs={{1,0},{2,1},{3,2},{4,3},{5,4},{6,5},{7,6},{8,7},{9,8},{10,9},{11,1... | collective-permute-start | bytes 98312 | tf_op jit(solution)/shard_map/ppermute | solution.py:488
  125.8 0.0 copy-start.3
  125.8 1.0 copy-done.3
  126.9 2.2 %shard_map.118.saved_ref = f32[1536,256]{1,0:T(8,128)S(1)} custom-call(bf16[128,24,128]{2,1,0:T(8,128)(2,1)S(1)} %all-to-all-done.payload_ref, f32[21,8,128]{2,1,0:T(8,128)S(1)} %broadcast_in_dim.15.taps_ref, bf16[960,256]{1,0:T(8,128)(2,1)S(1)} %copy-done.3), custom_call_target="tpu_custom_call" | custom-call | tf_op jit(solution)/shard_map/pallas_call | solution.py:545
  129.0 0.0 copy-start.1
  129.0 0.9 shard_map.116
  130.0 0.3 collective-permute-done.1.edge_ref
  130.3 0.6 shard_map.117.grad_q_ref
  130.9 0.0 copy-start.6
  130.9 0.7 copy-done.6
  131.6 13.9 %all-to-all-done.3 = f16[128,5,2,128]{3,2,1,0:T(2,128)(2,1)} async-done(((f16[128,5,2,128]{3,2,1,0:T(2,128)(2,1)}), f16[128,5,2,128]{3,2,1,0:T(2,128)(2,1)}, u32[]{:S(2)}, u32[]{:S(2)}) %all-to-all-start.3) | async-done | bytes 327712 | tf_op jit(solution)/shard_map/all_to_all | solution.py:482
  145.4 1.1 fusion.1.dconv_ref
  146.6 0.0 copy-start.4
  146.6 1.0 copy-done.4
  147.6 5.5 %shard_map.119 = bf16[128,24,128]{2,1,0:T(8,128)(2,1)S(1)} custom-call(f32[1280,128]{1,0:T(8,128)S(1)} %fusion.1.dconv_ref, bf16[128,24,128]{2,1,0:T(8,128)(2,1)S(1)} %all-to-all-done.payload_ref, f32[1536,256]{1,0:T(8,128)S(1)} %shard_map.118.saved_ref, f32[21,8,128]{2,1,0:T(8,128)S(1)} %broadcast_in_dim.15.taps_ref, bf16[960,256]{1,0:T(8,128)(2,1)S(1)} %copy-done.4), custom_call_target="tpu_custom_call" | custom-call | tf_op jit(solution)/shard_map/pallas_call | solution.py:555
  153.1 0.0 copy-start.7
  153.1 51.8 %all_to_all.26.payload_ref = bf16[128,24,128]{2,1,0:T(8,128)(2,1)S(1)} all-to-all(bf16[128,24,128]{2,1,0:T(8,128)(2,1)S(1)} %shard_map.119), channel_id=1, replica_groups=mesh['dp'=2,'tensor'=4,'context'=64] {'dp','context'}, dimensions={0} | all-to-all | bytes 1572864 | tf_op jit(solution)/shard_map/all_to_all | solution.py:482
  204.9 0.1 shard_map.121.own_ref
  205.0 1.9 collective-permute-start.2
  206.9 0.0 copy-done.7
  206.9 1.6 shard_map.120
  208.5 2.2 %collective-permute-done.2.other_ref = bf16[512,128]{1,0:T(8,128)(2,1)S(1)} collective-permute-done((bf16[512,128]{1,0:T(8,128)(2,1)S(1)}, bf16[512,128]{1,0:T(8,128)(2,1)S(1)}, u32[]{:S(2)}, u32[]{:S(2)}) %collective-permute-start.2) | collective-permute-done | bytes 131104 | tf_op jit(solution)/shard_map/ppermute | solution.py:571
  210.7 1.1 shard_map.122
  (11 shorter events, 0.1 us)
Async XLA Ops:
  0.6 23.2 %copy-start.10 = (f32[3,7,1024]{2,1,0:T(8,128)S(1)}, f32[3,7,1024]{2,1,0:T(8,128)}, u32[]{:S(2)}) copy-start(f32[3,7,1024]{2,1,0:T(8,128)} %param.11) | copy-start | bytes 258052
  3.1 62.5 %copy-start.2 = (bf16[960,256]{1,0:T(8,128)(2,1)S(1)}, bf16[960,256]{1,0:T(8,128)(2,1)}, u32[]{:S(2)}) copy-start(bf16[960,256]{1,0:T(8,128)(2,1)} %constant.33.clone.table_ref) | copy-start | bytes 1474564
  3.1 62.4 %all-to-all-start = ((bf16[128,24,128]{2,1,0:T(8,128)(2,1)}), bf16[128,24,128]{2,1,0:T(8,128)(2,1)S(1)}, u32[]{:S(2)}, u32[]{:S(2)}) async-start(bf16[128,24,128]{2,1,0:T(8,128)(2,1)} %shard_map.111), calls=%async_computation | async-start | bytes 1572864 | tf_op jit(solution)/shard_map/all_to_all | solution.py:482
  65.6 14.8 %copy-start.5 = (bf16[1,128,1024]{2,1,0:T(8,128)(2,1)S(1)}, bf16[1,128,1024]{2,1,0:T(8,128)(2,1)}, u32[]{:S(2)}) copy-start(bf16[1,128,1024]{2,1,0:T(8,128)(2,1)} %param.8) | copy-start | bytes 786436
  65.6 20.7 %copy-start.8 = (bf16[1,128,1024]{2,1,0:T(8,128)(2,1)S(1)}, bf16[1,128,1024]{2,1,0:T(8,128)(2,1)}, u32[]{:S(2)}) copy-start(bf16[1,128,1024]{2,1,0:T(8,128)(2,1)} %param.14) | copy-start | bytes 786436
  65.6 20.7 %copy-start.9 = (f32[1024]{0:T(1024)S(1)}, f32[1024]{0:T(1024)}, u32[]{:S(2)}) copy-start(f32[1024]{0:T(1024)} %param.13) | copy-start | bytes 12292
  70.7 30.7 %all-to-all-start.1 = ((f16[128,8,128]{2,1,0:T(8,128)(2,1)}), f16[128,8,128]{2,1,0:T(8,128)(2,1)S(1)}, u32[]{:S(2)}, u32[]{:S(2)}) async-start(f16[128,8,128]{2,1,0:T(8,128)(2,1)} %fusion.5), calls=%async_computation.1 | async-start | bytes 524288 | tf_op jit(solution)/shard_map/all_to_all | solution.py:482
  80.4 5.9 %collective-permute-start = (bf16[8,1024]{1,0:T(8,128)(2,1)S(1)}, bf16[8,1024]{1,0:T(8,128)(2,1)S(1)}, u32[]{:S(2)}, u32[]{:S(2)}) collective-permute-start(bf16[8,1024]{1,0:T(8,128)(2,1)S(1)} %slice_bitcast_fusion.1), channel_id=1, source_target_pairs={{0,1},{1,2},{2,3},{3,4},{4,5},{5,6},{6,7},{7,8},{8,9},{9,10},{10,1... | collective-permute-start | bytes 49160 | tf_op jit(solution)/shard_map/ppermute | solution.py:488
  86.9 24.1 %copy-start = (f32[1024,128]{1,0:T(8,128)}, f32[1024,128]{1,0:T(8,128)S(1)}, u32[]{:S(2)}) copy-start(f32[1024,128]{1,0:T(8,128)S(1)} %get-tuple-element.15.grad_z_ref) | copy-start | bytes 1572868
  112.0 33.4 %all-to-all-start.3 = ((f16[128,5,2,128]{3,2,1,0:T(2,128)(2,1)}), f16[128,5,2,128]{3,2,1,0:T(2,128)(2,1)}, u32[]{:S(2)}, u32[]{:S(2)}) async-start(f16[128,5,2,128]{3,2,1,0:T(2,128)(2,1)} %bitcast.12), calls=%async_computation.3 | async-start | bytes 655360 | tf_op jit(solution)/shard_map/all_to_all | solution.py:482
  122.8 7.4 %collective-permute-start.1 = (f32[8,1024]{1,0:T(8,128)}, f32[8,1024]{1,0:T(8,128)S(1)}, u32[]{:S(2)}, u32[]{:S(2)}) collective-permute-start(f32[8,1024]{1,0:T(8,128)} %get-tuple-element.17), channel_id=1, source_target_pairs={{1,0},{2,1},{3,2},{4,3},{5,4},{6,5},{7,6},{8,7},{9,8},{10,9},{11,1... | collective-permute-start | bytes 98312 | tf_op jit(solution)/shard_map/ppermute | solution.py:488
  125.8 1.0 copy-start.3
  129.0 1.3 copy-start.1
  130.9 0.7 copy-start.6
  146.6 1.0 copy-start.4
  153.1 53.8 %copy-start.7 = (bf16[128,1024]{1,0:T(8,128)(2,1)S(1)}, bf16[128,1024]{1,0:T(8,128)(2,1)}, u32[]{:S(2)}) copy-start(bf16[128,1024]{1,0:T(8,128)(2,1)} %copy-done.6) | copy-start | bytes 786436
  205.0 5.7 %collective-permute-start.2 = (bf16[512,128]{1,0:T(8,128)(2,1)S(1)}, bf16[512,128]{1,0:T(8,128)(2,1)S(1)}, u32[]{:S(2)}, u32[]{:S(2)}) collective-permute-start(bf16[512,128]{1,0:T(8,128)(2,1)S(1)} %shard_map.121.own_ref), channel_id=1, source_target_pairs={{0,256},{256,0},{1,257},{257,1},{2,258},{258,2},{3,259},{259,3},{4... | collective-permute-start | bytes 393224 | tf_op jit(solution)/shard_map/ppermute | solution.py:571
